TPU v7x, 32 devices: a whole 2x2x4 slice. The times are simulated.
32 devices in a mesh: dp: 8 (over z, core), tensor: 4 (over y, x).
Axes of the slice: x: 2, y: 2, z: 4, core: 2. Of those that a mesh axis runs over, the one named last changes fastest.
Arguments:
- hidden_in: bfloat16 [2048, 1536], P(('dp', 'tensor')), may hold values from -0.75 to 0.75
- queries: bfloat16 [2048, 1536], P(('dp', 'tensor')), may hold values from -9 to 9
- draft_kv: bfloat16 [2048, 2, 512], P(('dp', 'tensor')), may hold values from -9 to 9
- cache_kv: bfloat16 [32, 2048, 2, 512], P('dp', 'tensor'), may hold values from -6 to 6
- cache_len: int32 [32], P('dp'), may hold values from 256 to 2048, as said below
- parents: int32 [32, 64], P('dp'), may hold values from -1 to 62, as said below
- path: int32 [32, 8], P('dp'), may hold values from 0 to 56, as said below
- routes: int32 [8, 256, 8], P(None, 'tensor'), may hold values from 0 to 15, all different within a row; in each aligned block of 64 rows (0 to 63, 64 to 127, ..., all dimensions but the last counted through in order) at most 64 rows name the same one
- w_out: bfloat16 [1536, 1536], P('tensor'), may hold values from -0.15625 to 0.15625
- router: float32 [1536, 16], replicated
- norm_gain: float32 [1536], replicated, may hold values from 0.1 to 1.9
- w_gate: bfloat16 [16, 1536, 512], P('dp'), may hold values from -0.15625 to 0.15625
- w_up: bfloat16 [16, 1536, 512], P('dp'), may hold values from -0.15625 to 0.15625
- w_down: bfloat16 [16, 512, 1536], P('dp'), may hold values from -0.25 to 0.25
Outputs:
- hidden_out: bfloat16 [2048, 1536], P(('dp', 'tensor'))
- compacted: bfloat16 [32, 8, 1024], P('dp')
Inputs may be any that keep to these rules, and one draw needn't show every extreme that they name: `parents`: the root is token 0 with parent -1; for i >= 1 the parent of token i is one of tokens i - 8 to i - 1 that are not below 0; in request 0 every token i >= 8 has parent i - 8. Row r lists the tokens of depth 0 to 7 along one root-to-node path of request r's tree; the token of depth k is at most 8 * k. `cache_len`: request 0 has exactly 2048 cached positions. `routes`: the 8 experts of a token differ; in each aligned block of 64 tokens (the tokens of one device between sublayers) any expert may be named by every token.
All inputs are finite; a program needn't handle non-finite values.
Results may differ from a plain program's by a relative error of at most 0.028.
Values may be sent and summed in bfloat16 or wider, within the bound.
No kernel may reach another device: no remote copies, remote signals or barrier semaphores. Data moves between devices by JAX's collectives and lax.ppermute only.
A program may use at most 192 MiB of HBM per device.

v0:
```python
import jax
import jax.numpy as jnp
from jax import lax
from jax.sharding import PartitionSpec as P

QH = 24
KVH = 8
HD = 64
TOP = 8
SINKS = 4
WINDOW = 1024


NEG = -1e30


def merged(array, axis, combine):
    everything = jax.tree.map(
        lambda part, kind: lax.all_gather(part.astype(kind), axis),
        array,
        (jnp.bfloat16, jnp.bfloat16, jnp.bfloat16, jnp.bfloat16),
    )

    def take(k):
        return jax.tree.map(lambda part, own: part[k].astype(own.dtype), everything, array)

    return lax.fori_loop(
        1, lax.axis_size(axis), lambda k, so_far: combine(so_far, take(k)), take(0)
    )


def rotate(values, positions):
    half = values.shape[-1] // 2
    inverse = 10000.0 ** (-2.0 * jnp.arange(half, dtype=jnp.float32) / values.shape[-1])
    angle = positions.astype(jnp.float32)[:, None] * inverse[None, :]
    cosine = jnp.cos(angle)[:, None, :]
    sine = jnp.sin(angle)[:, None, :]
    first = values[..., :half]
    second = values[..., half:]
    return jnp.concatenate(
        [first * cosine - second * sine, second * cosine + first * sine], axis=-1
    )


def closure(parents):
    count = parents.shape[-1]
    index = jnp.arange(count, dtype=jnp.int32)
    linked = (parents[..., :, None] == index).astype(jnp.float32) + jnp.eye(
        count, dtype=jnp.float32
    )
    for level in range((count - 1).bit_length()):
        linked = jnp.minimum(
            jnp.einsum("...ij,...jk->...ik", linked, linked, precision=lax.Precision.HIGHEST), 1.0
        )
    return linked


def expert_slots(chosen, experts):
    flat_hits = (
        chosen.reshape(-1)[:, None] == jnp.arange(experts, dtype=jnp.int32)[None, :]
    ).astype(jnp.int32)
    before = jnp.cumsum(flat_hits, axis=0) - flat_hits
    return jnp.sum(before * flat_hits, axis=1).reshape(chosen.shape)


def routed_gates(normed, router, chosen):
    logits = jnp.dot(normed, router, preferred_element_type=jnp.float32)
    picked = (chosen[..., None] == jnp.arange(router.shape[1], dtype=jnp.int32)).astype(jnp.float32)
    routed = jnp.sum(picked * logits[:, None, :], axis=-1)
    return jax.nn.softmax(routed, axis=-1)


def body(
    hidden_in,
    queries,
    draft_kv,
    cache_kv,
    cache_len,
    parents,
    path,
    routes,
    w_out,
    router,
    norm_gain,
    w_gate,
    w_up,
    w_down,
):
    tensor_count = lax.axis_size("tensor")
    tensor_index = lax.axis_index("tensor")
    data_count = lax.axis_size("dp")
    data_index = lax.axis_index("dp")
    requests = parents.shape[0]
    draft = parents.shape[1]
    tok_sub = queries.shape[0]
    group_rows = requests * draft
    cache_rows = cache_kv.shape[1]
    groups = QH // KVH
    scale = HD ** (-0.5)
    own_start = tensor_index * tok_sub
    ancestry = closure(parents)
    depth = jnp.sum(ancestry, axis=-1).astype(jnp.int32) - 1
    positions = cache_len[:, None] + depth
    own_pos = lax.dynamic_slice_in_dim(positions.reshape(-1), own_start, tok_sub)
    query_rot = (
        rotate(queries.astype(jnp.float32).reshape(tok_sub, QH, HD), own_pos)
        .reshape(tok_sub, QH * HD)
        .astype(jnp.bfloat16)
    )
    key_rot = (
        rotate(draft_kv[:, 0].astype(jnp.float32).reshape(tok_sub, KVH, HD), own_pos)
        .reshape(tok_sub, KVH * HD)
        .astype(jnp.bfloat16)
    )
    own_values = draft_kv[:, 1]
    all_queries = lax.all_gather(query_rot, "tensor", axis=0, tiled=True)
    query_heads = all_queries.reshape(requests, draft, KVH, groups, HD)
    cache_keys = cache_kv[:, :, 0].reshape(requests, cache_rows, KVH, HD)
    cache_values = cache_kv[:, :, 1].reshape(requests, cache_rows, KVH, HD)
    key_pos = tensor_index * cache_rows + jnp.arange(cache_rows, dtype=jnp.int32)
    far_ok = (key_pos[None, None, :] < cache_len[:, None, None]) & (
        (key_pos[None, None, :] < SINKS) | (positions[:, :, None] - key_pos[None, None, :] < WINDOW)
    )
    far_ok = far_ok[:, None, None]
    far_scores = (
        jnp.einsum("rigqd,rjgd->rgqij", query_heads, cache_keys, preferred_element_type=jnp.float32)
        * scale
    )
    far_scores = jnp.where(far_ok, far_scores, NEG)
    flat_queries = all_queries.reshape(group_rows, KVH, groups, HD)
    near_scores = (
        jnp.einsum(
            "agqd,bgd->gqab",
            flat_queries,
            key_rot.reshape(tok_sub, KVH, HD),
            preferred_element_type=jnp.float32,
        )
        * scale
    )
    same_request = (
        jnp.arange(requests, dtype=jnp.int32)[:, None]
        == jnp.arange(requests, dtype=jnp.int32)[None, :]
    ).astype(jnp.float32)
    family = (same_request[:, None, :, None] * ancestry[:, :, None, :]).reshape(
        group_rows, group_rows
    )
    near_ok = (lax.dynamic_slice_in_dim(family, own_start, tok_sub, axis=1) > 0.5)[None, None]
    near_scores = jnp.where(near_ok, near_scores, NEG)

    def rows_far(values):
        return jnp.transpose(values, (0, 3, 1, 2)).reshape(group_rows, QH)

    def rows_near(values):
        return jnp.transpose(values, (2, 0, 1)).reshape(group_rows, QH)

    local_top = jnp.maximum(
        rows_far(jnp.max(far_scores, axis=-1)), rows_near(jnp.max(near_scores, axis=-1))
    )
    wanted = (jnp.arange(requests, dtype=jnp.int32)[:, None] * draft + path).reshape(-1)
    chooser = (wanted[:, None] == own_start + jnp.arange(tok_sub, dtype=jnp.int32)[None, :]).astype(
        jnp.bfloat16
    )
    own_packed = jnp.concatenate([key_rot, own_values], axis=1)
    pieces = jnp.dot(chooser, own_packed, preferred_element_type=jnp.float32)
    col_width = QH * HD // tensor_count
    col_start = tensor_index * col_width
    far_top = jnp.transpose(local_top.reshape(requests, draft, KVH, groups), (0, 2, 3, 1))[
        ..., None
    ]
    near_top = jnp.transpose(local_top.reshape(group_rows, KVH, groups), (1, 2, 0))[..., None]
    far_weights = jnp.where(far_ok, jnp.exp(far_scores - far_top), 0.0)
    near_weights = jnp.where(near_ok, jnp.exp(near_scores - near_top), 0.0)
    totals = rows_far(jnp.sum(far_weights, axis=-1)) + rows_near(jnp.sum(near_weights, axis=-1))
    blended = jnp.einsum(
        "rgqij,rjgd->rigqd",
        far_weights.astype(jnp.bfloat16),
        cache_values,
        preferred_element_type=jnp.float32,
    ).reshape(group_rows, QH * HD)
    blended = blended + jnp.einsum(
        "gqab,bgd->agqd",
        near_weights.astype(jnp.bfloat16),
        own_values.reshape(tok_sub, KVH, HD),
        preferred_element_type=jnp.float32,
    ).reshape(group_rows, QH * HD)
    totals, blended = (totals, blended)

    def combine(first_part, second_part):
        top = jnp.maximum(first_part[0], second_part[0])
        first_scale = jnp.exp(first_part[0] - top)
        second_scale = jnp.exp(second_part[0] - top)
        sums = first_part[1] * first_scale + second_part[1] * second_scale
        joined = (
            first_part[2].reshape(-1, QH, HD) * first_scale[..., None]
            + second_part[2].reshape(-1, QH, HD) * second_scale[..., None]
        )
        return (top, sums, joined.reshape(first_part[2].shape), first_part[3] + second_part[3])

    top, totals, blended, pieces = merged((local_top, totals, blended, pieces), "tensor", combine)
    attention = (
        (blended.reshape(group_rows, QH, HD) / totals[..., None])
        .reshape(group_rows, QH * HD)
        .astype(jnp.bfloat16)
    )
    attention = lax.dynamic_slice_in_dim(attention, col_start, col_width, axis=1)
    compacted = pieces.reshape(requests, path.shape[1], 2 * KVH * HD).astype(jnp.bfloat16)
    attended = lax.psum_scatter(
        jnp.dot(attention, w_out, preferred_element_type=jnp.float32).astype(jnp.bfloat16),
        "tensor",
        scatter_dimension=0,
        tiled=True,
    ).astype(jnp.float32)
    mixed_state = hidden_in.astype(jnp.float32) + attended
    normed = (
        mixed_state
        * lax.rsqrt(jnp.mean(mixed_state * mixed_state, axis=-1, keepdims=True) + 1e-06)
        * norm_gain
    ).astype(jnp.bfloat16)
    local_experts = w_gate.shape[0]
    experts = local_experts * data_count
    capacity = min(tok_sub, 3 * tok_sub * TOP // experts)
    width = normed.shape[1]
    chosen = lax.dynamic_index_in_dim(routes, data_index, 0, keepdims=False)
    gates = routed_gates(normed, router, chosen)
    slots = expert_slots(chosen, experts)
    hits = (chosen[:, :, None, None] == jnp.arange(experts, dtype=jnp.int32)[:, None]) & (
        slots[:, :, None, None] == jnp.arange(capacity, dtype=jnp.int32)[None, :]
    )
    spread_rows = (
        jnp.transpose(jnp.sum(hits.astype(jnp.float32), axis=1), (1, 2, 0))
        .reshape(experts * capacity, tok_sub)
        .astype(jnp.bfloat16)
    )
    outgoing = (
        jnp.dot(spread_rows, normed, preferred_element_type=jnp.float32)
        .astype(jnp.bfloat16)
        .reshape(data_count, local_experts, capacity, width)
    )
    received = lax.all_to_all(outgoing, "dp", split_axis=0, concat_axis=0, tiled=True)
    gate_hidden = jnp.einsum("secd,edf->secf", received, w_gate, preferred_element_type=jnp.float32)
    up_hidden = jnp.einsum("secd,edf->secf", received, w_up, preferred_element_type=jnp.float32)
    activated = (jax.nn.silu(gate_hidden) * up_hidden).astype(jnp.bfloat16)
    produced = jnp.einsum(
        "secf,efd->secd", activated, w_down, preferred_element_type=jnp.float32
    ).astype(jnp.bfloat16)
    returned = lax.all_to_all(produced, "dp", split_axis=0, concat_axis=0, tiled=True).reshape(
        experts * capacity, width
    )
    picked = jnp.take(returned, (chosen * capacity + slots).reshape(-1), axis=0).reshape(
        tok_sub, TOP, width
    )
    moe = jnp.sum(gates[..., None] * picked.astype(jnp.float32), axis=1)
    hidden_out = (mixed_state + moe).astype(jnp.bfloat16)
    return (hidden_out, compacted)


def solution(mesh):
    in_specs = (
        P(("dp", "tensor"), None),
        P(("dp", "tensor"), None),
        P(("dp", "tensor"), None, None),
        P("dp", "tensor", None, None),
        P("dp"),
        P("dp", None),
        P("dp", None),
        P(None, "tensor", None),
        P("tensor", None),
        P(),
        P(),
        P("dp", None, None),
        P("dp", None, None),
        P("dp", None, None),
    )
    out_specs = (P(("dp", "tensor"), None), P("dp", None, None))
    return jax.shard_map(body, mesh=mesh, in_specs=in_specs, out_specs=out_specs, check_vma=False)
```

profile of v0, /device:TPU:0, one launch (start us, length us, event | category | flops | bytes accessed | tf_op | source)
XLA Modules:
  0.0 420.5 jit_solution(16695685115206903146)
XLA Ops:
  7.8 2.0 slice.51
  9.8 1.9 convert_reduce_fusion.1
  11.7 1.1 convolution_minimum_fusion.5
  13.9 0.9 fusion.82
  15.6 2.0 reshape.475
  17.9 1.8 subtract_convert_fusion
  19.9 0.9 convert_element_type.231
  20.9 15.4 %all_gather.21 = bf16[256,1536]{1,0:T(8,128)(2,1)} all-gather(bf16[64,1536]{1,0:T(8,128)(2,1)} %convert_element_type.231), channel_id=1, replica_groups=mesh['dp'=8,'tensor'=4] {'tensor'}, dimensions={0}, use_global_device_ids=true | all-gather | bytes 983040 | tf_op jit(solution)/shard_map/all_gather | solution.py:116
  36.3 2.3 copy.136
  38.6 5.1 %reshape.500 = bf16[4,64,8,3,64]{4,3,2,1,0:T(4,128)(2,1)} reshape(bf16[256,1536]{1,0:T(8,128)(2,1)} %all_gather.21) | data formatting | bytes 1572864 | tf_op jit(solution)/shard_map/reshape | solution.py:117
  45.9 1.0 reshape.476
  47.8 1.8 broadcast_multiply_fusion
  49.6 1.4 mul.289
  51.1 1.1 multiply_subtract_fusion
  52.3 2.6 fusion.83
  55.7 10.0 %fusion.80 = (bf16[4,512,1,512]{3,2,1,0:T(2,128)(2,1)}, bf16[4,512,1,512]{3,2,1,0:T(2,128)(2,1)}) fusion(bf16[4,512,2,512]{3,2,1,0:T(2,128)(2,1)} %param.19), kind=kLoop, calls=%fused_computation.153 | loop fusion | bytes 8388608 | tf_op jit(solution)/shard_map/slice | solution.py:119
  65.7 10.5 %copy.142 = bf16[4,512,1,512]{1,3,0,2:T(8,128)(2,1)} copy(bf16[4,512,1,512]{3,2,1,0:T(2,128)(2,1)} %get-tuple-element.278) | data formatting | bytes 4194304 | tf_op jit(solution)/shard_map/slice | solution.py:119
  76.2 10.5 %copy.130 = bf16[4,512,1,512]{1,3,0,2:T(8,128)(2,1)} copy(bf16[4,512,1,512]{3,2,1,0:T(2,128)(2,1)} %get-tuple-element.279) | data formatting | bytes 4194304 | tf_op jit(solution)/shard_map/slice | solution.py:118
  87.5 9.2 %bitcast_reduce_fusion = (f32[4,8,3,64]{3,2,1,0:T(4,128)S(1)}, f32[4,8,64,3,512]{4,2,3,1,0:T(8,128)}) fusion(pred[4,64,512]{2,1,0:T(8,128)(4,1)S(1)} %fusion.46, bf16[4,512,8,64,1]{1,3,4,2,0:T(8,128)(2,1)} %bitcast.216, bf16[4,64,8,3,64]{4,3,2,1,0:T(4,128)(2,1)} %reshape.500), kind=kOutput, calls=%fused_computation.13 | convolution fusion | flops 412084224 | bytes 15622144 | tf_op jit(solution)/shard_map/rigqd,rjgd->rgqij/dot_general | solution.py:126
  98.0 1.5 reshape.502
  99.6 1.4 maximum_bitcast_fusion
  100.9 8.0 %fusion.23 = f32[4,64,8,3,64]{4,1,3,2,0:T(8,128)} fusion(bf16[4,512,8,64,1]{1,3,4,2,0:T(8,128)(2,1)} %bitcast.220, f32[4,8,64,3,512]{4,2,3,1,0:T(8,128)} %get-tuple-element.291, f32[4,8,3,64]{3,2,1,0:T(4,128)} %fusion.55, pred[4,64,512]{2,1,0:T(8,128)(4,1)S(1)} %fusion.46), kind=kOutput, calls=%fused_computation.42 | convolution fusion | flops 418381824 | bytes 16408576 | tf_op jit(solution)/shard_map/rgqij,rjgd->rigqd/dot_general | solution.py:174
  108.9 4.9 %copy.143 = f32[4,64,8,3,64]{1,0,4,3,2:T(4,128)} copy(f32[4,64,8,3,64]{4,1,3,2,0:T(8,128)} %fusion.23) | data formatting | bytes 3145728 | tf_op jit(solution)/shard_map/rgqij,rjgd->rigqd/transpose | solution.py:174
  113.8 4.1 reshape.465
  118.0 1.9 fusion.39
  119.9 1.1 add_convert_fusion
  121.0 2.3 copy.146
  128.2 1.7 fusion.37
  129.9 7.5 %fusion.6 = f32[4,8,3,64]{3,2,1,0:T(4,128)S(1)} fusion(f32[4,8,64,3,512]{4,2,3,1,0:T(8,128)} %get-tuple-element.291, f32[4,8,3,64]{3,2,1,0:T(4,128)} %fusion.55, pred[4,64,512]{2,1,0:T(8,128)(4,1)S(1)} %fusion.46), kind=kLoop, calls=%fused_computation.18 | loop fusion | flops 15722496 | bytes 12763136 | tf_op jit(solution)/shard_map/reduce_sum | solution.py:173
  137.6 7.3 %all_gather.22 = bf16[4,256,24]{1,2,0:T(8,128)(2,1)S(1)} all-gather(bf16[1,256,24]{1,2,0:T(8,128)(2,1)S(1)} %max.37), channel_id=1, replica_groups=mesh['dp'=8,'tensor'=4] {'tensor'}, dimensions={0}, use_global_device_ids=true | all-gather | bytes 61440 | tf_op jit(solution)/shard_map/all_gather | solution.py:19
  144.9 8.7 %all_gather.23 = bf16[4,256,24]{1,2,0:T(8,128)(2,1)S(1)} all-gather(bf16[1,256,24]{1,2,0:T(8,128)(2,1)S(1)} %add_convert_fusion.3), channel_id=1, replica_groups=mesh['dp'=8,'tensor'=4] {'tensor'}, dimensions={0}, use_global_device_ids=true | all-gather | bytes 61440 | tf_op jit(solution)/shard_map/all_gather | solution.py:19
  153.5 1.0 convolution_convert_fusion.3
  154.6 10.9 %all-gather = bf16[128,1024]{1,0:T(8,128)(2,1)} all-gather(bf16[32,1024]{1,0:T(8,128)(2,1)S(1)} %convolution_convert_fusion.3), channel_id=2, replica_groups=mesh['dp'=8,'tensor'=4] {'tensor'}, dimensions={0}, use_global_device_ids=true | all-gather | bytes 327680 | tf_op jit(solution)/shard_map/all_gather | solution.py:19
  166.3 3.9 all-gather.3.cloned.1.call-done
  170.2 2.5 fusion.41
  172.7 3.0 copy.148
  175.7 24.8 %while.21 = (s32[]{:T(128)}, f32[256,24]{0,1:T(8,128)S(1)}, f32[256,24]{0,1:T(8,128)S(1)}, f32[256,1536]{0,1:T(8,128)}, f32[32,1024]{1,0:T(8,128)S(1)}, /*index=...) while((s32[]{:T(128)}, f32[256,24]{0,1:T(8,128)S(1)}, ...), condition=%wide.region_6.7_spmd, body=%wide.region_5.6_spmd.sunk | while | flops 1687557 | bytes 7626915 | solution.py:27
  176.6 2.1 constant_dynamic-slice_fusion.4
  178.7 2.3 copy.205
  181.0 3.0 fusion.104
  184.9 2.1 constant_dynamic-slice_fusion.4
  187.0 2.3 copy.205
  189.3 3.0 fusion.104
  193.2 2.1 constant_dynamic-slice_fusion.4
  195.3 2.3 copy.205
  197.6 3.0 fusion.104
  200.7 2.9 convolution_convert_fusion.2
  206.4 1.1 reduce-window.6
  209.6 3.3 convert_reduce_fusion
  212.9 1.8 convert_element_type.260
  214.7 15.2 %reduce-scatter.2.cloned.1.call-done = bf16[64,1536]{1,0:T(8,128)(2,1)} async-done(((bf16[256,1536]{1,0:T(8,128)(2,1)}), bf16[64,1536]{1,0:T(8,128)(2,1)}) %reduce-scatter.2.cloned.1.call-update) | async-done | bytes 196624 | tf_op jit(solution)/shard_map/reduce_scatter | solution.py:207
  229.9 1.1 multiply_reduce_fusion.1
  231.0 2.0 convolution_convert_fusion.1
  233.1 76.2 %all_to_all.10 = bf16[8,2,64,1536]{3,2,1,0:T(8,128)(2,1)S(1)} all-to-all(bf16[8,2,64,1536]{3,2,1,0:T(8,128)(2,1)S(1)} %bitcast.217), channel_id=1, replica_groups=mesh['dp'=8,'tensor'=4] {'dp'}, dimensions={0} | all-to-all | bytes 6291456 | tf_op jit(solution)/shard_map/all_to_all | solution.py:239
  309.3 1.7 copy-done.2
  311.0 3.1 fusion.15
  314.1 8.6 %fusion.11 = bf16[8,2,64,1536]{3,2,0,1:T(8,128)(2,1)} fusion(bf16[2,512,1536]{2,1,0:T(8,128)(2,1)S(1)} %copy-done, f32[2,8,64,512]{3,2,1,0:T(8,128)} %fusion.15, bf16[2,1536,512]{2,1,0:T(8,128)(2,1)} %param.28, bf16[8,2,64,1536]{3,2,1,0:T(8,128)(2,1)} %copy-done.2), kind=kOutput, calls=%fused_computation.25 | convolution fusion | flops 3225944064 | bytes 14680064 | tf_op jit(solution)/shard_map/secf,efd->secd/dot_general | solution.py:243
  322.7 3.9 copy.159
  326.6 4.7 %all-to-all-start.1 = ((bf16[8,2,64,1536]{3,2,1,0:T(8,128)(2,1)}), bf16[8,2,64,1536]{3,2,1,0:T(8,128)(2,1)}, u32[]{:S(2)}, u32[]{:S(2)}) async-start(bf16[8,2,64,1536]{3,2,1,0:T(8,128)(2,1)} %copy.159), calls=%async_computation.2 | async-start | bytes 6291456 | tf_op jit(solution)/shard_map/all_to_all | solution.py:246
  332.3 1.2 fusion.78
  333.7 68.8 %all-to-all-done.1 = bf16[8,2,64,1536]{3,2,1,0:T(8,128)(2,1)} async-done(((bf16[8,2,64,1536]{3,2,1,0:T(8,128)(2,1)}), bf16[8,2,64,1536]{3,2,1,0:T(8,128)(2,1)}, u32[]{:S(2)}, u32[]{:S(2)}) %all-to-all-start.1) | async-done | bytes 3145760 | tf_op jit(solution)/shard_map/all_to_all | solution.py:246
  402.5 6.7 %gather_fusion = bf16[512,1536]{1,0:T(8,128)(2,1)} fusion(bf16[1024,1536]{1,0:T(8,128)(2,1)} %bitcast.49, s32[1024]{0:T(1024)S(1)} %pad_clamp_fusion), kind=kCustom, calls=%fused_computation | custom fusion | bytes 3147776 | tf_op jit(solution)/shard_map/jit(_take)/gather | solution.py:249
  409.2 2.7 multiply_reduce_fusion
  412.0 1.7 add_convert_fusion.2
  (112 shorter events, 23.9 us)
Async XLA Ops:
  7.2 306.9 %copy-start = (bf16[2,512,1536]{2,1,0:T(8,128)(2,1)S(1)}, bf16[2,512,1536]{2,1,0:T(8,128)(2,1)}, u32[]{:S(2)}) copy-start(bf16[2,512,1536]{2,1,0:T(8,128)(2,1)} %param.29) | copy-start | bytes 9437188
  7.2 163.1 %all-gather.3.cloned.1.call-start = ((), (), s32[]{:S(2)}) async-start(), calls=%async_computation.3 | async-start | bytes 3932160 | tf_op jit(solution)/shard_map/all_gather | solution.py:19
  7.8 35.9 %copy-start.11 = (s32[512]{0:T(512)}, s32[512]{0:T(512)S(1)}, u32[]{:S(2)}) copy-start(s32[512]{0:T(512)S(1)} %iota_add_fusion) | copy-start | bytes 6148
  15.5 4.1 copy-start.12
  17.9 1.8 copy-start.7
  17.9 1.8 copy-start.8
  19.9 23.8 %copy-start.14 = (s32[4]{0:T(128)S(1)}, s32[4]{0:T(128)}, u32[]{:S(2)}) copy-start(s32[4]{0:T(128)} %param.20) | copy-start | bytes 52
  20.9 23.5 %copy-start.4 = (bf16[64,1,512]{2,1,0:T(2,128)(2,1)S(1)}, bf16[64,1,512]{2,1,0:T(2,128)(2,1)}, u32[]{:S(2)}) copy-start(bf16[64,1,512]{2,1,0:T(2,128)(2,1)} %slice.51) | copy-start | bytes 196612
  20.9 24.3 %copy-start.6 = (f32[4,64,64]{2,1,0:T(8,128)S(1)}, f32[4,64,64]{2,1,0:T(8,128)}, u32[]{:S(2)}) copy-start(f32[4,64,64]{2,1,0:T(8,128)} %get-tuple-element.289) | copy-start | bytes 196612
  55.0 10.7 %copy-start.5 = (f32[8,3,256]{2,1,0:T(4,128)}, f32[8,3,256]{2,1,0:T(4,128)S(1)}, u32[]{:S(2)}) copy-start(f32[8,3,256]{2,1,0:T(4,128)S(1)} %get-tuple-element.292) | copy-start | bytes 73732
  87.5 9.2 %copy-start.9 = (f32[4,64,8,3]{1,0,3,2:T(4,128)S(1)}, f32[4,64,8,3]{1,0,3,2:T(4,128)}, u32[]{:S(2)}) copy-start(f32[4,64,8,3]{1,0,3,2:T(4,128)} %reshape.501) | copy-start | bytes 73732
  118.0 1.9 copy-start.1
  123.3 106.6 %reduce-scatter.2.cloned.1.call-start = ((), (), s32[]{:S(2)}) async-start(), calls=%async_computation.4 | async-start | bytes 983040 | tf_op jit(solution)/shard_map/reduce_scatter | solution.py:207
  129.9 23.6 %copy-start.10 = (bf16[64,1,512]{2,0,1:T(8,128)(2,1)S(1)}, bf16[64,1,512]{2,0,1:T(8,128)(2,1)}, u32[]{:S(2)}) copy-start(bf16[64,1,512]{2,0,1:T(8,128)(2,1)} %copy.203) | copy-start | bytes 196612
  129.9 23.6 %copy-start.15 = (s32[32]{0:T(128)S(1)}, s32[32]{0:T(128)}, u32[]{:S(2)}) copy-start(s32[32]{0:T(128)} %eq.127) | copy-start | bytes 388
  200.5 29.3 %copy-start.3 = (bf16[64,1536]{1,0:T(8,128)(2,1)S(1)}, bf16[64,1536]{1,0:T(8,128)(2,1)}, u32[]{:S(2)}) copy-start(bf16[64,1536]{1,0:T(8,128)(2,1)} %param.16) | copy-start | bytes 589828
  200.7 30.3 %copy-start.13 = (f32[1536]{0:T(1024)S(1)}, f32[1536]{0:T(1024)}, u32[]{:S(2)}) copy-start(f32[1536]{0:T(1024)} %param.26) | copy-start | bytes 18436
  233.0 77.9 %copy-start.16 = (bf16[2,1536,512]{2,1,0:T(8,128)(2,1)S(1)}, bf16[2,1536,512]{2,1,0:T(8,128)(2,1)}, u32[]{:S(2)}) copy-start(bf16[2,1536,512]{2,1,0:T(8,128)(2,1)} %param.27) | copy-start | bytes 9437188
  309.3 1.7 copy-start.2
  326.6 76.0 %all-to-all-start.1 = ((bf16[8,2,64,1536]{3,2,1,0:T(8,128)(2,1)}), bf16[8,2,64,1536]{3,2,1,0:T(8,128)(2,1)}, u32[]{:S(2)}, u32[]{:S(2)}) async-start(bf16[8,2,64,1536]{3,2,1,0:T(8,128)(2,1)} %copy.159), calls=%async_computation.2 | async-start | bytes 6291456 | tf_op jit(solution)/shard_map/all_to_all | solution.py:246
Sparse Core Ops, SparseCore 0:
  123.4 46.7 all-gather.2
  203.7 26.1 reduce-scatter.1
where the time goes:
time: 423 us; the launch traced here: 420 us
  blocking collectives  118 us (28%)
  local copies, waits for them, and re-layouts  99.8 us (24%)
  waiting for transfers between devices  88 us (21%)
  other arithmetic  51.1 us (12%)
  matrix products  43.7 us (10%)
  between operations  14.5 us (3%)
  starting transfers between devices  5 us (1%)
    all_to_all x1, blocking collectives, body(): lax.all_to_all(outgoing, 'dp', split_axis=0, concat_axis=0, tiled=True)  76.2 us
    all_to_all x1, waiting for transfers between devices, body(): lax.all_to_all(produced, 'dp', split_axis=0, concat_axis=0, tiled=True)  68.8 us
    all_gather x3, blocking collectives, merged(): lax.all_gather(part.astype(kind), axis)  26.8 us
    slice x2, local copies, waits for them, and re-layouts, body(): cache_values = cache_kv[:, :, 1].reshape(requests, cache_rows, KVH, HD)  20.5 us
    all_gather x1, blocking collectives, body(): all_queries = lax.all_gather(query_rot, 'tensor', axis=0, tiled=True)  15.4 us
    reduce_scatter x1, waiting for transfers between devices, body(): lax.psum_scatter(jnp.dot(attention, w_out, preferred_element_type=jnp.flo...  15.2 us
    dynamic_slice x6, local copies, waits for them, and re-layouts, take(): part[k].astype(own.dtype)  13.1 us
    slice x1, local copies, waits for them, and re-layouts, body(): cache_keys = cache_kv[:, :, 0].reshape(requests, cache_rows, KVH, HD)  10.5 us
  transfers between devices with their start and end apart: 3, of which 3 were waited for; matrix products, arithmetic and copies ran while one was open for 7% of the time, Pallas kernels for 0%

commit v1 on v0

v1 whole, which is shorter than its diff:
```python
import functools

import jax
import jax.numpy as jnp
import numpy as np
from jax import lax
from jax.experimental import pallas as pl
from jax.experimental.pallas import tpu as pltpu
from jax.sharding import PartitionSpec as P

QH = 24
KVH = 8
HD = 64
TOP = 8
SINKS = 4
WINDOW = 1024

LANES = 128
PAIRS = KVH * HD // LANES
GROUPS = QH // KVH
CORES = 2
NEG = -1e30
FLOOR = -1e6
BF = jnp.bfloat16
F32 = jnp.float32
LOG2E = 1.4426950408889634
VMEM_LIMIT = 60 * 1024 * 1024

_half = HD // 2
INVERSE = np.tile(
    (10000.0 ** (-2.0 * np.arange(_half, dtype=np.float64) / HD)).astype(np.float32), LANES // _half
).reshape(1, LANES)


def params(**kw):
    return pltpu.CompilerParams(vmem_limit_bytes=VMEM_LIMIT, **kw)


def whole():
    return pl.BlockSpec(memory_space=pltpu.VMEM)


def scalars():
    return pl.BlockSpec(memory_space=pltpu.SMEM)


def exchange(x, axis, size, step):
    return lax.ppermute(x, axis, [(i, i ^ step) for i in range(size)])


def lane_index(shape):
    return lax.broadcasted_iota(jnp.int32, shape, len(shape) - 1)


def prelude_kernel(
    where_ref, len_ref, path_ref, par_ref, inv_ref, q_ref, kv_ref,
    pay_ref, key_ref, val_ref, anc_ref, pos_ref, kv_f, pos_own, anc_all,
):
    requests, draft = par_ref.shape
    n = q_ref.shape[0]
    own_start = where_ref[0] * n
    request = own_start // draft
    offset = own_start % draft
    row = lax.broadcasted_iota(jnp.int32, (draft, draft), 0)
    col = lax.broadcasted_iota(jnp.int32, (draft, draft), 1)
    eye = (row == col).astype(F32)
    linked = [
        ((row == par_ref[r : r + 1, :]).astype(F32) + eye).T.astype(BF) for r in range(requests)
    ]
    for level in range((draft - 1).bit_length()):
        linked = [
            jnp.minimum(jnp.dot(m, m, preferred_element_type=F32), 1.0).astype(BF) for m in linked
        ]
    for r in range(requests):
        ancestry = linked[r].astype(F32)
        depth = jnp.sum(ancestry, axis=-1, keepdims=True) - 1.0
        place = depth + len_ref[r].astype(F32)
        pos_ref[r * draft : (r + 1) * draft, :] = jnp.broadcast_to(place, (draft, LANES))
        anc_all[r] = ancestry
    anc_ref[...] = anc_all[request]
    own = pl.multiple_of(own_start, 8)
    angle = pos_ref[pl.ds(own, n), :] * inv_ref[...]
    lane = lane_index((n, LANES))
    front = lane % HD < HD // 2
    cosine = jnp.cos(angle)
    sine = jnp.sin(angle)
    sine = jnp.where(front, -sine, sine)
    low = lane < HD

    def turned(x):
        partner = jnp.where(
            front, pltpu.roll(x, LANES - HD // 2, axis=1), pltpu.roll(x, HD // 2, axis=1)
        )
        return x * cosine + partner * sine

    kv_f[...] = kv_ref[...].astype(F32)
    picks = []
    slot = lax.broadcasted_iota(jnp.int32, (path_ref.shape[1], n), 0)
    token = lax.broadcasted_iota(jnp.int32, (path_ref.shape[1], n), 1) + offset
    wanted = jnp.full(slot.shape, -1, jnp.int32)
    for k in range(path_ref.shape[1]):
        wanted = jnp.where(slot == k, path_ref[request, k], wanted)
    chooser = (wanted == token).astype(BF)
    keys, vals = [], []
    for b in range(PAIRS):
        keys.append(turned(kv_f[pl.ds(2 * b, n, stride=2 * PAIRS), :]).astype(BF))
        vals.append(kv_f[pl.ds(2 * b + 1, n, stride=2 * PAIRS), :].astype(BF))
        key_ref[:, b * LANES : (b + 1) * LANES] = keys[b]
        val_ref[:, b * LANES : (b + 1) * LANES] = vals[b]
    packed = jnp.concatenate(keys + vals, axis=1)
    picked = jnp.dot(chooser, packed, preferred_element_type=F32).astype(BF)
    pay_ref[n:, : packed.shape[1]] = picked
    pay_ref[n:, packed.shape[1] :] = jnp.zeros(
        (path_ref.shape[1], pay_ref.shape[1] - packed.shape[1]), BF
    )
    for b in range(PAIRS):
        x0, x1, x2 = [
            turned(q_ref[:, (GROUPS * b + i) * LANES : (GROUPS * b + i + 1) * LANES].astype(F32))
            for i in range(GROUPS)
        ]
        y0 = jnp.where(low, x0, x1)
        y1 = jnp.where(low, pltpu.roll(x0, HD, axis=1), pltpu.roll(x2, HD, axis=1))
        y2 = jnp.where(low, x1, x2)
        for i, y in enumerate((y0, y1, y2)):
            pay_ref[:n, (GROUPS * b + i) * LANES : (GROUPS * b + i + 1) * LANES] = y.astype(BF)


def prelude(where, cache_len, path, parents, queries, kv):
    requests, draft = parents.shape
    n, width = queries.shape
    kv_width = KVH * HD
    return pl.pallas_call(
        prelude_kernel,
        out_shape=(
            jax.ShapeDtypeStruct((n + path.shape[1], width), BF),
            jax.ShapeDtypeStruct((n, kv_width), BF),
            jax.ShapeDtypeStruct((n, kv_width), BF),
            jax.ShapeDtypeStruct((draft, draft), F32),
            jax.ShapeDtypeStruct((requests * draft, LANES), F32),
        ),
        in_specs=[scalars(), scalars(), scalars(), whole(), whole(), whole(), whole()],
        out_specs=(whole(),) * 5,
        scratch_shapes=[
            pltpu.VMEM(kv.shape, F32),
            pltpu.VMEM((n, LANES), F32),
            pltpu.VMEM((requests, draft, draft), F32),
        ],
        compiler_params=params(),
        name="prelude",
    )(where, cache_len, path, parents, jnp.asarray(INVERSE), queries, kv)


def attend_kernel(
    step, near, where_ref, len_ref, pay_ref, kv_ref, key_ref, val_ref, anc_ref, pos_ref,
    out_ref, kv_f,
):
    draft = anc_ref.shape[0]
    n = key_ref.shape[0]
    cells = kv_ref.shape[1] // (2 * PAIRS)
    me = where_ref[0]
    start = (me ^ step) * n
    request = start // draft
    key_start = me * cells
    place = pos_ref[pl.ds(pl.multiple_of(start, 8), n), :][:, :1]
    key_pos = (lane_index((n, cells)) + key_start).astype(F32)
    far_ok = (key_pos < len_ref[request].astype(F32)) & (
        (key_pos < SINKS) | (place - key_pos < WINDOW)
    )
    bias = jnp.where(far_ok, 0.0, NEG)
    bias = jnp.concatenate([bias] * (2 * GROUPS), axis=0)
    if near:
        own = me * n
        same = (own // draft) == request
        line = anc_ref[pl.ds(pl.multiple_of(start % draft, 8), n), :]
        if n != draft:
            pick = (
                lax.broadcasted_iota(jnp.int32, (draft, n), 0)
                == lax.broadcasted_iota(jnp.int32, (draft, n), 1) + own % draft
            ).astype(BF)
            line = jnp.dot(line.astype(BF), pick, preferred_element_type=F32)
        seen = jnp.where(same, line, 0.0)
        near_bias = jnp.where(seen > 0.5, 0.0, NEG)
        near_bias = jnp.concatenate([near_bias] * (2 * GROUPS), axis=0)
    kv_f[...] = kv_ref[0].astype(F32)
    low = lane_index((n, LANES)) < HD
    lane = lane_index((n, LANES))
    stats = jnp.zeros((n, LANES), F32)
    turn = (((1,), (1,)), ((), ()))
    factor = HD ** (-0.5) * LOG2E
    for b in range(PAIRS):
        keys = kv_f[pl.ds(2 * b, cells, stride=2 * PAIRS), :].astype(BF)
        vals = kv_f[pl.ds(2 * b + 1, cells, stride=2 * PAIRS), :].astype(BF)
        blocks = [
            pay_ref[:n, (GROUPS * b + i) * LANES : (GROUPS * b + i + 1) * LANES]
            for i in range(GROUPS)
        ]
        zero = jnp.zeros((n, LANES), BF)
        rows = jnp.concatenate(
            [jnp.where(low, x, zero) for x in blocks] + [jnp.where(low, zero, x) for x in blocks],
            axis=0,
        )
        scores = lax.dot_general(rows, keys, turn, preferred_element_type=F32) * factor + bias
        top = jnp.max(scores, axis=-1, keepdims=True)
        if near:
            near_scores = (
                lax.dot_general(
                    rows, key_ref[:, b * LANES : (b + 1) * LANES], turn, preferred_element_type=F32
                )
                * factor
                + near_bias
            )
            top = jnp.maximum(top, jnp.max(near_scores, axis=-1, keepdims=True))
        top = jnp.maximum(top, FLOOR)
        top = (top + jnp.abs(top) * (2.0**-7)).astype(BF).astype(F32)
        weights = jnp.exp2(scores - top)
        total = jnp.sum(weights, axis=-1, keepdims=True)
        blend = jnp.dot(weights.astype(BF), vals, preferred_element_type=F32)
        if near:
            near_weights = jnp.exp2(near_scores - top)
            total = total + jnp.sum(near_weights, axis=-1, keepdims=True)
            blend = blend + jnp.dot(
                near_weights.astype(BF),
                val_ref[:, b * LANES : (b + 1) * LANES],
                preferred_element_type=F32,
            )
        high = total.astype(BF).astype(F32)
        rest = total - high
        for i in range(GROUPS):
            first = slice(i * n, (i + 1) * n)
            second = slice((GROUPS + i) * n, (GROUPS + i + 1) * n)
            block = GROUPS * b + i
            out_ref[:, block * LANES : (block + 1) * LANES] = jnp.where(
                low, blend[first], blend[second]
            ).astype(BF)
            for part, rows_of in enumerate((first, second)):
                at = 2 * block + part
                stats = jnp.where(lane == at, top[rows_of], stats)
                stats = jnp.where(lane == QH + at, high[rows_of], stats)
                stats = jnp.where(lane == 2 * QH + at, rest[rows_of], stats)
    out_ref[:, QH * HD :] = stats.astype(BF)


def attend(step, near, where, cache_len, payload, cache, keys, vals, ancestry, pos):
    n = keys.shape[0]
    draft = ancestry.shape[0]
    span = cache.shape[1]

    def cache_block(i, where_ref, len_ref):
        return ((where_ref[0] ^ step) * n // draft, 0, 0)

    def full(x):
        return pl.BlockSpec(x.shape, lambda i, *_: (0,) * x.ndim)

    return pl.pallas_call(
        functools.partial(attend_kernel, step, near),
        out_shape=jax.ShapeDtypeStruct((n, QH * HD + LANES), BF),
        grid_spec=pltpu.PrefetchScalarGridSpec(
            num_scalar_prefetch=2,
            grid=(1,),
            in_specs=[
                full(payload),
                pl.BlockSpec((1, span, LANES), cache_block),
                full(keys),
                full(vals),
                full(ancestry),
                full(pos),
            ],
            out_specs=pl.BlockSpec((n, QH * HD + LANES), lambda i, *_: (0, 0)),
            scratch_shapes=[pltpu.VMEM((span, LANES), F32)],
        ),
        compiler_params=params(),
        name="attend",
    )(where, cache_len, payload, cache, keys, vals, ancestry, pos)


def join_kernel(count, where_ref, *refs):
    parts, rest = refs[:count], refs[count:]
    pieces, rest = rest[:count], rest[count:]
    hidden_ref, gain_ref, mixed_ref, normed_ref, att, weight, sems = rest
    n = hidden_ref.shape[0]
    depth = pieces[0].shape[0]
    width = QH * HD
    me = where_ref[0]
    copies = []
    for k in range(count):
        at = pl.multiple_of((me ^ k) * depth, 16)
        copies.append(
            pltpu.make_async_copy(pieces[k], weight.at[pl.ds(at, depth), :], sems.at[k])
        )
        copies[-1].start()
    stats = [p[:, width:].astype(F32) for p in parts]
    top = stats[0]
    for s in stats[1:]:
        top = jnp.maximum(top, s)
    scales = [jnp.exp2(s - top) for s in stats]
    total = jnp.zeros((n, LANES), F32)
    for s, scale in zip(stats, scales):
        sums = pltpu.roll(s, LANES - QH, axis=1) + pltpu.roll(s, LANES - 2 * QH, axis=1)
        total = total + scale * sums
    inverse = 1.0 / total
    scales = [scale * inverse for scale in scales]
    low = lane_index((n, LANES)) < HD

    for b in range(PAIRS):
        joined = []
        for i in range(GROUPS):
            block = GROUPS * b + i
            acc = jnp.zeros((n, LANES), F32)
            for p, scale in zip(parts, scales):
                by = jnp.where(
                    low, scale[:, 2 * block : 2 * block + 1], scale[:, 2 * block + 1 : 2 * block + 2]
                )
                acc = acc + by * p[:, block * LANES : (block + 1) * LANES].astype(F32)
            joined.append(acc)
        turned = pltpu.roll(joined[1], HD, axis=1)
        back = (
            jnp.where(low, joined[0], turned),
            jnp.where(low, joined[2], joined[0]),
            jnp.where(low, turned, joined[2]),
        )
        for i in range(GROUPS):
            block = GROUPS * b + i
            att[:, block * LANES : (block + 1) * LANES] = back[i].astype(BF)
    for copy in copies:
        copy.wait()
    attended = jnp.dot(att[...], weight[...], preferred_element_type=F32)
    mixed = hidden_ref[...].astype(F32) + attended
    mixed_ref[...] = mixed
    square = jnp.mean(mixed * mixed, axis=-1, keepdims=True)
    normed_ref[...] = (mixed * lax.rsqrt(square + 1e-06) * gain_ref[...]).astype(BF)


def join(where, parts, pieces, hidden_in, gain):
    n, width = hidden_in.shape
    count = len(parts)
    inner = QH * HD
    return pl.pallas_call(
        functools.partial(join_kernel, count),
        out_shape=(
            jax.ShapeDtypeStruct((n, width), F32),
            jax.ShapeDtypeStruct((n, width), BF),
        ),
        in_specs=[scalars()]
        + [whole()] * count
        + [pl.BlockSpec(memory_space=pl.ANY)] * count
        + [whole(), whole()],
        out_specs=(whole(), whole()),
        scratch_shapes=[
            pltpu.VMEM((n, inner), BF),
            pltpu.VMEM((inner, width), BF),
            pltpu.SemaphoreType.DMA((count,)),
        ],
        compiler_params=params(),
        name="join",
    )(where, *parts, *pieces, hidden_in, gain)


def experts_kernel(
    count, where_ref, routes_ref, router_ref, gate_hbm, up_hbm, down_hbm, *refs
):
    slots, (own_ref, other_ref, x, acc, gates_s, wg, wu, wd, sems) = refs[:count], refs[count:]
    n, width = slots[0].shape
    local = gate_hbm.shape[0]
    experts = router_ref.shape[1]
    me = where_ref[1]
    copies = []
    for e in range(local):
        for j, (src, dst) in enumerate(((gate_hbm, wg), (up_hbm, wu), (down_hbm, wd))):
            copies.append(pltpu.make_async_copy(src.at[e], dst.at[e], sems.at[3 * e + j]))
            copies[-1].start()
    router = router_ref[...]
    router_high = router.astype(BF)
    router_low = (router - router_high.astype(F32)).astype(BF)
    for s in range(count):
        x[s * n : (s + 1) * n, :] = slots[s][...]
    rows = count * n
    logits = jnp.dot(x[...], router_high, preferred_element_type=F32) + jnp.dot(
        x[...], router_low, preferred_element_type=F32
    )
    lane = lane_index((n, experts))
    for s in range(count):
        chosen = routes_ref[me ^ s]
        hit = lane == chosen[:, 0:1]
        for k in range(1, chosen.shape[1]):
            hit = hit | (lane == chosen[:, k : k + 1])
        part = jnp.where(hit, logits[s * n : (s + 1) * n, :], NEG)
        part = jnp.exp(part - jnp.max(part, axis=-1, keepdims=True))
        part = jnp.where(hit, part, 0.0)
        gates_s[s * n : (s + 1) * n, :] = part / jnp.sum(part, axis=-1, keepdims=True)
    tile = min(rows, 256)
    for e in range(local):
        for j in range(3):
            copies[3 * e + j].wait()
        for t in range(rows // tile):
            span = slice(t * tile, (t + 1) * tile)
            block = x[span, :]
            gate_hidden = jnp.dot(block, wg[e], preferred_element_type=F32)
            up_hidden = jnp.dot(block, wu[e], preferred_element_type=F32)
            activated = (gate_hidden / (1.0 + jnp.exp(-gate_hidden)) * up_hidden).astype(BF)
            made = jnp.dot(activated, wd[e], preferred_element_type=F32).astype(BF).astype(F32)
            mine = lane_index((tile, experts)) == me * local + e
            gate = jnp.sum(jnp.where(mine, gates_s[span, :], 0.0), axis=-1, keepdims=True)
            if e == 0:
                acc[span, :] = gate * made
            else:
                acc[span, :] = acc[span, :] + gate * made
    for s in range(count):
        if s % CORES == 0:
            own_ref[s // CORES] = acc[s * n : (s + 1) * n, :]
        else:
            other_ref[s // CORES] = acc[s * n : (s + 1) * n, :].astype(BF)


def experts_part(where, routes, router, w_gate, w_up, w_down, slots):
    count = len(slots)
    n, width = slots[0].shape
    local, _, hidden = w_gate.shape
    return pl.pallas_call(
        functools.partial(experts_kernel, count),
        out_shape=(
            jax.ShapeDtypeStruct((count // CORES, n, width), F32),
            jax.ShapeDtypeStruct((count // CORES, n, width), BF),
        ),
        in_specs=[scalars(), whole(), whole()]
        + [pl.BlockSpec(memory_space=pl.ANY)] * 3
        + [whole()] * count,
        out_specs=(whole(), whole()),
        scratch_shapes=[
            pltpu.VMEM((count * n, width), BF),
            pltpu.VMEM((count * n, width), F32),
            pltpu.VMEM((count * n, router.shape[1]), F32),
            pltpu.VMEM((local, width, hidden), BF),
            pltpu.VMEM((local, width, hidden), BF),
            pltpu.VMEM((local, hidden, width), BF),
            pltpu.SemaphoreType.DMA((3 * local,)),
        ],
        compiler_params=params(),
        name="experts",
    )(where, routes, router, w_gate, w_up, w_down, *slots)


def accepted_kernel(count, n, where_ref, *refs):
    out_ref = refs[count]
    requests = out_ref.shape[0]
    draft = count * n // requests
    out_ref[...] = jnp.zeros(out_ref.shape, out_ref.dtype)
    for k in range(count):
        request = (where_ref[0] ^ k) * n // draft
        out_ref[request] = out_ref[request] + refs[k][:, : out_ref.shape[2]]


def accepted(where, payloads, requests, entries, n):
    count = len(payloads)
    block = pl.BlockSpec((entries, payloads[0].shape[1]), lambda i: (n // entries, 0))
    return pl.pallas_call(
        functools.partial(accepted_kernel, count, n),
        out_shape=jax.ShapeDtypeStruct((requests, entries, 2 * KVH * HD), BF),
        grid=(1,),
        in_specs=[scalars()] + [block] * count,
        out_specs=pl.BlockSpec((requests, entries, 2 * KVH * HD), lambda i: (0, 0, 0)),
        compiler_params=params(),
        name="accepted",
    )(where, *payloads)


def rows_by_lane_block(kv):
    lead, (tokens, two, width) = kv.shape[:-3], kv.shape[-3:]
    split = kv.reshape(*lead, tokens, two, width // LANES, LANES)
    return jnp.swapaxes(split, -3, -2).reshape(*lead, tokens * two * width // LANES, LANES)


def body(
    hidden_in, queries, draft_kv, cache_kv, cache_len, parents, path, routes,
    w_out, router, norm_gain, w_gate, w_up, w_down,
):
    tensor = lax.axis_size("tensor")
    data = lax.axis_size("dp")
    n = queries.shape[0]
    requests, draft = parents.shape
    where = jnp.stack([lax.axis_index("tensor"), lax.axis_index("dp")]).astype(jnp.int32)
    payload, keys, vals, ancestry, pos = prelude(
        where, cache_len, path, parents, queries, rows_by_lane_block(draft_kv)
    )
    cache = rows_by_lane_block(cache_kv)
    payloads = [payload] + [exchange(payload, "tensor", tensor, k) for k in range(1, tensor)]
    pieces = [w_out] + [exchange(w_out, "tensor", tensor, k) for k in range(1, tensor)]
    parts = []
    for k in range(tensor):
        near = k < max(1, draft // n)
        part = attend(k, near, where, cache_len, payloads[k], cache, keys, vals, ancestry, pos)
        parts.append(part if k == 0 else exchange(part, "tensor", tensor, k))
    compacted = accepted(where, payloads, requests, path.shape[1], n)
    mixed, normed = join(where, parts, pieces, hidden_in, norm_gain.reshape(1, -1))

    steps = data // CORES
    lines = [normed] + [exchange(normed, "dp", data, CORES * k) for k in range(1, steps)]
    slots = []
    for line in lines:
        slots += [line, exchange(line, "dp", data, 1)]
    own, other = experts_part(where, routes, router, w_gate, w_up, w_down, slots)
    chip = own + exchange(other, "dp", data, 1).astype(F32)
    total = mixed + chip[0]
    low = chip.astype(BF)
    for k in range(1, steps):
        total = total + exchange(low[k], "dp", data, CORES * k).astype(F32)
    return total.astype(BF), compacted


def solution(mesh):
    in_specs = (
        P(("dp", "tensor"), None),
        P(("dp", "tensor"), None),
        P(("dp", "tensor"), None, None),
        P("dp", "tensor", None, None),
        P("dp"),
        P("dp", None),
        P("dp", None),
        P(None, "tensor", None),
        P("tensor", None),
        P(),
        P(),
        P("dp", None, None),
        P("dp", None, None),
        P("dp", None, None),
    )
    out_specs = (P(("dp", "tensor"), None), P("dp", None, None))
    return jax.shard_map(body, mesh=mesh, in_specs=in_specs, out_specs=out_specs, check_vma=False)
```

time: 423 us -> 157 us (0.37)
  blocking collectives: 118 us -> 0 us
  local copies, waits for them, and re-layouts: 99.8 us -> 8.2 us
  other arithmetic: 51.1 us -> 3.11 us
  matrix products: 43.7 us -> 0 us
  Pallas kernels: 0 us -> 41.2 us
  starting transfers between devices: 5 us -> 21.8 us
  between operations: 14.5 us -> 0.83 us
  waiting for transfers between devices: 88 us -> 80.9 us
    ppermute x0 -> x20, waiting for transfers between devices: none -> 80.9 us  [exchange(): return lax.ppermute(x, axis, [(i, i ^ step) for i in range(size)])]
    all_to_all x1 -> x0, blocking collectives: 76.2 us -> none  [body(): lax.all_to_all(outgoing, 'dp', split_axis=0, concat_axis=0, tiled=True)]
    all_to_all x1 -> x0, waiting for transfers between devices: 68.8 us -> none  [body(): lax.all_to_all(produced, 'dp', split_axis=0, concat_axis=0, tiled=True)]
    dot_general x16 -> x0, matrix products: 43.7 us -> none  [the longest x1 9.21 us: body(): jnp.einsum('rigqd,rjgd->rgqij', query_heads, cache_keys, preferred_elemen...]
    all_gather x4 -> x0, blocking collectives: 42.2 us -> none  [the longest x3 26.8 us: merged(): lax.all_gather(part.astype(kind), axis)]
    pallas_call x0 -> x8, Pallas kernels: none -> 41.2 us  [the longest x4 18.5 us: attend(): pl.pallas_call(functools.partial(attend_kernel, step, near), out_shape=ja...]
    slice x7 -> x0, local copies, waits for them, and re-layouts: 34.8 us -> none  [the longest x2 20.5 us: body(): cache_values = cache_kv[:, :, 1].reshape(requests, cache_rows, KVH, HD)]
    ppermute x0 -> x20, starting transfers between devices: none -> 21.8 us  [exchange(): return lax.ppermute(x, axis, [(i, i ^ step) for i in range(size)])]
  transfers between devices with their start and end apart: 3 -> 20, of which waited for: 3 -> 7; matrix products, arithmetic and copies ran while one was open for 7% -> 3% of each run, Pallas kernels for 0% -> 15%
where the time goes in v1:
time: 157 us; the launch traced here: 156 us
  waiting for transfers between devices  80.9 us (52%)
  Pallas kernels  41.2 us (26%)
  starting transfers between devices  21.8 us (14%)
  local copies, waits for them, and re-layouts  8.2 us (5%)
  other arithmetic  3.11 us (2%)
    ppermute x20, waiting for transfers between devices, exchange(): return lax.ppermute(x, axis, [(i, i ^ step) for i in range(size)])  80.9 us
    ppermute x20, starting transfers between devices, exchange(): return lax.ppermute(x, axis, [(i, i ^ step) for i in range(size)])  21.8 us
    pallas_call x4, Pallas kernels, attend(): pl.pallas_call(functools.partial(attend_kernel, step, near), out_shape=ja...  18.5 us
    pallas_call x1, Pallas kernels, experts_part(): pl.pallas_call(functools.partial(experts_kernel, count), out_shape=(jax.S...  12.5 us
    unnamed x34, local copies, waits for them, and re-layouts  7.56 us
    pallas_call x1, Pallas kernels, join(): pl.pallas_call(functools.partial(join_kernel, count), out_shape=(jax.Shap...  5.67 us
  transfers between devices with their start and end apart: 20, of which 7 were waited for; matrix products, arithmetic and copies ran while one was open for 3% of the time, Pallas kernels for 15%

profile of v1, /device:TPU:0, one launch (start us, length us, event | category | flops | bytes accessed | tf_op | source)
XLA Modules:
  0.0 156.1 jit_solution(5321200858842601492)
XLA Ops:
  0.6 3.0 %collective-permute-start.7 = (bf16[384,1536]{1,0:T(8,128)(2,1)}, bf16[384,1536]{1,0:T(8,128)(2,1)S(1)}, u32[]{:S(2)}, u32[]{:S(2)}) collective-permute-start(bf16[384,1536]{1,0:T(8,128)(2,1)} %refs_4_.1), channel_id=1, source_target_pairs={{0,2},{1,3},{2,0},{3,1},{4,6},{5,7},{6,4},{7,5},{8,10},{9,11},{10,... | collective-permute-start | bytes 3538952 | tf_op jit(solution)/shard_map/ppermute | solution.py:48
  3.7 1.5 collective-permute-start.6
  5.2 0.1 collective-permute-start.8
  5.2 0.6 pad_add_fusion.where_ref
  5.8 3.1 %prelude.1 = (bf16[72,1536]{1,0:T(8,128)(2,1)}, bf16[64,512]{1,0:T(8,128)(2,1)}, bf16[64,512]{1,0:T(8,128)(2,1)}, f32[64,64]{1,0:T(8,128)}, f32[256,128]{1,0:T(8,128)}) custom-call(s32[2]{0:T(128)} %pad_add_fusion.where_ref, s32[4]{0:T(128)} %len_ref.9, s32[4,8]{1,0:T(4,128)} %path_ref.1, s32[4,64]{1,0:T(4,128)} %par_ref.1, ...), custom_call_target="tpu_custom_call" | custom-call | tf_op jit(solution)/shard_map/prelude/pallas_call | solution.py:132
  8.9 2.9 %collective-permute-start.4 = (bf16[72,1536]{1,0:T(8,128)(2,1)}, bf16[72,1536]{1,0:T(8,128)(2,1)S(1)}, u32[]{:S(2)}, u32[]{:S(2)}) collective-permute-start(bf16[72,1536]{1,0:T(8,128)(2,1)} %get-tuple-element.11.pay_ref.refs_0_), channel_id=1, source_target_pairs={{0,3},{1,2},{2,1},{3,0},{4,7},{5,6},{6,5},{7,4},{8,11},{9,10},{10,... | collective-permute-start | bytes 663560 | tf_op jit(solution)/shard_map/ppermute | solution.py:48
  11.8 0.5 collective-permute-start.2
  12.3 48.9 %collective-permute-done.4.pay_ref.refs_3_ = bf16[72,1536]{1,0:T(8,128)(2,1)S(1)} collective-permute-done((bf16[72,1536]{1,0:T(8,128)(2,1)}, bf16[72,1536]{1,0:T(8,128)(2,1)S(1)}, u32[]{:S(2)}, u32[]{:S(2)}) %collective-permute-start.4) | collective-permute-done | bytes 221216 | tf_op jit(solution)/shard_map/ppermute | solution.py:48
  61.2 1.6 %collective-permute-start = (bf16[72,1536]{1,0:T(8,128)(2,1)}, bf16[72,1536]{1,0:T(8,128)(2,1)}, u32[]{:S(2)}, u32[]{:S(2)}) collective-permute-start(bf16[72,1536]{1,0:T(8,128)(2,1)} %get-tuple-element.11.pay_ref.refs_0_), channel_id=1, source_target_pairs={{0,1},{1,0},{2,3},{3,2},{4,5},{5,4},{6,7},{7,6},{8,9},{9,8},{10,11... | collective-permute-start | bytes 663560 | tf_op jit(solution)/shard_map/ppermute | solution.py:48
  62.9 0.0 copy-done.3
  62.9 4.4 %attend.7 = bf16[64,1664]{1,0:T(8,128)(2,1)} custom-call(s32[2]{0:T(128)} %pad_add_fusion.where_ref, s32[4]{0:T(128)} %len_ref.9, bf16[72,1536]{1,0:T(8,128)(2,1)} %copy-done.3, bf16[4,4096,128]{2,1,0:T(8,128)(2,1)} %bitcast.30, bf16[64,512]{1,0:T(8,128)(2,1)} %get-tuple-element.12.key_ref, bf16[64,512]{1,0:T(8,128)(2,1)} %get-tuple-element.13.val_ref, ...), custom_call_target="tpu_custom_call" | custom-call | tf_op jit(solution)/shard_map/attend/pallas_call | solution.py:254
  67.3 0.0 collective-permute-done.2.pay_ref.refs_2_
  67.3 1.6 %collective-permute-start.5 = (bf16[64,1664]{1,0:T(8,128)(2,1)}, bf16[64,1664]{1,0:T(8,128)(2,1)S(1)}, u32[]{:S(2)}, u32[]{:S(2)}) collective-permute-start(bf16[64,1664]{1,0:T(8,128)(2,1)} %attend.7), channel_id=1, source_target_pairs={{0,3},{1,2},{2,1},{3,0},{4,7},{5,6},{6,5},{7,4},{8,11},{9,10},{10,... | collective-permute-start | bytes 638984 | tf_op jit(solution)/shard_map/ppermute | solution.py:48
  68.9 0.0 copy-done.4
  68.9 4.4 %attend.6 = bf16[64,1664]{1,0:T(8,128)(2,1)} custom-call(s32[2]{0:T(128)} %pad_add_fusion.where_ref, s32[4]{0:T(128)} %len_ref.9, bf16[72,1536]{1,0:T(8,128)(2,1)} %copy-done.4, bf16[4,4096,128]{2,1,0:T(8,128)(2,1)} %bitcast.31, bf16[64,512]{1,0:T(8,128)(2,1)} %get-tuple-element.12.key_ref, bf16[64,512]{1,0:T(8,128)(2,1)} %get-tuple-element.13.val_ref, ...), custom_call_target="tpu_custom_call" | custom-call | tf_op jit(solution)/shard_map/attend/pallas_call | solution.py:254
  73.3 0.0 collective-permute-done.pay_ref.refs_1_
  73.3 0.6 collective-permute-start.3
  73.9 4.4 %attend.5 = bf16[64,1664]{1,0:T(8,128)(2,1)} custom-call(s32[2]{0:T(128)} %pad_add_fusion.where_ref, s32[4]{0:T(128)} %len_ref.9, bf16[72,1536]{1,0:T(8,128)(2,1)} %collective-permute-done.pay_ref.refs_1_, bf16[4,4096,128]{2,1,0:T(8,128)(2,1)} %bitcast.32, bf16[64,512]{1,0:T(8,128)(2,1)} %get-tuple-element.12.key_ref, ...), custom_call_target="tpu_custom_call" | custom-call | tf_op jit(solution)/shard_map/attend/pallas_call | solution.py:254
  78.3 0.0 collective-permute-done.5.refs_3_
  78.3 1.3 collective-permute-start.1
  79.7 5.2 %attend.4.refs_0_ = bf16[64,1664]{1,0:T(8,128)(2,1)} custom-call(s32[2]{0:T(128)} %pad_add_fusion.where_ref, s32[4]{0:T(128)} %len_ref.9, bf16[72,1536]{1,0:T(8,128)(2,1)} %get-tuple-element.11.pay_ref.refs_0_, bf16[4,4096,128]{2,1,0:T(8,128)(2,1)} %bitcast.33, bf16[64,512]{1,0:T(8,128)(2,1)} %get-tuple-element.12.key_ref, ...), custom_call_target="tpu_custom_call" | custom-call | tf_op jit(solution)/shard_map/attend/pallas_call | solution.py:254
  84.9 0.6 reshape.23.refs_9_
  85.5 0.0 collective-permute-done.3.refs_2_
  85.5 0.0 collective-permute-done.1.refs_1_
  85.5 0.0 collective-permute-done.7.refs_6_
  85.5 0.0 collective-permute-done.6.refs_5_
  85.6 0.0 collective-permute-done.8.refs_7_
  85.6 0.6 copy-done.7
  86.2 0.4 copy-done
  86.6 0.4 copy-done.1
  87.0 1.0 copy-done.2
  88.0 5.7 %join.1 = (f32[64,1536]{1,0:T(8,128)}, bf16[64,1536]{1,0:T(8,128)(2,1)}) custom-call(s32[2]{0:T(128)} %pad_add_fusion.where_ref, bf16[64,1664]{1,0:T(8,128)(2,1)} %attend.4.refs_0_, bf16[64,1664]{1,0:T(8,128)(2,1)} %collective-permute-done.1.refs_1_, bf16[64,1664]{1,0:T(8,128)(2,1)} %copy-done.7, bf16[64,1664]{1,0:T(8,128)(2,1)} %copy-done.6, ...), custom_call_target="tpu_custom_call" | custom-call | tf_op jit(solution)/shard_map/join/pallas_call | solution.py:337
  93.7 3.7 %collective-permute-start.14 = (bf16[64,1536]{1,0:T(8,128)(2,1)}, bf16[64,1536]{1,0:T(8,128)(2,1)S(1)}, u32[]{:S(2)}, u32[]{:S(2)}) collective-permute-start(bf16[64,1536]{1,0:T(8,128)(2,1)} %get-tuple-element.17.refs_0_), channel_id=1, source_target_pairs={{0,24},{4,28},{8,16},{12,20},{16,8},{20,12},{24,0},{28,4},{1,25},{... | collective-permute-start | bytes 589832 | tf_op jit(solution)/shard_map/ppermute | solution.py:48
  97.4 0.0 collective-permute-start.12
  97.4 0.8 collective-permute-start.10
  98.2 0.0 collective-permute-start.9
  98.2 5.5 %collective-permute-done.14.refs_6_ = bf16[64,1536]{1,0:T(8,128)(2,1)S(1)} collective-permute-done((bf16[64,1536]{1,0:T(8,128)(2,1)}, bf16[64,1536]{1,0:T(8,128)(2,1)S(1)}, u32[]{:S(2)}, u32[]{:S(2)}) %collective-permute-start.14) | collective-permute-done | bytes 196640 | tf_op jit(solution)/shard_map/ppermute | solution.py:48
  103.6 0.0 collective-permute-start.15
  103.6 8.3 %collective-permute-done.12.refs_4_ = bf16[64,1536]{1,0:T(8,128)(2,1)S(1)} collective-permute-done((bf16[64,1536]{1,0:T(8,128)(2,1)}, bf16[64,1536]{1,0:T(8,128)(2,1)S(1)}, u32[]{:S(2)}, u32[]{:S(2)}) %collective-permute-start.12) | collective-permute-done | bytes 196640 | tf_op jit(solution)/shard_map/ppermute | solution.py:48
  111.9 0.0 collective-permute-start.13
  111.9 0.0 collective-permute-done.10.refs_2_
  111.9 0.5 collective-permute-start.11
  112.4 1.6 %copy.19.routes_ref = s32[8,64,8]{2,1,0:T(8,128)} copy(s32[8,64,8]{1,2,0:T(8,128)} %param.22) | data formatting | bytes 32768 | tf_op args[7]
  114.0 2.1 %copy.20.router_ref = f32[1536,16]{1,0:T(8,128)} copy(f32[1536,16]{0,1:T(8,128)} %param.24) | data formatting | bytes 196608 | tf_op args[9]
  116.1 0.0 collective-permute-done.9.refs_1_
  116.1 0.0 collective-permute-done.15.refs_7_
  116.1 0.0 collective-permute-done.13.refs_5_
  116.1 0.0 collective-permute-done.11.refs_3_
  116.2 0.6 copy-done.11
  116.8 0.1 copy-done.12
  116.8 0.1 copy-done.13
  116.9 0.7 copy-done.14
  117.6 12.5 %experts.1 = (f32[4,64,1536]{2,1,0:T(8,128)}, bf16[4,64,1536]{2,1,0:T(8,128)(2,1)}) custom-call(s32[2]{0:T(128)} %pad_add_fusion.where_ref, s32[8,64,8]{2,1,0:T(8,128)} %copy.19.routes_ref, f32[1536,16]{1,0:T(8,128)} %copy.20.router_ref, bf16[2,1536,512]{2,1,0:T(8,128)(2,1)} %gate_hbm.1, bf16[2,1536,512]{2,1,0:T(8,128)(2,1)} %up_hbm.1, ...), custom_call_target="tpu_custom_call" | custom-call | tf_op jit(solution)/shard_map/experts/pallas_call | solution.py:418
  130.1 0.2 collective-permute-start.16
  130.3 2.4 %collective-permute-done.16 = bf16[4,64,1536]{2,1,0:T(8,128)(2,1)S(1)} collective-permute-done((bf16[4,64,1536]{2,1,0:T(8,128)(2,1)}, bf16[4,64,1536]{2,1,0:T(8,128)(2,1)S(1)}, u32[]{:S(2)}, u32[]{:S(2)}) %collective-permute-start.16) | collective-permute-done | bytes 786464 | tf_op jit(solution)/shard_map/ppermute | solution.py:48
  132.7 1.7 %fusion.5 = (bf16[4,64,1536]{2,1,0:T(8,128)(2,1)S(1)}, f32[4,64,1536]{2,1,0:T(8,128)S(1)}) fusion(f32[4,64,1536]{2,1,0:T(8,128)} %get-tuple-element.18, bf16[4,64,1536]{2,1,0:T(8,128)(2,1)S(1)} %collective-permute-done.16), kind=kLoop, calls=%fused_computation.11 | loop fusion | flops 1179648 | bytes 4718592 | tf_op jit(solution)/shard_map/convert_element_type | solution.py:503
  134.5 0.1 collective-permute-start.17
  134.5 2.5 %collective-permute-start.19 = (bf16[64,1536]{1,0:T(8,128)(2,1)S(1)}, bf16[64,1536]{1,0:T(8,128)(2,1)S(1)}, u32[]{:S(2)}, u32[]{:S(2)}) collective-permute-start(bf16[64,1536]{1,0:T(8,128)(2,1)S(1)} %get-tuple-element.23), channel_id=1, source_target_pairs={{0,24},{4,28},{8,16},{12,20},{16,8},{20,12},{24,0},{28,4},{1,25},{... | collective-permute-start | bytes 589832 | tf_op jit(solution)/shard_map/ppermute | solution.py:48
  137.1 0.9 collective-permute-start.18
  138.0 1.5 accepted.1
  139.5 2.0 %collective-permute-done.17 = bf16[64,1536]{1,0:T(8,128)(2,1)S(1)} collective-permute-done((bf16[64,1536]{1,0:T(8,128)(2,1)S(1)}, bf16[64,1536]{1,0:T(8,128)(2,1)S(1)}, u32[]{:S(2)}, u32[]{:S(2)}) %collective-permute-start.17) | collective-permute-done | bytes 196640 | tf_op jit(solution)/shard_map/ppermute | solution.py:48
  141.5 5.5 %collective-permute-done.19 = bf16[64,1536]{1,0:T(8,128)(2,1)S(1)} collective-permute-done((bf16[64,1536]{1,0:T(8,128)(2,1)S(1)}, bf16[64,1536]{1,0:T(8,128)(2,1)S(1)}, u32[]{:S(2)}, u32[]{:S(2)}) %collective-permute-start.19) | collective-permute-done | bytes 196640 | tf_op jit(solution)/shard_map/ppermute | solution.py:48
  147.0 8.3 %collective-permute-done.18 = bf16[64,1536]{1,0:T(8,128)(2,1)S(1)} collective-permute-done((bf16[64,1536]{1,0:T(8,128)(2,1)S(1)}, bf16[64,1536]{1,0:T(8,128)(2,1)S(1)}, u32[]{:S(2)}, u32[]{:S(2)}) %collective-permute-start.18) | collective-permute-done | bytes 196640 | tf_op jit(solution)/shard_map/ppermute | solution.py:48
  155.3 0.8 fusion.4
  (23 shorter events, 0.1 us)
Async XLA Ops:
  0.6 84.9 %collective-permute-start.7 = (bf16[384,1536]{1,0:T(8,128)(2,1)}, bf16[384,1536]{1,0:T(8,128)(2,1)S(1)}, u32[]{:S(2)}, u32[]{:S(2)}) collective-permute-start(bf16[384,1536]{1,0:T(8,128)(2,1)} %refs_4_.1), channel_id=1, source_target_pairs={{0,2},{1,3},{2,0},{3,1},{4,6},{5,7},{6,4},{7,5},{8,10},{9,11},{10,... | collective-permute-start | bytes 3538952 | tf_op jit(solution)/shard_map/ppermute | solution.py:48
  3.7 81.9 %collective-permute-start.6 = (bf16[384,1536]{1,0:T(8,128)(2,1)}, bf16[384,1536]{1,0:T(8,128)(2,1)S(1)}, u32[]{:S(2)}, u32[]{:S(2)}) collective-permute-start(bf16[384,1536]{1,0:T(8,128)(2,1)} %refs_4_.1), channel_id=1, source_target_pairs={{0,1},{1,0},{2,3},{3,2},{4,5},{5,4},{6,7},{7,6},{8,9},{9,8},{10,11... | collective-permute-start | bytes 3538952 | tf_op jit(solution)/shard_map/ppermute | solution.py:48
  5.2 80.4 %collective-permute-start.8 = (bf16[384,1536]{1,0:T(8,128)(2,1)}, bf16[384,1536]{1,0:T(8,128)(2,1)S(1)}, u32[]{:S(2)}, u32[]{:S(2)}) collective-permute-start(bf16[384,1536]{1,0:T(8,128)(2,1)} %refs_4_.1), channel_id=1, source_target_pairs={{0,3},{1,2},{2,1},{3,0},{4,7},{5,6},{6,5},{7,4},{8,11},{9,10},{10,... | collective-permute-start | bytes 3538952 | tf_op jit(solution)/shard_map/ppermute | solution.py:48
  8.9 52.3 %collective-permute-start.4 = (bf16[72,1536]{1,0:T(8,128)(2,1)}, bf16[72,1536]{1,0:T(8,128)(2,1)S(1)}, u32[]{:S(2)}, u32[]{:S(2)}) collective-permute-start(bf16[72,1536]{1,0:T(8,128)(2,1)} %get-tuple-element.11.pay_ref.refs_0_), channel_id=1, source_target_pairs={{0,3},{1,2},{2,1},{3,0},{4,7},{5,6},{6,5},{7,4},{8,11},{9,10},{10,... | collective-permute-start | bytes 663560 | tf_op jit(solution)/shard_map/ppermute | solution.py:48
  11.8 55.5 %collective-permute-start.2 = (bf16[72,1536]{1,0:T(8,128)(2,1)}, bf16[72,1536]{1,0:T(8,128)(2,1)S(1)}, u32[]{:S(2)}, u32[]{:S(2)}) collective-permute-start(bf16[72,1536]{1,0:T(8,128)(2,1)} %get-tuple-element.11.pay_ref.refs_0_), channel_id=1, source_target_pairs={{0,2},{1,3},{2,0},{3,1},{4,6},{5,7},{6,4},{7,5},{8,10},{9,11},{10,... | collective-permute-start | bytes 663560 | tf_op jit(solution)/shard_map/ppermute | solution.py:48
  61.2 1.6 %copy-start.3 = (bf16[72,1536]{1,0:T(8,128)(2,1)}, bf16[72,1536]{1,0:T(8,128)(2,1)S(1)}, u32[]{:S(2)}) copy-start(bf16[72,1536]{1,0:T(8,128)(2,1)S(1)} %collective-permute-done.4.pay_ref.refs_3_) | copy-start | bytes 663556
  61.2 12.1 %collective-permute-start = (bf16[72,1536]{1,0:T(8,128)(2,1)}, bf16[72,1536]{1,0:T(8,128)(2,1)}, u32[]{:S(2)}, u32[]{:S(2)}) collective-permute-start(bf16[72,1536]{1,0:T(8,128)(2,1)} %get-tuple-element.11.pay_ref.refs_0_), channel_id=1, source_target_pairs={{0,1},{1,0},{2,3},{3,2},{4,5},{5,4},{6,7},{7,6},{8,9},{9,8},{10,11... | collective-permute-start | bytes 663560 | tf_op jit(solution)/shard_map/ppermute | solution.py:48
  67.3 1.6 %copy-start.4 = (bf16[72,1536]{1,0:T(8,128)(2,1)}, bf16[72,1536]{1,0:T(8,128)(2,1)S(1)}, u32[]{:S(2)}) copy-start(bf16[72,1536]{1,0:T(8,128)(2,1)S(1)} %collective-permute-done.2.pay_ref.refs_2_) | copy-start | bytes 663556
  67.3 11.1 %collective-permute-start.5 = (bf16[64,1664]{1,0:T(8,128)(2,1)}, bf16[64,1664]{1,0:T(8,128)(2,1)S(1)}, u32[]{:S(2)}, u32[]{:S(2)}) collective-permute-start(bf16[64,1664]{1,0:T(8,128)(2,1)} %attend.7), channel_id=1, source_target_pairs={{0,3},{1,2},{2,1},{3,0},{4,7},{5,6},{6,5},{7,4},{8,11},{9,10},{10,... | collective-permute-start | bytes 638984 | tf_op jit(solution)/shard_map/ppermute | solution.py:48
  73.3 12.2 %collective-permute-start.3 = (bf16[64,1664]{1,0:T(8,128)(2,1)}, bf16[64,1664]{1,0:T(8,128)(2,1)S(1)}, u32[]{:S(2)}, u32[]{:S(2)}) collective-permute-start(bf16[64,1664]{1,0:T(8,128)(2,1)} %attend.6), channel_id=1, source_target_pairs={{0,2},{1,3},{2,0},{3,1},{4,6},{5,7},{6,4},{7,5},{8,10},{9,11},{10,... | collective-permute-start | bytes 638984 | tf_op jit(solution)/shard_map/ppermute | solution.py:48
  78.3 6.6 %copy-start.15 = (f32[1536]{0:T(1024)S(1)}, f32[1536]{0:T(1024)}, u32[]{:S(2)}) copy-start(f32[1536]{0:T(1024)} %param.25) | copy-start | bytes 18436
  78.3 6.6 %copy-start.6 = (bf16[64,1664]{1,0:T(8,128)(2,1)}, bf16[64,1664]{1,0:T(8,128)(2,1)S(1)}, u32[]{:S(2)}) copy-start(bf16[64,1664]{1,0:T(8,128)(2,1)S(1)} %collective-permute-done.5.refs_3_) | copy-start | bytes 638980
  78.3 7.2 %collective-permute-start.1 = (bf16[64,1664]{1,0:T(8,128)(2,1)}, bf16[64,1664]{1,0:T(8,128)(2,1)}, u32[]{:S(2)}, u32[]{:S(2)}) collective-permute-start(bf16[64,1664]{1,0:T(8,128)(2,1)} %attend.5), channel_id=1, source_target_pairs={{0,1},{1,0},{2,3},{3,2},{4,5},{5,4},{6,7},{7,6},{8,9},{9,8},{10,11... | collective-permute-start | bytes 638984 | tf_op jit(solution)/shard_map/ppermute | solution.py:48
  85.5 0.7 copy-start.7
  85.5 1.1 copy-start
  85.6 1.4 copy-start.1
  87.0 1.0 copy-start.2
  93.7 9.9 %collective-permute-start.14 = (bf16[64,1536]{1,0:T(8,128)(2,1)}, bf16[64,1536]{1,0:T(8,128)(2,1)S(1)}, u32[]{:S(2)}, u32[]{:S(2)}) collective-permute-start(bf16[64,1536]{1,0:T(8,128)(2,1)} %get-tuple-element.17.refs_0_), channel_id=1, source_target_pairs={{0,24},{4,28},{8,16},{12,20},{16,8},{20,12},{24,0},{28,4},{1,25},{... | collective-permute-start | bytes 589832 | tf_op jit(solution)/shard_map/ppermute | solution.py:48
  97.4 14.5 %collective-permute-start.12 = (bf16[64,1536]{1,0:T(8,128)(2,1)}, bf16[64,1536]{1,0:T(8,128)(2,1)S(1)}, u32[]{:S(2)}, u32[]{:S(2)}) collective-permute-start(bf16[64,1536]{1,0:T(8,128)(2,1)} %get-tuple-element.17.refs_0_), channel_id=1, source_target_pairs={{0,16},{4,20},{8,24},{12,28},{16,0},{20,4},{24,8},{28,12},{1,17},{... | collective-permute-start | bytes 589832 | tf_op jit(solution)/shard_map/ppermute | solution.py:48
  97.4 14.5 %collective-permute-start.10 = (bf16[64,1536]{1,0:T(8,128)(2,1)}, bf16[64,1536]{1,0:T(8,128)(2,1)S(1)}, u32[]{:S(2)}, u32[]{:S(2)}) collective-permute-start(bf16[64,1536]{1,0:T(8,128)(2,1)} %get-tuple-element.17.refs_0_), channel_id=1, source_target_pairs={{0,8},{4,12},{8,0},{12,4},{16,24},{20,28},{24,16},{28,20},{1,9},{5... | collective-permute-start | bytes 589832 | tf_op jit(solution)/shard_map/ppermute | solution.py:48
  98.2 17.9 %collective-permute-start.9 = (bf16[64,1536]{1,0:T(8,128)(2,1)}, bf16[64,1536]{1,0:T(8,128)(2,1)S(1)}, u32[]{:S(2)}, u32[]{:S(2)}) collective-permute-start(bf16[64,1536]{1,0:T(8,128)(2,1)} %get-tuple-element.17.refs_0_), channel_id=1, source_target_pairs={{0,4},{4,0},{8,12},{12,8},{16,20},{20,16},{24,28},{28,24},{1,5},{5... | collective-permute-start | bytes 589832 | tf_op jit(solution)/shard_map/ppermute | solution.py:48
  103.6 12.5 %copy-start.8 = (bf16[64,1536]{1,0:T(8,128)(2,1)}, bf16[64,1536]{1,0:T(8,128)(2,1)S(1)}, u32[]{:S(2)}) copy-start(bf16[64,1536]{1,0:T(8,128)(2,1)S(1)} %collective-permute-done.14.refs_6_) | copy-start | bytes 589828
  103.6 12.4 %collective-permute-start.15 = (bf16[64,1536]{1,0:T(8,128)(2,1)S(1)}, bf16[64,1536]{1,0:T(8,128)(2,1)S(1)}, u32[]{:S(2)}, u32[]{:S(2)}) collective-permute-start(bf16[64,1536]{1,0:T(8,128)(2,1)S(1)} %collective-permute-done.14.refs_6_), channel_id=1, source_target_pairs={{0,4},{4,0},{8,12},{12,8},{16,20},{20,16},{24,28},{28,24},{1,5},{5... | collective-permute-start | bytes 589832 | tf_op jit(solution)/shard_map/ppermute | solution.py:48
  111.9 4.2 %copy-start.9 = (bf16[64,1536]{1,0:T(8,128)(2,1)}, bf16[64,1536]{1,0:T(8,128)(2,1)S(1)}, u32[]{:S(2)}) copy-start(bf16[64,1536]{1,0:T(8,128)(2,1)S(1)} %collective-permute-done.12.refs_4_) | copy-start | bytes 589828
  111.9 4.2 %collective-permute-start.13 = (bf16[64,1536]{1,0:T(8,128)(2,1)S(1)}, bf16[64,1536]{1,0:T(8,128)(2,1)S(1)}, u32[]{:S(2)}, u32[]{:S(2)}) collective-permute-start(bf16[64,1536]{1,0:T(8,128)(2,1)S(1)} %collective-permute-done.12.refs_4_), channel_id=1, source_target_pairs={{0,4},{4,0},{8,12},{12,8},{16,20},{20,16},{24,28},{28,24},{1,5},{5... | collective-permute-start | bytes 589832 | tf_op jit(solution)/shard_map/ppermute | solution.py:48
  111.9 4.2 %copy-start.10 = (bf16[64,1536]{1,0:T(8,128)(2,1)}, bf16[64,1536]{1,0:T(8,128)(2,1)S(1)}, u32[]{:S(2)}) copy-start(bf16[64,1536]{1,0:T(8,128)(2,1)S(1)} %collective-permute-done.10.refs_2_) | copy-start | bytes 589828
  111.9 4.2 %collective-permute-start.11 = (bf16[64,1536]{1,0:T(8,128)(2,1)S(1)}, bf16[64,1536]{1,0:T(8,128)(2,1)S(1)}, u32[]{:S(2)}, u32[]{:S(2)}) collective-permute-start(bf16[64,1536]{1,0:T(8,128)(2,1)S(1)} %collective-permute-done.10.refs_2_), channel_id=1, source_target_pairs={{0,4},{4,0},{8,12},{12,8},{16,20},{20,16},{24,28},{28,24},{1,5},{5... | collective-permute-start | bytes 589832 | tf_op jit(solution)/shard_map/ppermute | solution.py:48
  116.1 0.7 copy-start.11
  116.1 0.7 copy-start.12
  116.1 0.8 copy-start.13
  116.9 0.7 copy-start.14
  130.1 2.6 %collective-permute-start.16 = (bf16[4,64,1536]{2,1,0:T(8,128)(2,1)}, bf16[4,64,1536]{2,1,0:T(8,128)(2,1)S(1)}, u32[]{:S(2)}, u32[]{:S(2)}) collective-permute-start(bf16[4,64,1536]{2,1,0:T(8,128)(2,1)} %get-tuple-element.19), channel_id=1, source_target_pairs={{0,4},{4,0},{8,12},{12,8},{16,20},{20,16},{24,28},{28,24},{1,5},{5... | collective-permute-start | bytes 2359304 | tf_op jit(solution)/shard_map/ppermute | solution.py:48
  134.4 20.9 %copy-start.5 = (f32[64,1536]{1,0:T(8,128)S(1)}, f32[64,1536]{1,0:T(8,128)}, u32[]{:S(2)}) copy-start(f32[64,1536]{1,0:T(8,128)} %get-tuple-element.16) | copy-start | bytes 1179652
  134.5 7.0 %collective-permute-start.17 = (bf16[64,1536]{1,0:T(8,128)(2,1)S(1)}, bf16[64,1536]{1,0:T(8,128)(2,1)S(1)}, u32[]{:S(2)}, u32[]{:S(2)}) collective-permute-start(bf16[64,1536]{1,0:T(8,128)(2,1)S(1)} %get-tuple-element.22), channel_id=1, source_target_pairs={{0,8},{4,12},{8,0},{12,4},{16,24},{20,28},{24,16},{28,20},{1,9},{5... | collective-permute-start | bytes 589832 | tf_op jit(solution)/shard_map/ppermute | solution.py:48
  134.5 12.5 %collective-permute-start.19 = (bf16[64,1536]{1,0:T(8,128)(2,1)S(1)}, bf16[64,1536]{1,0:T(8,128)(2,1)S(1)}, u32[]{:S(2)}, u32[]{:S(2)}) collective-permute-start(bf16[64,1536]{1,0:T(8,128)(2,1)S(1)} %get-tuple-element.23), channel_id=1, source_target_pairs={{0,24},{4,28},{8,16},{12,20},{16,8},{20,12},{24,0},{28,4},{1,25},{... | collective-permute-start | bytes 589832 | tf_op jit(solution)/shard_map/ppermute | solution.py:48
  137.1 18.2 %collective-permute-start.18 = (bf16[64,1536]{1,0:T(8,128)(2,1)S(1)}, bf16[64,1536]{1,0:T(8,128)(2,1)S(1)}, u32[]{:S(2)}, u32[]{:S(2)}) collective-permute-start(bf16[64,1536]{1,0:T(8,128)(2,1)S(1)} %get-tuple-element.24), channel_id=1, source_target_pairs={{0,16},{4,20},{8,24},{12,28},{16,0},{20,4},{24,8},{28,12},{1,17},{... | collective-permute-start | bytes 589832 | tf_op jit(solution)/shard_map/ppermute | solution.py:48

commit v2 on v1

--- a/solution.py
+++ b/solution.py
@@ -24,7 +24,7 @@
 BF = jnp.bfloat16
 F32 = jnp.float32
 LOG2E = 1.4426950408889634
-VMEM_LIMIT = 60 * 1024 * 1024
+MIB = 1024 * 1024
 
 _half = HD // 2
 INVERSE = np.tile(
@@ -32,12 +32,16 @@
 ).reshape(1, LANES)
 
 
-def params(**kw):
-    return pltpu.CompilerParams(vmem_limit_bytes=VMEM_LIMIT, **kw)
+def params(mib):
+    return pltpu.CompilerParams(vmem_limit_bytes=mib * MIB)
 
 
 def whole():
     return pl.BlockSpec(memory_space=pltpu.VMEM)
+
+
+def blocked(x):
+    return pl.BlockSpec(x.shape, lambda i: (0,) * x.ndim)
 
 
 def scalars():
@@ -138,25 +142,77 @@
             jax.ShapeDtypeStruct((draft, draft), F32),
             jax.ShapeDtypeStruct((requests * draft, LANES), F32),
         ),
-        in_specs=[scalars(), scalars(), scalars(), whole(), whole(), whole(), whole()],
+        grid=(1,),
+        in_specs=[scalars(), scalars(), scalars()]
+        + [blocked(x) for x in (parents, INVERSE, queries, kv)],
         out_specs=(whole(),) * 5,
         scratch_shapes=[
             pltpu.VMEM(kv.shape, F32),
             pltpu.VMEM((n, LANES), F32),
             pltpu.VMEM((requests, draft, draft), F32),
         ],
-        compiler_params=params(),
+        compiler_params=params(8),
         name="prelude",
     )(where, cache_len, path, parents, jnp.asarray(INVERSE), queries, kv)
 
 
+def prepare_kernel(cache_ref, routes_ref, router_ref, out_ref, bias_ref, route_w_ref, kv_f):
+    cells = out_ref.shape[2]
+    kv_f[...] = cache_ref[0].astype(F32)
+    for j in range(2 * PAIRS):
+        out_ref[0, j] = kv_f[pl.ds(j, cells, stride=2 * PAIRS), :].astype(BF)
+
+    @pl.when(pl.program_id(0) == 0)
+    def _():
+        experts = router_ref.shape[0]
+        router = router_ref[...]
+        high = router.astype(BF)
+        route_w_ref[:experts, :] = high
+        route_w_ref[experts:, :] = (router - high.astype(F32)).astype(BF)
+        for d in range(routes_ref.shape[0]):
+            chosen = routes_ref[d]
+            expert = lax.broadcasted_iota(jnp.int32, (experts, chosen.shape[1]), 0)
+            hit = expert == chosen[0:1, :]
+            for k in range(1, chosen.shape[0]):
+                hit = hit | (expert == chosen[k : k + 1, :])
+            bias_ref[d] = jnp.where(hit, 0.0, NEG).T
+
+
+def prepare(cache, routes, router):
+    requests, span, _ = cache.shape
+    cells = span // (2 * PAIRS)
+    experts, width = router.shape
+    blocks, top, n = routes.shape
+    return pl.pallas_call(
+        prepare_kernel,
+        out_shape=(
+            jax.ShapeDtypeStruct((requests, 2 * PAIRS, cells, LANES), BF),
+            jax.ShapeDtypeStruct((blocks, n, experts), F32),
+            jax.ShapeDtypeStruct((2 * experts, width), BF),
+        ),
+        grid=(requests,),
+        in_specs=[
+            pl.BlockSpec((1, span, LANES), lambda r: (r, 0, 0)),
+            pl.BlockSpec((blocks, top, n), lambda r: (0, 0, 0)),
+            pl.BlockSpec((experts, width), lambda r: (0, 0)),
+        ],
+        out_specs=(
+            pl.BlockSpec((1, 2 * PAIRS, cells, LANES), lambda r: (r, 0, 0, 0)),
+            pl.BlockSpec((blocks, n, experts), lambda r: (0, 0, 0)),
+            pl.BlockSpec((2 * experts, width), lambda r: (0, 0)),
+        ),
+        scratch_shapes=[pltpu.VMEM((span, LANES), F32)],
+        compiler_params=params(12),
+        name="prepare",
+    )(cache, routes, router)
+
+
 def attend_kernel(
-    step, near, where_ref, len_ref, pay_ref, kv_ref, key_ref, val_ref, anc_ref, pos_ref,
-    out_ref, kv_f,
+    step, near, where_ref, len_ref, pay_ref, kv_ref, key_ref, val_ref, anc_ref, pos_ref, out_ref
 ):
     draft = anc_ref.shape[0]
     n = key_ref.shape[0]
-    cells = kv_ref.shape[1] // (2 * PAIRS)
+    cells = kv_ref.shape[2]
     me = where_ref[0]
     start = (me ^ step) * n
     request = start // draft
@@ -181,15 +237,14 @@
         seen = jnp.where(same, line, 0.0)
         near_bias = jnp.where(seen > 0.5, 0.0, NEG)
         near_bias = jnp.concatenate([near_bias] * (2 * GROUPS), axis=0)
-    kv_f[...] = kv_ref[0].astype(F32)
     low = lane_index((n, LANES)) < HD
     lane = lane_index((n, LANES))
     stats = jnp.zeros((n, LANES), F32)
     turn = (((1,), (1,)), ((), ()))
     factor = HD ** (-0.5) * LOG2E
     for b in range(PAIRS):
-        keys = kv_f[pl.ds(2 * b, cells, stride=2 * PAIRS), :].astype(BF)
-        vals = kv_f[pl.ds(2 * b + 1, cells, stride=2 * PAIRS), :].astype(BF)
+        keys = kv_ref[request, 2 * b]
+        vals = kv_ref[request, 2 * b + 1]
         blocks = [
             pay_ref[:n, (GROUPS * b + i) * LANES : (GROUPS * b + i + 1) * LANES]
             for i in range(GROUPS)
@@ -242,51 +297,204 @@
 
 def attend(step, near, where, cache_len, payload, cache, keys, vals, ancestry, pos):
     n = keys.shape[0]
-    draft = ancestry.shape[0]
-    span = cache.shape[1]
-
-    def cache_block(i, where_ref, len_ref):
-        return ((where_ref[0] ^ step) * n // draft, 0, 0)
-
-    def full(x):
-        return pl.BlockSpec(x.shape, lambda i, *_: (0,) * x.ndim)
-
     return pl.pallas_call(
         functools.partial(attend_kernel, step, near),
         out_shape=jax.ShapeDtypeStruct((n, QH * HD + LANES), BF),
-        grid_spec=pltpu.PrefetchScalarGridSpec(
-            num_scalar_prefetch=2,
-            grid=(1,),
-            in_specs=[
-                full(payload),
-                pl.BlockSpec((1, span, LANES), cache_block),
-                full(keys),
-                full(vals),
-                full(ancestry),
-                full(pos),
-            ],
-            out_specs=pl.BlockSpec((n, QH * HD + LANES), lambda i, *_: (0, 0)),
-            scratch_shapes=[pltpu.VMEM((span, LANES), F32)],
-        ),
-        compiler_params=params(),
+        in_specs=[scalars(), scalars()] + [whole()] * 6,
+        out_specs=whole(),
+        compiler_params=params(12),
         name="attend",
     )(where, cache_len, payload, cache, keys, vals, ancestry, pos)
 
 
+SPAN = 2 * GROUPS
+
+
+def attend_split_kernel(
+    step, near, count, where_ref, len_ref, pay_ref, kv_ref, key_ref, val_ref, anc_ref, pos_ref, *refs
+):
+    out_refs = refs[-count:]
+    n = key_ref.shape[0]
+    cells = kv_ref.shape[2]
+    me = where_ref[0]
+    start = (me ^ step) * n
+    request = me ^ step
+    place = pos_ref[pl.ds(pl.multiple_of(start, 8), n), :][:, :1]
+    key_pos = (lane_index((n, cells)) + me * cells).astype(F32)
+    far_ok = (key_pos < len_ref[request].astype(F32)) & (
+        (key_pos < SINKS) | (place - key_pos < WINDOW)
+    )
+    bias = jnp.where(far_ok, 0.0, NEG)
+    bias = jnp.concatenate([bias] * SPAN, axis=0)
+    if near:
+        near_bias = jnp.where(anc_ref[...] > 0.5, 0.0, NEG)
+        near_bias = jnp.concatenate([near_bias] * SPAN, axis=0)
+    lane = lane_index((n, LANES))
+    low = lane < HD
+    turn = (((1,), (1,)), ((), ()))
+    factor = HD ** (-0.5) * LOG2E
+    for j in range(count):
+        b = me ^ j
+        stats = jnp.zeros((n, LANES), F32) if near else out_refs[j][count * GROUPS].astype(F32)
+        blocks = [
+            pay_ref[:n, pl.ds(pl.multiple_of((GROUPS * b + i) * LANES, LANES), LANES)]
+            for i in range(GROUPS)
+        ]
+        zero = jnp.zeros((n, LANES), BF)
+        rows = jnp.concatenate(
+            [jnp.where(low, x, zero) for x in blocks] + [jnp.where(low, zero, x) for x in blocks],
+            axis=0,
+        )
+        scores = (
+            lax.dot_general(rows, kv_ref[request, 2 * b], turn, preferred_element_type=F32) * factor
+            + bias
+        )
+        top = jnp.max(scores, axis=-1, keepdims=True)
+        if near:
+            at_pair = pl.ds(pl.multiple_of(b * LANES, LANES), LANES)
+            near_scores = (
+                lax.dot_general(rows, key_ref[:, at_pair], turn, preferred_element_type=F32) * factor
+                + near_bias
+            )
+            top = jnp.maximum(top, jnp.max(near_scores, axis=-1, keepdims=True))
+        top = jnp.maximum(top, FLOOR)
+        top = (top + jnp.abs(top) * (2.0**-7)).astype(BF).astype(F32)
+        weights = jnp.exp2(scores - top)
+        total = jnp.sum(weights, axis=-1, keepdims=True)
+        blend = jnp.dot(weights.astype(BF), kv_ref[request, 2 * b + 1], preferred_element_type=F32)
+        if near:
+            near_weights = jnp.exp2(near_scores - top)
+            total = total + jnp.sum(near_weights, axis=-1, keepdims=True)
+            blend = blend + jnp.dot(
+                near_weights.astype(BF), val_ref[:, at_pair], preferred_element_type=F32
+            )
+        high = total.astype(BF).astype(F32)
+        rest = total - high
+        for i in range(GROUPS):
+            first = slice(i * n, (i + 1) * n)
+            second = slice((GROUPS + i) * n, (GROUPS + i + 1) * n)
+            out_refs[j][step * GROUPS + i] = jnp.where(low, blend[first], blend[second]).astype(BF)
+            for part, rows_of in enumerate((first, second)):
+                at = 3 * SPAN * step + 2 * i + part
+                stats = jnp.where(lane == at, top[rows_of], stats)
+                stats = jnp.where(lane == at + SPAN, high[rows_of], stats)
+                stats = jnp.where(lane == at + 2 * SPAN, rest[rows_of], stats)
+        out_refs[j][count * GROUPS] = stats.astype(BF)
+
+
+def attend_split(step, count, where, cache_len, payload, cache, keys, vals, ancestry, pos, outs):
+    n = keys.shape[0]
+    shape = jax.ShapeDtypeStruct((count * GROUPS + 1, n, LANES), BF)
+    return pl.pallas_call(
+        functools.partial(attend_split_kernel, step, step == 0, count),
+        out_shape=(shape,) * count,
+        in_specs=[scalars(), scalars()] + [whole()] * (6 + len(outs)),
+        out_specs=(whole(),) * count,
+        input_output_aliases={8 + j: j for j in range(len(outs))},
+        compiler_params=params(12),
+        name="attend",
+    )(where, cache_len, payload, cache, keys, vals, ancestry, pos, *outs)
+
+
+def join_split_kernel(count, weight_ref, *refs):
+    parts, out_refs, att = refs[:count], refs[count:-1], refs[-1]
+    n = parts[0].shape[1]
+    lane = lane_index((n, LANES))
+    low = lane < HD
+    shifts = [p[count * GROUPS].astype(F32) for p in parts]
+    totals = [
+        pltpu.roll(s, LANES - SPAN, axis=1) + pltpu.roll(s, LANES - 2 * SPAN, axis=1)
+        for s in shifts
+    ]
+    for k in range(count):
+        moves = [(LANES - 3 * SPAN * (j ^ k)) % LANES for j in range(count)]
+        tops = [pltpu.roll(s, m, axis=1) if m else s for s, m in zip(shifts, moves)]
+        sums = [pltpu.roll(s, m, axis=1) if m else s for s, m in zip(totals, moves)]
+        top = functools.reduce(jnp.maximum, tops)
+        scales = [jnp.exp2(t - top) for t in tops]
+        inverse = 1.0 / functools.reduce(jnp.add, [a * b for a, b in zip(scales, sums)])
+        scales = [scale * inverse for scale in scales]
+        joined = []
+        for i in range(GROUPS):
+            acc = jnp.zeros((n, LANES), F32)
+            for j in range(count):
+                by = jnp.where(
+                    low, scales[j][:, 2 * i : 2 * i + 1], scales[j][:, 2 * i + 1 : 2 * i + 2]
+                )
+                acc = acc + by * parts[j][(j ^ k) * GROUPS + i].astype(F32)
+            joined.append(acc)
+        turned = pltpu.roll(joined[1], HD, axis=1)
+        back = (
+            jnp.where(low, joined[0], turned),
+            jnp.where(low, joined[2], joined[0]),
+            jnp.where(low, turned, joined[2]),
+        )
+        for i in range(GROUPS):
+            att[k * n : (k + 1) * n, i * LANES : (i + 1) * LANES] = back[i].astype(BF)
+    for k in list(range(1, count)) + [0]:
+        product = jnp.dot(att[k * n : (k + 1) * n, :], weight_ref[...], preferred_element_type=F32)
+        out_refs[k][...] = product.astype(out_refs[k].dtype)
+
+
+def join_split(weight, parts):
+    count = len(parts)
+    n = parts[0].shape[1]
+    width = weight.shape[1]
+    return pl.pallas_call(
+        functools.partial(join_split_kernel, count),
+        out_shape=tuple(
+            jax.ShapeDtypeStruct((n, width), BF if k else F32) for k in range(count)
+        ),
+        in_specs=[whole()] * (1 + count),
+        out_specs=(whole(),) * count,
+        scratch_shapes=[pltpu.VMEM((count * n, weight.shape[0]), BF)],
+        compiler_params=params(12),
+        name="join",
+    )(weight, *parts)
+
+
+def norm_kernel(hidden_ref, gain_ref, own_ref, *refs):
+    others, (mixed_ref, normed_ref) = refs[:-2], refs[-2:]
+    mixed = hidden_ref[...].astype(F32) + own_ref[...]
+    for other in others:
+        mixed = mixed + other[...].astype(F32)
+    mixed_ref[...] = mixed
+    square = jnp.mean(mixed * mixed, axis=-1, keepdims=True)
+    normed_ref[...] = (mixed * lax.rsqrt(square + 1e-06) * gain_ref[...]).astype(BF)
+
+
+def norm(hidden_in, gain, own, others):
+    return pl.pallas_call(
+        norm_kernel,
+        out_shape=(
+            jax.ShapeDtypeStruct(hidden_in.shape, F32),
+            jax.ShapeDtypeStruct(hidden_in.shape, BF),
+        ),
+        in_specs=[whole()] * (3 + len(others)),
+        out_specs=(whole(), whole()),
+        compiler_params=params(4),
+        name="norm",
+    )(hidden_in, gain, own, *others)
+
+
 def join_kernel(count, where_ref, *refs):
     parts, rest = refs[:count], refs[count:]
-    pieces, rest = rest[:count], rest[count:]
+    shares = 2 * count - 1
+    pieces, rest = rest[:shares], rest[shares:]
     hidden_ref, gain_ref, mixed_ref, normed_ref, att, weight, sems = rest
     n = hidden_ref.shape[0]
     depth = pieces[0].shape[0]
+    half = depth // CORES
     width = QH * HD
     me = where_ref[0]
+    core = where_ref[1] % CORES
+    starts = [me * depth]
+    for k in range(1, count):
+        starts += [(me ^ k) * depth + core * half, (me ^ k) * depth + (1 - core) * half]
     copies = []
-    for k in range(count):
-        at = pl.multiple_of((me ^ k) * depth, 16)
-        copies.append(
-            pltpu.make_async_copy(pieces[k], weight.at[pl.ds(at, depth), :], sems.at[k])
-        )
+    for j, (piece, start) in enumerate(zip(pieces, starts)):
+        rows = weight.at[pl.ds(pl.multiple_of(start, 16), piece.shape[0]), :]
+        copies.append(pltpu.make_async_copy(piece, rows, sems.at[j]))
         copies[-1].start()
     stats = [p[:, width:].astype(F32) for p in parts]
     top = stats[0]
@@ -342,101 +550,61 @@
         ),
         in_specs=[scalars()]
         + [whole()] * count
-        + [pl.BlockSpec(memory_space=pl.ANY)] * count
+        + [pl.BlockSpec(memory_space=pl.ANY)] * len(pieces)
         + [whole(), whole()],
         out_specs=(whole(), whole()),
         scratch_shapes=[
             pltpu.VMEM((n, inner), BF),
             pltpu.VMEM((inner, width), BF),
-            pltpu.SemaphoreType.DMA((count,)),
+            pltpu.SemaphoreType.DMA((len(pieces),)),
         ],
-        compiler_params=params(),
+        compiler_params=params(14),
         name="join",
     )(where, *parts, *pieces, hidden_in, gain)
 
 
 def experts_kernel(
-    count, where_ref, routes_ref, router_ref, gate_hbm, up_hbm, down_hbm, *refs
+    step, where_ref, bias_ref, route_ref, wg, wu, wd, a_ref, b_ref, own_ref, other_ref
 ):
-    slots, (own_ref, other_ref, x, acc, gates_s, wg, wu, wd, sems) = refs[:count], refs[count:]
-    n, width = slots[0].shape
-    local = gate_hbm.shape[0]
-    experts = router_ref.shape[1]
+    n, width = a_ref.shape
+    local = wg.shape[0]
+    experts = bias_ref.shape[2]
     me = where_ref[1]
-    copies = []
+    x = jnp.concatenate([a_ref[...], b_ref[...]], axis=0)
+    logits = lax.dot_general(
+        x, route_ref[...], (((1,), (1,)), ((), ())), preferred_element_type=F32
+    )
+    logits = logits[:, :experts] + logits[:, experts:]
+    first = CORES * step
+    logits = logits + jnp.concatenate([bias_ref[me ^ first], bias_ref[me ^ (first + 1)]], axis=0)
+    gates = jnp.exp(logits - jnp.max(logits, axis=-1, keepdims=True))
+    gates = gates / jnp.sum(gates, axis=-1, keepdims=True)
+    lane = lane_index(gates.shape)
+    acc = None
     for e in range(local):
-        for j, (src, dst) in enumerate(((gate_hbm, wg), (up_hbm, wu), (down_hbm, wd))):
-            copies.append(pltpu.make_async_copy(src.at[e], dst.at[e], sems.at[3 * e + j]))
-            copies[-1].start()
-    router = router_ref[...]
-    router_high = router.astype(BF)
-    router_low = (router - router_high.astype(F32)).astype(BF)
-    for s in range(count):
-        x[s * n : (s + 1) * n, :] = slots[s][...]
-    rows = count * n
-    logits = jnp.dot(x[...], router_high, preferred_element_type=F32) + jnp.dot(
-        x[...], router_low, preferred_element_type=F32
-    )
-    lane = lane_index((n, experts))
-    for s in range(count):
-        chosen = routes_ref[me ^ s]
-        hit = lane == chosen[:, 0:1]
-        for k in range(1, chosen.shape[1]):
-            hit = hit | (lane == chosen[:, k : k + 1])
-        part = jnp.where(hit, logits[s * n : (s + 1) * n, :], NEG)
-        part = jnp.exp(part - jnp.max(part, axis=-1, keepdims=True))
-        part = jnp.where(hit, part, 0.0)
-        gates_s[s * n : (s + 1) * n, :] = part / jnp.sum(part, axis=-1, keepdims=True)
-    tile = min(rows, 256)
-    for e in range(local):
-        for j in range(3):
-            copies[3 * e + j].wait()
-        for t in range(rows // tile):
-            span = slice(t * tile, (t + 1) * tile)
-            block = x[span, :]
-            gate_hidden = jnp.dot(block, wg[e], preferred_element_type=F32)
-            up_hidden = jnp.dot(block, wu[e], preferred_element_type=F32)
-            activated = (gate_hidden / (1.0 + jnp.exp(-gate_hidden)) * up_hidden).astype(BF)
-            made = jnp.dot(activated, wd[e], preferred_element_type=F32).astype(BF).astype(F32)
-            mine = lane_index((tile, experts)) == me * local + e
-            gate = jnp.sum(jnp.where(mine, gates_s[span, :], 0.0), axis=-1, keepdims=True)
-            if e == 0:
-                acc[span, :] = gate * made
-            else:
-                acc[span, :] = acc[span, :] + gate * made
-    for s in range(count):
-        if s % CORES == 0:
-            own_ref[s // CORES] = acc[s * n : (s + 1) * n, :]
-        else:
-            other_ref[s // CORES] = acc[s * n : (s + 1) * n, :].astype(BF)
-
-
-def experts_part(where, routes, router, w_gate, w_up, w_down, slots):
-    count = len(slots)
-    n, width = slots[0].shape
-    local, _, hidden = w_gate.shape
-    return pl.pallas_call(
-        functools.partial(experts_kernel, count),
+        gate_hidden = jnp.dot(x, wg[e], preferred_element_type=F32)
+        up_hidden = jnp.dot(x, wu[e], preferred_element_type=F32)
+        activated = (gate_hidden / (1.0 + jnp.exp(-gate_hidden)) * up_hidden).astype(BF)
+        made = jnp.dot(activated, wd[e], preferred_element_type=F32).astype(BF).astype(F32)
+        gate = jnp.sum(jnp.where(lane == me * local + e, gates, 0.0), axis=-1, keepdims=True)
+        acc = gate * made if acc is None else acc + gate * made
+    own_ref[...] = acc[:n]
+    other_ref[...] = acc[n:].astype(BF)
+
+
+def experts_part(step, where, bias, route, w_gate, w_up, w_down, a, b):
+    n, width = a.shape
+    return pl.pallas_call(
+        functools.partial(experts_kernel, step),
         out_shape=(
-            jax.ShapeDtypeStruct((count // CORES, n, width), F32),
-            jax.ShapeDtypeStruct((count // CORES, n, width), BF),
+            jax.ShapeDtypeStruct((n, width), F32),
+            jax.ShapeDtypeStruct((n, width), BF),
         ),
-        in_specs=[scalars(), whole(), whole()]
-        + [pl.BlockSpec(memory_space=pl.ANY)] * 3
-        + [whole()] * count,
+        in_specs=[scalars()] + [whole()] * 7,
         out_specs=(whole(), whole()),
-        scratch_shapes=[
-            pltpu.VMEM((count * n, width), BF),
-            pltpu.VMEM((count * n, width), F32),
-            pltpu.VMEM((count * n, router.shape[1]), F32),
-            pltpu.VMEM((local, width, hidden), BF),
-            pltpu.VMEM((local, width, hidden), BF),
-            pltpu.VMEM((local, hidden, width), BF),
-            pltpu.SemaphoreType.DMA((3 * local,)),
-        ],
-        compiler_params=params(),
+        compiler_params=params(12),
         name="experts",
-    )(where, routes, router, w_gate, w_up, w_down, *slots)
+    )(where, bias, route, w_gate, w_up, w_down, a, b)
 
 
 def accepted_kernel(count, n, where_ref, *refs):
@@ -458,7 +626,7 @@
         grid=(1,),
         in_specs=[scalars()] + [block] * count,
         out_specs=pl.BlockSpec((requests, entries, 2 * KVH * HD), lambda i: (0, 0, 0)),
-        compiler_params=params(),
+        compiler_params=params(4),
         name="accepted",
     )(where, *payloads)
 
@@ -483,26 +651,54 @@
     )
     cache = rows_by_lane_block(cache_kv)
     payloads = [payload] + [exchange(payload, "tensor", tensor, k) for k in range(1, tensor)]
-    pieces = [w_out] + [exchange(w_out, "tensor", tensor, k) for k in range(1, tensor)]
-    parts = []
-    for k in range(tensor):
-        near = k < max(1, draft // n)
-        part = attend(k, near, where, cache_len, payloads[k], cache, keys, vals, ancestry, pos)
-        parts.append(part if k == 0 else exchange(part, "tensor", tensor, k))
+    unpacked, bias, route = prepare(cache, jnp.swapaxes(routes, 1, 2), router.T)
+    gain = norm_gain.reshape(1, -1)
+    if n == draft and tensor == PAIRS:
+        parts = ()
+        for k in range(tensor):
+            parts = attend_split(
+                k, tensor, where, cache_len, payloads[k], unpacked, keys, vals, ancestry, pos, parts
+            )
+        parts = [parts[0]] + [exchange(parts[j], "tensor", tensor, j) for j in range(1, tensor)]
+        products = join_split(w_out, parts)
+        others = [exchange(products[k], "tensor", tensor, k) for k in range(1, tensor)]
+        mixed, normed = norm(hidden_in, gain, products[0], others)
+    else:
+        half = w_out.shape[0] // CORES
+        mine = lax.dynamic_slice_in_dim(w_out, lax.axis_index("dp") % CORES * half, half, 0)
+        mine = lax.optimization_barrier((mine, *payloads[1:]))[0]
+        fetched = [exchange(mine, "tensor", tensor, k) for k in range(1, tensor)]
+        parts = []
+        for k in range(tensor):
+            near = k < max(1, draft // n)
+            part = attend(k, near, where, cache_len, payloads[k], unpacked, keys, vals, ancestry, pos)
+            parts.append(part if k == 0 else exchange(part, "tensor", tensor, k))
+        pieces = [w_out]
+        for piece in fetched:
+            pieces += [piece, exchange(piece, "dp", data, 1)]
+        mixed, normed = join(where, parts, pieces, hidden_in, gain)
     compacted = accepted(where, payloads, requests, path.shape[1], n)
-    mixed, normed = join(where, parts, pieces, hidden_in, norm_gain.reshape(1, -1))
 
     steps = data // CORES
-    lines = [normed] + [exchange(normed, "dp", data, CORES * k) for k in range(1, steps)]
-    slots = []
-    for line in lines:
-        slots += [line, exchange(line, "dp", data, 1)]
-    own, other = experts_part(where, routes, router, w_gate, w_up, w_down, slots)
-    chip = own + exchange(other, "dp", data, 1).astype(F32)
-    total = mixed + chip[0]
-    low = chip.astype(BF)
-    for k in range(1, steps):
-        total = total + exchange(low[k], "dp", data, CORES * k).astype(F32)
+    lines = {0: normed}
+    reach = steps // 2
+    while reach:
+        for k in [k for k in lines if k % (2 * reach) == 0]:
+            lines[k + reach] = exchange(lines[k], "dp", data, CORES * reach)
+        reach //= 2
+    total = mixed
+    last = None
+    for k in sorted(lines, key=lambda k: (bin(k).count("1"), k)):
+        line = lines[k]
+        if last is not None:
+            line = lax.optimization_barrier((line, last))[0]
+        twin = exchange(line, "dp", data, 1)
+        own, other = experts_part(k, where, bias, route, w_gate, w_up, w_down, line, twin)
+        last = own
+        chip = own + exchange(other, "dp", data, 1).astype(F32)
+        if k:
+            chip = exchange(chip.astype(BF), "dp", data, CORES * k).astype(F32)
+        total = total + chip
     return total.astype(BF), compacted
 
 

time: 157 us -> 104 us (0.66)
  the two profiles are of different devices: /device:TPU:0 before, /device:TPU:16 now
where the time goes in v2:
time: 104 us; the launch traced here: 103 us
  waiting for transfers between devices  45.1 us (43%)
  Pallas kernels  26.5 us (25%)
  starting transfers between devices  21.4 us (21%)
  local copies, waits for them, and re-layouts  8.39 us (8%)
    ppermute x23, waiting for transfers between devices, exchange(): return lax.ppermute(x, axis, [(i, i ^ step) for i in range(size)])  45.1 us
    ppermute x23, starting transfers between devices, exchange(): return lax.ppermute(x, axis, [(i, i ^ step) for i in range(size)])  21.4 us
    pallas_call x4, Pallas kernels, experts_part(): pl.pallas_call(functools.partial(experts_kernel, step), out_shape=(jax.Sh...  9.72 us
    pallas_call x4, Pallas kernels, attend_split(): pl.pallas_call(functools.partial(attend_split_kernel, step, step == 0, co...  8.57 us
    unnamed x32, local copies, waits for them, and re-layouts  8.38 us
    pallas_call x1, Pallas kernels, prepare(): pl.pallas_call(prepare_kernel, out_shape=(jax.ShapeDtypeStruct((requests,...  2.53 us
    pallas_call x1, Pallas kernels, join_split(): pl.pallas_call(functools.partial(join_split_kernel, count), out_shape=tup...  2.34 us
  transfers between devices with their start and end apart: 23, of which 11 were waited for; matrix products, arithmetic and copies ran while one was open for 0% of the time, Pallas kernels for 19%

profile of v2, /device:TPU:16, one launch (start us, length us, event | category | flops | bytes accessed | tf_op | source)
XLA Modules:
  0.0 103.3 jit_solution(3948275038986713046)
XLA Ops:
  0.6 0.0 copy-start.11
  0.6 0.1 pad_add_fusion.where_ref
  0.7 0.9 copy-done.6
  1.7 0.9 copy-done.7
  2.6 0.7 copy-done.10
  3.2 0.7 copy-done.12
  3.9 0.7 copy-done.13
  4.6 0.7 copy-done.14
  5.2 1.9 %prelude.1 = (bf16[72,1536]{1,0:T(8,128)(2,1)S(1)}, bf16[64,512]{1,0:T(8,128)(2,1)S(1)}, bf16[64,512]{1,0:T(8,128)(2,1)S(1)}, f32[64,64]{1,0:T(8,128)S(1)}, f32[256,128]{1,0:T(8,128)S(1)}) custom-call(s32[2]{0:T(128)S(1)} %pad_add_fusion.where_ref, s32[4]{0:T(128)S(1)} %copy-done.10, s32[4,8]{1,0:T(4,128)S(1)} %copy-done.12, s32[4,64]{1,0:T(4,128)S(1)} %copy-done.13, ...), custom_call_target="tpu_custom_call" | custom-call | tf_op jit(solution)/shard_map/prelude/pallas_call | solution.py:136
  7.1 1.6 %collective-permute-start.2 = (bf16[72,1536]{1,0:T(8,128)(2,1)S(1)}, bf16[72,1536]{1,0:T(8,128)(2,1)S(1)}, u32[]{:S(2)}, u32[]{:S(2)}) collective-permute-start(bf16[72,1536]{1,0:T(8,128)(2,1)S(1)} %get-tuple-element.43.pay_ref.refs_0_), channel_id=1, source_target_pairs={{0,1},{1,0},{2,3},{3,2},{4,5},{5,4},{6,7},{7,6},{8,9},{9,8},{10,11... | collective-permute-start | bytes 663560 | tf_op jit(solution)/shard_map/ppermute | solution.py:52
  8.7 1.5 %collective-permute-start.1 = (bf16[72,1536]{1,0:T(8,128)(2,1)S(1)}, bf16[72,1536]{1,0:T(8,128)(2,1)S(1)}, u32[]{:S(2)}, u32[]{:S(2)}) collective-permute-start(bf16[72,1536]{1,0:T(8,128)(2,1)S(1)} %get-tuple-element.43.pay_ref.refs_0_), channel_id=1, source_target_pairs={{0,2},{1,3},{2,0},{3,1},{4,6},{5,7},{6,4},{7,5},{8,10},{9,11},{10,... | collective-permute-start | bytes 663560 | tf_op jit(solution)/shard_map/ppermute | solution.py:52
  10.2 0.5 collective-permute-start
  10.7 2.2 %copy-done.3 = bf16[4,512,2,512]{3,2,1,0:T(2,128)(2,1)S(1)} copy-done((bf16[4,512,2,512]{3,2,1,0:T(2,128)(2,1)S(1)}, bf16[4,512,2,512]{3,2,1,0:T(2,128)(2,1)}, u32[]{:S(2)}) %copy-start.3) | copy-done | bytes 4194328
  12.9 0.9 copy-done.8
  13.8 0.8 copy-done.9
  14.5 2.5 %prepare.1 = (bf16[4,8,512,128]{3,2,1,0:T(8,128)(2,1)S(1)}, f32[8,64,16]{2,1,0:T(8,128)S(1)}, bf16[32,1536]{1,0:T(8,128)(2,1)S(1)}) custom-call(bf16[4,4096,128]{2,1,0:T(8,128)(2,1)S(1)} %bitcast.14, s32[8,8,64]{2,1,0:T(8,128)S(1)} %bitcast.17, f32[16,1536]{1,0:T(8,128)S(1)} %bitcast.16), custom_call_target="tpu_custom_call" | custom-call | tf_op jit(solution)/shard_map/prepare/pallas_call | solution.py:186
  17.1 2.7 %attend.4 = (bf16[13,64,128]{2,1,0:T(8,128)(2,1)S(1)}, bf16[13,64,128]{2,1,0:T(8,128)(2,1)S(1)}, bf16[13,64,128]{2,1,0:T(8,128)(2,1)S(1)}, bf16[13,64,128]{2,1,0:T(8,128)(2,1)S(1)}) custom-call(s32[2]{0:T(128)S(1)} %pad_add_fusion.where_ref, s32[4]{0:T(128)S(1)} %copy-done.11, bf16[72,1536]{1,0:T(8,128)(2,1)S(1)} %get-tuple-element.43.pay_ref.refs_0_, ...), custom_call_target="tpu_custom_call" | custom-call | tf_op jit(solution)/shard_map/attend/pallas_call | solution.py:388
  19.8 0.0 collective-permute-done.2.pay_ref.refs_1_
  19.8 1.9 %attend.5 = (bf16[13,64,128]{2,1,0:T(8,128)(2,1)S(1)}, bf16[13,64,128]{2,1,0:T(8,128)(2,1)S(1)}, bf16[13,64,128]{2,1,0:T(8,128)(2,1)S(1)}, bf16[13,64,128]{2,1,0:T(8,128)(2,1)S(1)}) custom-call(s32[2]{0:T(128)S(1)} %pad_add_fusion.where_ref, s32[4]{0:T(128)S(1)} %copy-done.11, ...), custom_call_target="tpu_custom_call", output_to_operand_aliasing={{0}: (8, {}), {1}: (9, {}), {2}: (10, {}), {3}: (11, {})} | custom-call | tf_op jit(solution)/shard_map/attend/pallas_call | solution.py:388
  21.8 0.0 collective-permute-done.1.pay_ref.refs_2_
  21.8 0.0 copy-start.5
  21.8 0.0 copy-start.2
  21.8 2.0 %attend.6 = (bf16[13,64,128]{2,1,0:T(8,128)(2,1)S(1)}, bf16[13,64,128]{2,1,0:T(8,128)(2,1)S(1)}, bf16[13,64,128]{2,1,0:T(8,128)(2,1)S(1)}, bf16[13,64,128]{2,1,0:T(8,128)(2,1)S(1)}) custom-call(s32[2]{0:T(128)S(1)} %pad_add_fusion.where_ref, s32[4]{0:T(128)S(1)} %copy-done.11, ...), custom_call_target="tpu_custom_call", output_to_operand_aliasing={{0}: (8, {}), {1}: (9, {}), {2}: (10, {}), {3}: (11, {})} | custom-call | tf_op jit(solution)/shard_map/attend/pallas_call | solution.py:388
  23.8 0.0 copy-start.4
  23.8 0.0 copy-start.15
  23.8 0.0 copy-start
  23.8 0.0 copy-start.1
  23.8 1.9 %attend.7 = (bf16[13,64,128]{2,1,0:T(8,128)(2,1)S(1)}, bf16[13,64,128]{2,1,0:T(8,128)(2,1)S(1)}, bf16[13,64,128]{2,1,0:T(8,128)(2,1)S(1)}, bf16[13,64,128]{2,1,0:T(8,128)(2,1)S(1)}) custom-call(s32[2]{0:T(128)S(1)} %pad_add_fusion.where_ref, s32[4]{0:T(128)S(1)} %copy-done.11, ...), custom_call_target="tpu_custom_call", output_to_operand_aliasing={{0}: (8, {}), {1}: (9, {}), {2}: (10, {}), {3}: (11, {})} | custom-call | tf_op jit(solution)/shard_map/attend/pallas_call | solution.py:388
  25.8 1.6 %collective-permute-start.3 = (bf16[13,64,128]{2,1,0:T(8,128)(2,1)S(1)}, bf16[13,64,128]{2,1,0:T(8,128)(2,1)S(1)}, u32[]{:S(2)}, u32[]{:S(2)}) collective-permute-start(bf16[13,64,128]{2,1,0:T(8,128)(2,1)S(1)} %get-tuple-element.62), channel_id=1, source_target_pairs={{0,1},{1,0},{2,3},{3,2},{4,5},{5,4},{6,7},{7,6},{8,9},{9,8},{10,11... | collective-permute-start | bytes 638984 | tf_op jit(solution)/shard_map/ppermute | solution.py:52
  27.3 1.5 %collective-permute-start.4 = (bf16[13,64,128]{2,1,0:T(8,128)(2,1)S(1)}, bf16[13,64,128]{2,1,0:T(8,128)(2,1)S(1)}, u32[]{:S(2)}, u32[]{:S(2)}) collective-permute-start(bf16[13,64,128]{2,1,0:T(8,128)(2,1)S(1)} %get-tuple-element.63), channel_id=1, source_target_pairs={{0,2},{1,3},{2,0},{3,1},{4,6},{5,7},{6,4},{7,5},{8,10},{9,11},{10,... | collective-permute-start | bytes 638984 | tf_op jit(solution)/shard_map/ppermute | solution.py:52
  28.8 0.5 collective-permute-start.5
  29.3 4.7 %collective-permute-done.3.refs_1_ = bf16[13,64,128]{2,1,0:T(8,128)(2,1)S(1)} collective-permute-done((bf16[13,64,128]{2,1,0:T(8,128)(2,1)S(1)}, bf16[13,64,128]{2,1,0:T(8,128)(2,1)S(1)}, u32[]{:S(2)}, u32[]{:S(2)}) %collective-permute-start.3) | collective-permute-done | bytes 213024 | tf_op jit(solution)/shard_map/ppermute | solution.py:52
  34.0 3.8 %collective-permute-done.4.refs_2_ = bf16[13,64,128]{2,1,0:T(8,128)(2,1)S(1)} collective-permute-done((bf16[13,64,128]{2,1,0:T(8,128)(2,1)S(1)}, bf16[13,64,128]{2,1,0:T(8,128)(2,1)S(1)}, u32[]{:S(2)}, u32[]{:S(2)}) %collective-permute-start.4) | collective-permute-done | bytes 213024 | tf_op jit(solution)/shard_map/ppermute | solution.py:52
  37.8 2.3 %join.1 = (f32[64,1536]{1,0:T(8,128)S(1)}, bf16[64,1536]{1,0:T(8,128)(2,1)S(1)}, bf16[64,1536]{1,0:T(8,128)(2,1)S(1)}, bf16[64,1536]{1,0:T(8,128)(2,1)S(1)}) custom-call(bf16[384,1536]{1,0:T(8,128)(2,1)S(1)} %copy-done.4, bf16[13,64,128]{2,1,0:T(8,128)(2,1)S(1)} %get-tuple-element.61.refs_0_, bf16[13,64,128]{2,1,0:T(8,128)(2,1)S(1)} %collective-permute-done.3.refs_1_, ...), custom_call_target="tpu_custom_call" | custom-call | tf_op jit(solution)/shard_map/join/pallas_call | solution.py:443
  40.1 1.3 %collective-permute-start.6 = (bf16[64,1536]{1,0:T(8,128)(2,1)S(1)}, bf16[64,1536]{1,0:T(8,128)(2,1)S(1)}, u32[]{:S(2)}, u32[]{:S(2)}) collective-permute-start(bf16[64,1536]{1,0:T(8,128)(2,1)S(1)} %get-tuple-element.66), channel_id=1, source_target_pairs={{0,1},{1,0},{2,3},{3,2},{4,5},{5,4},{6,7},{7,6},{8,9},{9,8},{10,11... | collective-permute-start | bytes 589832 | tf_op jit(solution)/shard_map/ppermute | solution.py:52
  41.4 0.8 collective-permute-start.7
  42.2 1.4 %collective-permute-start.8 = (bf16[64,1536]{1,0:T(8,128)(2,1)S(1)}, bf16[64,1536]{1,0:T(8,128)(2,1)S(1)}, u32[]{:S(2)}, u32[]{:S(2)}) collective-permute-start(bf16[64,1536]{1,0:T(8,128)(2,1)S(1)} %get-tuple-element.68), channel_id=1, source_target_pairs={{0,3},{1,2},{2,1},{3,0},{4,7},{5,6},{6,5},{7,4},{8,11},{9,10},{10,... | collective-permute-start | bytes 589832 | tf_op jit(solution)/shard_map/ppermute | solution.py:52
  43.7 3.5 %collective-permute-done.6.refs_0_ = bf16[64,1536]{1,0:T(8,128)(2,1)S(1)} collective-permute-done((bf16[64,1536]{1,0:T(8,128)(2,1)S(1)}, bf16[64,1536]{1,0:T(8,128)(2,1)S(1)}, u32[]{:S(2)}, u32[]{:S(2)}) %collective-permute-start.6) | collective-permute-done | bytes 196640 | tf_op jit(solution)/shard_map/ppermute | solution.py:52
  47.2 3.0 %collective-permute-done.7.refs_1_ = bf16[64,1536]{1,0:T(8,128)(2,1)S(1)} collective-permute-done((bf16[64,1536]{1,0:T(8,128)(2,1)S(1)}, bf16[64,1536]{1,0:T(8,128)(2,1)S(1)}, u32[]{:S(2)}, u32[]{:S(2)}) %collective-permute-start.7) | collective-permute-done | bytes 196640 | tf_op jit(solution)/shard_map/ppermute | solution.py:52
  50.2 0.2 norm.1
  50.4 0.1 collective-permute-start.9
  50.5 1.6 %collective-permute-start.11 = (bf16[64,1536]{1,0:T(8,128)(2,1)S(1)}, bf16[64,1536]{1,0:T(8,128)(2,1)S(1)}, u32[]{:S(2)}, u32[]{:S(2)}) collective-permute-start(bf16[64,1536]{1,0:T(8,128)(2,1)S(1)} %get-tuple-element.72.a_ref), channel_id=1, source_target_pairs={{0,8},{4,12},{8,0},{12,4},{16,24},{20,28},{24,16},{28,20},{1,9},{5... | collective-permute-start | bytes 589832 | tf_op jit(solution)/shard_map/ppermute | solution.py:52
  52.2 2.4 %experts.4 = (f32[64,1536]{1,0:T(8,128)S(1)}, bf16[64,1536]{1,0:T(8,128)(2,1)S(1)}) custom-call(s32[2]{0:T(128)S(1)} %pad_add_fusion.where_ref, f32[8,64,16]{2,1,0:T(8,128)S(1)} %get-tuple-element.70.bias_ref, bf16[32,1536]{1,0:T(8,128)(2,1)S(1)} %get-tuple-element.71.route_ref, bf16[2,1536,512]{2,1,0:T(8,128)(2,1)S(1)} %copy-done, ...), custom_call_target="tpu_custom_call" | custom-call | tf_op jit(solution)/shard_map/experts/pallas_call | solution.py:597
  54.6 3.3 %collective-permute-done.11.a_ref = bf16[64,1536]{1,0:T(8,128)(2,1)S(1)} collective-permute-done((bf16[64,1536]{1,0:T(8,128)(2,1)S(1)}, bf16[64,1536]{1,0:T(8,128)(2,1)S(1)}, u32[]{:S(2)}, u32[]{:S(2)}) %collective-permute-start.11) | collective-permute-done | bytes 196640 | tf_op jit(solution)/shard_map/ppermute | solution.py:52
  57.8 0.3 collective-permute-start.15
  58.2 1.1 %collective-permute-done.12.b_ref = bf16[64,1536]{1,0:T(8,128)(2,1)S(1)} collective-permute-done((bf16[64,1536]{1,0:T(8,128)(2,1)S(1)}, bf16[64,1536]{1,0:T(8,128)(2,1)S(1)}, u32[]{:S(2)}, u32[]{:S(2)}) %collective-permute-start.12) | collective-permute-done | bytes 196640 | tf_op jit(solution)/shard_map/ppermute | solution.py:52
  59.3 2.6 %experts.5 = (f32[64,1536]{1,0:T(8,128)S(1)}, bf16[64,1536]{1,0:T(8,128)(2,1)S(1)}) custom-call(s32[2]{0:T(128)S(1)} %pad_add_fusion.where_ref, f32[8,64,16]{2,1,0:T(8,128)S(1)} %get-tuple-element.70.bias_ref, bf16[32,1536]{1,0:T(8,128)(2,1)S(1)} %get-tuple-element.71.route_ref, bf16[2,1536,512]{2,1,0:T(8,128)(2,1)S(1)} %copy-done, ...), custom_call_target="tpu_custom_call" | custom-call | tf_op jit(solution)/shard_map/experts/pallas_call | solution.py:597
  61.9 5.4 %collective-permute-done.15.a_ref = bf16[64,1536]{1,0:T(8,128)(2,1)S(1)} collective-permute-done((bf16[64,1536]{1,0:T(8,128)(2,1)S(1)}, bf16[64,1536]{1,0:T(8,128)(2,1)S(1)}, u32[]{:S(2)}, u32[]{:S(2)}) %collective-permute-start.15) | collective-permute-done | bytes 196640 | tf_op jit(solution)/shard_map/ppermute | solution.py:52
  67.2 4.6 %collective-permute-start.19 = (bf16[64,1536]{1,0:T(8,128)(2,1)S(1)}, bf16[64,1536]{1,0:T(8,128)(2,1)S(1)}, u32[]{:S(2)}, u32[]{:S(2)}) collective-permute-start(bf16[64,1536]{1,0:T(8,128)(2,1)S(1)} %collective-permute-done.15.a_ref), channel_id=1, source_target_pairs={{0,8},{4,12},{8,0},{12,4},{16,24},{20,28},{24,16},{28,20},{1,9},{5... | collective-permute-start | bytes 589832 | tf_op jit(solution)/shard_map/ppermute | solution.py:52
  71.8 0.2 collective-permute-start.13
  72.0 0.4 collective-permute-start.10
  72.3 2.4 %experts.6 = (f32[64,1536]{1,0:T(8,128)S(1)}, bf16[64,1536]{1,0:T(8,128)(2,1)S(1)}) custom-call(s32[2]{0:T(128)S(1)} %pad_add_fusion.where_ref, f32[8,64,16]{2,1,0:T(8,128)S(1)} %get-tuple-element.70.bias_ref, bf16[32,1536]{1,0:T(8,128)(2,1)S(1)} %get-tuple-element.71.route_ref, bf16[2,1536,512]{2,1,0:T(8,128)(2,1)S(1)} %copy-done, ...), custom_call_target="tpu_custom_call" | custom-call | tf_op jit(solution)/shard_map/experts/pallas_call | solution.py:597
  74.7 2.6 %collective-permute-done.19.a_ref = bf16[64,1536]{1,0:T(8,128)(2,1)S(1)} collective-permute-done((bf16[64,1536]{1,0:T(8,128)(2,1)S(1)}, bf16[64,1536]{1,0:T(8,128)(2,1)S(1)}, u32[]{:S(2)}, u32[]{:S(2)}) %collective-permute-start.19) | collective-permute-done | bytes 196640 | tf_op jit(solution)/shard_map/ppermute | solution.py:52
  77.3 0.5 collective-permute-start.17
  77.9 1.8 %collective-permute-start.14 = (bf16[64,1536]{1,0:T(8,128)(2,1)S(1)}, bf16[64,1536]{1,0:T(8,128)(2,1)S(1)}, u32[]{:S(2)}, u32[]{:S(2)}) collective-permute-start(bf16[64,1536]{1,0:T(8,128)(2,1)S(1)} %add_convert_fusion.3), channel_id=1, source_target_pairs={{0,8},{4,12},{8,0},{12,4},{16,24},{20,28},{24,16},{28,20},{1,9},{5... | collective-permute-start | bytes 589832 | tf_op jit(solution)/shard_map/ppermute | solution.py:52
  79.7 2.4 %experts.7 = (f32[64,1536]{1,0:T(8,128)S(1)}, bf16[64,1536]{1,0:T(8,128)(2,1)S(1)}) custom-call(s32[2]{0:T(128)S(1)} %pad_add_fusion.where_ref, f32[8,64,16]{2,1,0:T(8,128)S(1)} %get-tuple-element.70.bias_ref, bf16[32,1536]{1,0:T(8,128)(2,1)S(1)} %get-tuple-element.71.route_ref, bf16[2,1536,512]{2,1,0:T(8,128)(2,1)S(1)} %copy-done, ...), custom_call_target="tpu_custom_call" | custom-call | tf_op jit(solution)/shard_map/experts/pallas_call | solution.py:597
  82.1 0.1 collective-permute-start.21
  82.2 0.1 collective-permute-start.18
  82.3 1.3 %collective-permute-done.21 = bf16[64,1536]{1,0:T(8,128)(2,1)S(1)} collective-permute-done((bf16[64,1536]{1,0:T(8,128)(2,1)S(1)}, bf16[64,1536]{1,0:T(8,128)(2,1)S(1)}, u32[]{:S(2)}, u32[]{:S(2)}) %collective-permute-start.21) | collective-permute-done | bytes 196640 | tf_op jit(solution)/shard_map/ppermute | solution.py:52
  83.6 1.2 %collective-permute-start.22 = (bf16[64,1536]{1,0:T(8,128)(2,1)S(1)}, bf16[64,1536]{1,0:T(8,128)(2,1)S(1)}, u32[]{:S(2)}, u32[]{:S(2)}) collective-permute-start(bf16[64,1536]{1,0:T(8,128)(2,1)S(1)} %add_convert_fusion.1), channel_id=1, source_target_pairs={{0,24},{4,28},{8,16},{12,20},{16,8},{20,12},{24,0},{28,4},{1,25},{... | collective-permute-start | bytes 589832 | tf_op jit(solution)/shard_map/ppermute | solution.py:52
  84.8 1.2 %accepted.1 = bf16[4,8,1024]{2,1,0:T(8,128)(2,1)} custom-call(s32[2]{0:T(128)S(1)} %pad_add_fusion.where_ref, bf16[72,1536]{1,0:T(8,128)(2,1)S(1)} %get-tuple-element.43.pay_ref.refs_0_, bf16[72,1536]{1,0:T(8,128)(2,1)S(1)} %collective-permute-done.2.pay_ref.refs_1_, bf16[72,1536]{1,0:T(8,128)(2,1)S(1)} %collective-permute-done.1.pay_ref.refs_2_, ...), custom_call_target="tpu_custom_call" | custom-call | tf_op jit(solution)/shard_map/accepted/pallas_call | solution.py:623
  86.0 10.0 %collective-permute-done.18 = bf16[64,1536]{1,0:T(8,128)(2,1)S(1)} collective-permute-done((bf16[64,1536]{1,0:T(8,128)(2,1)S(1)}, bf16[64,1536]{1,0:T(8,128)(2,1)S(1)}, u32[]{:S(2)}, u32[]{:S(2)}) %collective-permute-start.18) | collective-permute-done | bytes 196640 | tf_op jit(solution)/shard_map/ppermute | solution.py:52
  96.0 6.5 %collective-permute-done.22 = bf16[64,1536]{1,0:T(8,128)(2,1)S(1)} collective-permute-done((bf16[64,1536]{1,0:T(8,128)(2,1)S(1)}, bf16[64,1536]{1,0:T(8,128)(2,1)S(1)}, u32[]{:S(2)}, u32[]{:S(2)}) %collective-permute-start.22) | collective-permute-done | bytes 196640 | tf_op jit(solution)/shard_map/ppermute | solution.py:52
  102.4 0.8 add_convert_fusion
  (33 shorter events, 0.2 us)
Async XLA Ops:
  0.6 16.4 %copy-start.11 = (s32[4]{0:T(128)S(1)}, s32[4]{0:T(128)}, u32[]{:S(2)}) copy-start(s32[4]{0:T(128)} %len_ref.9) | copy-start | bytes 52
  0.7 0.9 copy-start.6
  1.6 0.9 copy-start.7
  2.6 0.7 copy-start.10
  3.2 0.7 copy-start.12
  3.9 0.7 copy-start.13
  4.6 0.7 copy-start.14
  7.1 12.7 %collective-permute-start.2 = (bf16[72,1536]{1,0:T(8,128)(2,1)S(1)}, bf16[72,1536]{1,0:T(8,128)(2,1)S(1)}, u32[]{:S(2)}, u32[]{:S(2)}) collective-permute-start(bf16[72,1536]{1,0:T(8,128)(2,1)S(1)} %get-tuple-element.43.pay_ref.refs_0_), channel_id=1, source_target_pairs={{0,1},{1,0},{2,3},{3,2},{4,5},{5,4},{6,7},{7,6},{8,9},{9,8},{10,11... | collective-permute-start | bytes 663560 | tf_op jit(solution)/shard_map/ppermute | solution.py:52
  8.7 13.1 %collective-permute-start.1 = (bf16[72,1536]{1,0:T(8,128)(2,1)S(1)}, bf16[72,1536]{1,0:T(8,128)(2,1)S(1)}, u32[]{:S(2)}, u32[]{:S(2)}) collective-permute-start(bf16[72,1536]{1,0:T(8,128)(2,1)S(1)} %get-tuple-element.43.pay_ref.refs_0_), channel_id=1, source_target_pairs={{0,2},{1,3},{2,0},{3,1},{4,6},{5,7},{6,4},{7,5},{8,10},{9,11},{10,... | collective-permute-start | bytes 663560 | tf_op jit(solution)/shard_map/ppermute | solution.py:52
  10.2 13.6 %collective-permute-start = (bf16[72,1536]{1,0:T(8,128)(2,1)S(1)}, bf16[72,1536]{1,0:T(8,128)(2,1)S(1)}, u32[]{:S(2)}, u32[]{:S(2)}) collective-permute-start(bf16[72,1536]{1,0:T(8,128)(2,1)S(1)} %get-tuple-element.43.pay_ref.refs_0_), channel_id=1, source_target_pairs={{0,3},{1,2},{2,1},{3,0},{4,7},{5,6},{6,5},{7,4},{8,11},{9,10},{10,... | collective-permute-start | bytes 663560 | tf_op jit(solution)/shard_map/ppermute | solution.py:52
  10.7 2.2 %copy-start.3 = (bf16[4,512,2,512]{3,2,1,0:T(2,128)(2,1)S(1)}, bf16[4,512,2,512]{3,2,1,0:T(2,128)(2,1)}, u32[]{:S(2)}) copy-start(bf16[4,512,2,512]{3,2,1,0:T(2,128)(2,1)} %param.18) | copy-start | bytes 12582916
  12.9 0.9 copy-start.8
  13.8 0.8 copy-start.9
  21.8 28.5 %copy-start.5 = (bf16[64,1536]{1,0:T(8,128)(2,1)S(1)}, bf16[64,1536]{1,0:T(8,128)(2,1)}, u32[]{:S(2)}) copy-start(bf16[64,1536]{1,0:T(8,128)(2,1)} %hidden_ref.1) | copy-start | bytes 589828
  21.8 30.4 %copy-start.2 = (bf16[2,512,1536]{2,1,0:T(8,128)(2,1)S(1)}, bf16[2,512,1536]{2,1,0:T(8,128)(2,1)}, u32[]{:S(2)}) copy-start(bf16[2,512,1536]{2,1,0:T(8,128)(2,1)} %wd.7) | copy-start | bytes 9437188
  23.8 14.0 %copy-start.4 = (bf16[384,1536]{1,0:T(8,128)(2,1)S(1)}, bf16[384,1536]{1,0:T(8,128)(2,1)}, u32[]{:S(2)}) copy-start(bf16[384,1536]{1,0:T(8,128)(2,1)} %weight_ref.1) | copy-start | bytes 3538948
  23.8 19.9 %copy-start.15 = (f32[1536]{0:T(1024)S(1)}, f32[1536]{0:T(1024)}, u32[]{:S(2)}) copy-start(f32[1536]{0:T(1024)} %param.25) | copy-start | bytes 18436
  23.8 28.4 %copy-start = (bf16[2,1536,512]{2,1,0:T(8,128)(2,1)S(1)}, bf16[2,1536,512]{2,1,0:T(8,128)(2,1)}, u32[]{:S(2)}) copy-start(bf16[2,1536,512]{2,1,0:T(8,128)(2,1)} %wg.7) | copy-start | bytes 9437188
  23.8 28.4 %copy-start.1 = (bf16[2,1536,512]{2,1,0:T(8,128)(2,1)S(1)}, bf16[2,1536,512]{2,1,0:T(8,128)(2,1)}, u32[]{:S(2)}) copy-start(bf16[2,1536,512]{2,1,0:T(8,128)(2,1)} %wu.7) | copy-start | bytes 9437188
  25.8 8.3 %collective-permute-start.3 = (bf16[13,64,128]{2,1,0:T(8,128)(2,1)S(1)}, bf16[13,64,128]{2,1,0:T(8,128)(2,1)S(1)}, u32[]{:S(2)}, u32[]{:S(2)}) collective-permute-start(bf16[13,64,128]{2,1,0:T(8,128)(2,1)S(1)} %get-tuple-element.62), channel_id=1, source_target_pairs={{0,1},{1,0},{2,3},{3,2},{4,5},{5,4},{6,7},{7,6},{8,9},{9,8},{10,11... | collective-permute-start | bytes 638984 | tf_op jit(solution)/shard_map/ppermute | solution.py:52
  27.3 10.4 %collective-permute-start.4 = (bf16[13,64,128]{2,1,0:T(8,128)(2,1)S(1)}, bf16[13,64,128]{2,1,0:T(8,128)(2,1)S(1)}, u32[]{:S(2)}, u32[]{:S(2)}) collective-permute-start(bf16[13,64,128]{2,1,0:T(8,128)(2,1)S(1)} %get-tuple-element.63), channel_id=1, source_target_pairs={{0,2},{1,3},{2,0},{3,1},{4,6},{5,7},{6,4},{7,5},{8,10},{9,11},{10,... | collective-permute-start | bytes 638984 | tf_op jit(solution)/shard_map/ppermute | solution.py:52
  28.8 8.9 %collective-permute-start.5 = (bf16[13,64,128]{2,1,0:T(8,128)(2,1)S(1)}, bf16[13,64,128]{2,1,0:T(8,128)(2,1)S(1)}, u32[]{:S(2)}, u32[]{:S(2)}) collective-permute-start(bf16[13,64,128]{2,1,0:T(8,128)(2,1)S(1)} %get-tuple-element.64), channel_id=1, source_target_pairs={{0,3},{1,2},{2,1},{3,0},{4,7},{5,6},{6,5},{7,4},{8,11},{9,10},{10,... | collective-permute-start | bytes 638984 | tf_op jit(solution)/shard_map/ppermute | solution.py:52
  40.1 7.1 %collective-permute-start.6 = (bf16[64,1536]{1,0:T(8,128)(2,1)S(1)}, bf16[64,1536]{1,0:T(8,128)(2,1)S(1)}, u32[]{:S(2)}, u32[]{:S(2)}) collective-permute-start(bf16[64,1536]{1,0:T(8,128)(2,1)S(1)} %get-tuple-element.66), channel_id=1, source_target_pairs={{0,1},{1,0},{2,3},{3,2},{4,5},{5,4},{6,7},{7,6},{8,9},{9,8},{10,11... | collective-permute-start | bytes 589832 | tf_op jit(solution)/shard_map/ppermute | solution.py:52
  41.4 8.8 %collective-permute-start.7 = (bf16[64,1536]{1,0:T(8,128)(2,1)S(1)}, bf16[64,1536]{1,0:T(8,128)(2,1)S(1)}, u32[]{:S(2)}, u32[]{:S(2)}) collective-permute-start(bf16[64,1536]{1,0:T(8,128)(2,1)S(1)} %get-tuple-element.67), channel_id=1, source_target_pairs={{0,2},{1,3},{2,0},{3,1},{4,6},{5,7},{6,4},{7,5},{8,10},{9,11},{10,... | collective-permute-start | bytes 589832 | tf_op jit(solution)/shard_map/ppermute | solution.py:52
  42.2 8.0 %collective-permute-start.8 = (bf16[64,1536]{1,0:T(8,128)(2,1)S(1)}, bf16[64,1536]{1,0:T(8,128)(2,1)S(1)}, u32[]{:S(2)}, u32[]{:S(2)}) collective-permute-start(bf16[64,1536]{1,0:T(8,128)(2,1)S(1)} %get-tuple-element.68), channel_id=1, source_target_pairs={{0,3},{1,2},{2,1},{3,0},{4,7},{5,6},{6,5},{7,4},{8,11},{9,10},{10,... | collective-permute-start | bytes 589832 | tf_op jit(solution)/shard_map/ppermute | solution.py:52
  50.4 1.7 %collective-permute-start.9 = (bf16[64,1536]{1,0:T(8,128)(2,1)S(1)}, bf16[64,1536]{1,0:T(8,128)(2,1)S(1)}, u32[]{:S(2)}, u32[]{:S(2)}) collective-permute-start(bf16[64,1536]{1,0:T(8,128)(2,1)S(1)} %get-tuple-element.72.a_ref), channel_id=1, source_target_pairs={{0,4},{4,0},{8,12},{12,8},{16,20},{20,16},{24,28},{28,24},{1,5},{5... | collective-permute-start | bytes 589832 | tf_op jit(solution)/shard_map/ppermute | solution.py:52
  50.5 7.3 %collective-permute-start.11 = (bf16[64,1536]{1,0:T(8,128)(2,1)S(1)}, bf16[64,1536]{1,0:T(8,128)(2,1)S(1)}, u32[]{:S(2)}, u32[]{:S(2)}) collective-permute-start(bf16[64,1536]{1,0:T(8,128)(2,1)S(1)} %get-tuple-element.72.a_ref), channel_id=1, source_target_pairs={{0,8},{4,12},{8,0},{12,4},{16,24},{20,28},{24,16},{28,20},{1,9},{5... | collective-permute-start | bytes 589832 | tf_op jit(solution)/shard_map/ppermute | solution.py:52
  57.8 1.4 %collective-permute-start.12 = (bf16[64,1536]{1,0:T(8,128)(2,1)S(1)}, bf16[64,1536]{1,0:T(8,128)(2,1)S(1)}, u32[]{:S(2)}, u32[]{:S(2)}) collective-permute-start(bf16[64,1536]{1,0:T(8,128)(2,1)S(1)} %collective-permute-done.11.a_ref), channel_id=1, source_target_pairs={{0,4},{4,0},{8,12},{12,8},{16,20},{20,16},{24,28},{28,24},{1,5},{5... | collective-permute-start | bytes 589832 | tf_op jit(solution)/shard_map/ppermute | solution.py:52
  57.8 9.4 %collective-permute-start.15 = (bf16[64,1536]{1,0:T(8,128)(2,1)S(1)}, bf16[64,1536]{1,0:T(8,128)(2,1)S(1)}, u32[]{:S(2)}, u32[]{:S(2)}) collective-permute-start(bf16[64,1536]{1,0:T(8,128)(2,1)S(1)} %get-tuple-element.72.a_ref), channel_id=1, source_target_pairs={{0,16},{4,20},{8,24},{12,28},{16,0},{20,4},{24,8},{28,12},{1,17},{... | collective-permute-start | bytes 589832 | tf_op jit(solution)/shard_map/ppermute | solution.py:52
  67.2 5.1 %collective-permute-start.16 = (bf16[64,1536]{1,0:T(8,128)(2,1)S(1)}, bf16[64,1536]{1,0:T(8,128)(2,1)S(1)}, u32[]{:S(2)}, u32[]{:S(2)}) collective-permute-start(bf16[64,1536]{1,0:T(8,128)(2,1)S(1)} %collective-permute-done.15.a_ref), channel_id=1, source_target_pairs={{0,4},{4,0},{8,12},{12,8},{16,20},{20,16},{24,28},{28,24},{1,5},{5... | collective-permute-start | bytes 589832 | tf_op jit(solution)/shard_map/ppermute | solution.py:52
  67.2 10.1 %collective-permute-start.19 = (bf16[64,1536]{1,0:T(8,128)(2,1)S(1)}, bf16[64,1536]{1,0:T(8,128)(2,1)S(1)}, u32[]{:S(2)}, u32[]{:S(2)}) collective-permute-start(bf16[64,1536]{1,0:T(8,128)(2,1)S(1)} %collective-permute-done.15.a_ref), channel_id=1, source_target_pairs={{0,8},{4,12},{8,0},{12,4},{16,24},{20,28},{24,16},{28,20},{1,9},{5... | collective-permute-start | bytes 589832 | tf_op jit(solution)/shard_map/ppermute | solution.py:52
  71.8 6.0 %collective-permute-start.13 = (bf16[64,1536]{1,0:T(8,128)(2,1)S(1)}, bf16[64,1536]{1,0:T(8,128)(2,1)S(1)}, u32[]{:S(2)}, u32[]{:S(2)}) collective-permute-start(bf16[64,1536]{1,0:T(8,128)(2,1)S(1)} %get-tuple-element.77), channel_id=1, source_target_pairs={{0,4},{4,0},{8,12},{12,8},{16,20},{20,16},{24,28},{28,24},{1,5},{5... | collective-permute-start | bytes 589832 | tf_op jit(solution)/shard_map/ppermute | solution.py:52
  72.0 14.0 %collective-permute-start.10 = (bf16[64,1536]{1,0:T(8,128)(2,1)S(1)}, bf16[64,1536]{1,0:T(8,128)(2,1)S(1)}, u32[]{:S(2)}, u32[]{:S(2)}) collective-permute-start(bf16[64,1536]{1,0:T(8,128)(2,1)S(1)} %get-tuple-element.74), channel_id=1, source_target_pairs={{0,4},{4,0},{8,12},{12,8},{16,20},{20,16},{24,28},{28,24},{1,5},{5... | collective-permute-start | bytes 589832 | tf_op jit(solution)/shard_map/ppermute | solution.py:52
  77.3 2.4 %collective-permute-start.20 = (bf16[64,1536]{1,0:T(8,128)(2,1)S(1)}, bf16[64,1536]{1,0:T(8,128)(2,1)S(1)}, u32[]{:S(2)}, u32[]{:S(2)}) collective-permute-start(bf16[64,1536]{1,0:T(8,128)(2,1)S(1)} %collective-permute-done.19.a_ref), channel_id=1, source_target_pairs={{0,4},{4,0},{8,12},{12,8},{16,20},{20,16},{24,28},{28,24},{1,5},{5... | collective-permute-start | bytes 589832 | tf_op jit(solution)/shard_map/ppermute | solution.py:52
  77.3 4.8 %collective-permute-start.17 = (bf16[64,1536]{1,0:T(8,128)(2,1)S(1)}, bf16[64,1536]{1,0:T(8,128)(2,1)S(1)}, u32[]{:S(2)}, u32[]{:S(2)}) collective-permute-start(bf16[64,1536]{1,0:T(8,128)(2,1)S(1)} %get-tuple-element.80), channel_id=1, source_target_pairs={{0,4},{4,0},{8,12},{12,8},{16,20},{20,16},{24,28},{28,24},{1,5},{5... | collective-permute-start | bytes 589832 | tf_op jit(solution)/shard_map/ppermute | solution.py:52
  77.9 8.1 %collective-permute-start.14 = (bf16[64,1536]{1,0:T(8,128)(2,1)S(1)}, bf16[64,1536]{1,0:T(8,128)(2,1)S(1)}, u32[]{:S(2)}, u32[]{:S(2)}) collective-permute-start(bf16[64,1536]{1,0:T(8,128)(2,1)S(1)} %add_convert_fusion.3), channel_id=1, source_target_pairs={{0,8},{4,12},{8,0},{12,4},{16,24},{20,28},{24,16},{28,20},{1,9},{5... | collective-permute-start | bytes 589832 | tf_op jit(solution)/shard_map/ppermute | solution.py:52
  82.1 1.5 %collective-permute-start.21 = (bf16[64,1536]{1,0:T(8,128)(2,1)S(1)}, bf16[64,1536]{1,0:T(8,128)(2,1)S(1)}, u32[]{:S(2)}, u32[]{:S(2)}) collective-permute-start(bf16[64,1536]{1,0:T(8,128)(2,1)S(1)} %get-tuple-element.83), channel_id=1, source_target_pairs={{0,4},{4,0},{8,12},{12,8},{16,20},{20,16},{24,28},{28,24},{1,5},{5... | collective-permute-start | bytes 589832 | tf_op jit(solution)/shard_map/ppermute | solution.py:52
  82.2 13.8 %collective-permute-start.18 = (bf16[64,1536]{1,0:T(8,128)(2,1)S(1)}, bf16[64,1536]{1,0:T(8,128)(2,1)S(1)}, u32[]{:S(2)}, u32[]{:S(2)}) collective-permute-start(bf16[64,1536]{1,0:T(8,128)(2,1)S(1)} %add_convert_fusion.2), channel_id=1, source_target_pairs={{0,16},{4,20},{8,24},{12,28},{16,0},{20,4},{24,8},{28,12},{1,17},{... | collective-permute-start | bytes 589832 | tf_op jit(solution)/shard_map/ppermute | solution.py:52
  83.6 18.8 %collective-permute-start.22 = (bf16[64,1536]{1,0:T(8,128)(2,1)S(1)}, bf16[64,1536]{1,0:T(8,128)(2,1)S(1)}, u32[]{:S(2)}, u32[]{:S(2)}) collective-permute-start(bf16[64,1536]{1,0:T(8,128)(2,1)S(1)} %add_convert_fusion.1), channel_id=1, source_target_pairs={{0,24},{4,28},{8,16},{12,20},{16,8},{20,12},{24,0},{28,4},{1,25},{... | collective-permute-start | bytes 589832 | tf_op jit(solution)/shard_map/ppermute | solution.py:52

commit v3 on v2

--- a/solution.py
+++ b/solution.py
@@ -26,10 +26,10 @@
 LOG2E = 1.4426950408889634
 MIB = 1024 * 1024
 
-_half = HD // 2
-INVERSE = np.tile(
-    (10000.0 ** (-2.0 * np.arange(_half, dtype=np.float64) / HD)).astype(np.float32), LANES // _half
-).reshape(1, LANES)
+INVERSE = [
+    float(x)
+    for x in (10000.0 ** (-2.0 * np.arange(HD // 2, dtype=np.float64) / HD)).astype(np.float32)
+]
 
 
 def params(mib):
@@ -40,12 +40,16 @@
     return pl.BlockSpec(memory_space=pltpu.VMEM)
 
 
-def blocked(x):
-    return pl.BlockSpec(x.shape, lambda i: (0,) * x.ndim)
-
-
-def scalars():
-    return pl.BlockSpec(memory_space=pltpu.SMEM)
+def in_hbm():
+    return pl.BlockSpec(memory_space=pltpu.HBM)
+
+
+def fixed(x):
+    return pltpu.with_memory_space_constraint(x, pltpu.HBM)
+
+
+def cost(flops):
+    return pl.CostEstimate(flops=int(flops), bytes_accessed=0, transcendentals=0)
 
 
 def exchange(x, axis, size, step):
@@ -57,12 +61,26 @@
 
 
 def prelude_kernel(
-    where_ref, len_ref, path_ref, par_ref, inv_ref, q_ref, kv_ref,
-    pay_ref, key_ref, val_ref, anc_ref, pos_ref, kv_f, pos_own, anc_all,
+    len_hbm, path_hbm, par_hbm, q_hbm, kv_hbm,
+    pay_ref, key_ref, val_ref, anc_ref, pos_ref, lim_ref,
+    len_ref, path_ref, par_ref, q_ref, kv_ref, kv_f, anc_all, sems,
 ):
+    copies = [
+        pltpu.make_async_copy(src, dst, sems.at[j])
+        for j, (src, dst) in enumerate(
+            (
+                (par_hbm, par_ref), (len_hbm, len_ref), (path_hbm, path_ref),
+                (kv_hbm, kv_ref), (q_hbm, q_ref),
+            )
+        )
+    ]
+    for copy in copies:
+        copy.start()
+    for copy in copies[:3]:
+        copy.wait()
     requests, draft = par_ref.shape
     n = q_ref.shape[0]
-    own_start = where_ref[0] * n
+    own_start = lax.axis_index("tensor") * n
     request = own_start // draft
     offset = own_start % draft
     row = lax.broadcasted_iota(jnp.int32, (draft, draft), 0)
@@ -80,11 +98,16 @@
         depth = jnp.sum(ancestry, axis=-1, keepdims=True) - 1.0
         place = depth + len_ref[r].astype(F32)
         pos_ref[r * draft : (r + 1) * draft, :] = jnp.broadcast_to(place, (draft, LANES))
+        lim_ref[r] = jnp.full((8, LANES), len_ref[r].astype(F32))
         anc_all[r] = ancestry
     anc_ref[...] = anc_all[request]
     own = pl.multiple_of(own_start, 8)
-    angle = pos_ref[pl.ds(own, n), :] * inv_ref[...]
     lane = lane_index((n, LANES))
+    step = lane_index((8, LANES)) % (HD // 2)
+    inverse = jnp.full(step.shape, INVERSE[0], F32)
+    for k in range(1, HD // 2):
+        inverse = jnp.where(step == k, INVERSE[k], inverse)
+    angle = pos_ref[pl.ds(own, n), :] * inverse[:1, :]
     front = lane % HD < HD // 2
     cosine = jnp.cos(angle)
     sine = jnp.sin(angle)
@@ -97,8 +120,8 @@
         )
         return x * cosine + partner * sine
 
+    copies[3].wait()
     kv_f[...] = kv_ref[...].astype(F32)
-    picks = []
     slot = lax.broadcasted_iota(jnp.int32, (path_ref.shape[1], n), 0)
     token = lax.broadcasted_iota(jnp.int32, (path_ref.shape[1], n), 1) + offset
     wanted = jnp.full(slot.shape, -1, jnp.int32)
@@ -111,6 +134,7 @@
         vals.append(kv_f[pl.ds(2 * b + 1, n, stride=2 * PAIRS), :].astype(BF))
         key_ref[:, b * LANES : (b + 1) * LANES] = keys[b]
         val_ref[:, b * LANES : (b + 1) * LANES] = vals[b]
+    copies[4].wait()
     packed = jnp.concatenate(keys + vals, axis=1)
     picked = jnp.dot(chooser, packed, preferred_element_type=F32).astype(BF)
     pay_ref[n:, : packed.shape[1]] = picked
@@ -129,7 +153,7 @@
             pay_ref[:n, (GROUPS * b + i) * LANES : (GROUPS * b + i + 1) * LANES] = y.astype(BF)
 
 
-def prelude(where, cache_len, path, parents, queries, kv):
+def prelude(cache_len, path, parents, queries, kv):
     requests, draft = parents.shape
     n, width = queries.shape
     kv_width = KVH * HD
@@ -141,41 +165,57 @@
             jax.ShapeDtypeStruct((n, kv_width), BF),
             jax.ShapeDtypeStruct((draft, draft), F32),
             jax.ShapeDtypeStruct((requests * draft, LANES), F32),
+            jax.ShapeDtypeStruct((requests, 8, LANES), F32),
         ),
-        grid=(1,),
-        in_specs=[scalars(), scalars(), scalars()]
-        + [blocked(x) for x in (parents, INVERSE, queries, kv)],
-        out_specs=(whole(),) * 5,
+        in_specs=[in_hbm()] * 5,
+        out_specs=(whole(),) * 6,
         scratch_shapes=[
+            pltpu.SMEM(cache_len.shape, jnp.int32),
+            pltpu.SMEM(path.shape, jnp.int32),
+            pltpu.VMEM(parents.shape, jnp.int32),
+            pltpu.VMEM(queries.shape, BF),
+            pltpu.VMEM(kv.shape, BF),
             pltpu.VMEM(kv.shape, F32),
-            pltpu.VMEM((n, LANES), F32),
             pltpu.VMEM((requests, draft, draft), F32),
+            pltpu.SemaphoreType.DMA((5,)),
         ],
         compiler_params=params(8),
+        cost_estimate=cost(1e7),
         name="prelude",
-    )(where, cache_len, path, parents, jnp.asarray(INVERSE), queries, kv)
-
-
-def prepare_kernel(cache_ref, routes_ref, router_ref, out_ref, bias_ref, route_w_ref, kv_f):
-    cells = out_ref.shape[2]
-    kv_f[...] = cache_ref[0].astype(F32)
-    for j in range(2 * PAIRS):
-        out_ref[0, j] = kv_f[pl.ds(j, cells, stride=2 * PAIRS), :].astype(BF)
-
-    @pl.when(pl.program_id(0) == 0)
-    def _():
-        experts = router_ref.shape[0]
-        router = router_ref[...]
-        high = router.astype(BF)
-        route_w_ref[:experts, :] = high
-        route_w_ref[experts:, :] = (router - high.astype(F32)).astype(BF)
-        for d in range(routes_ref.shape[0]):
-            chosen = routes_ref[d]
-            expert = lax.broadcasted_iota(jnp.int32, (experts, chosen.shape[1]), 0)
-            hit = expert == chosen[0:1, :]
-            for k in range(1, chosen.shape[0]):
-                hit = hit | (expert == chosen[k : k + 1, :])
-            bias_ref[d] = jnp.where(hit, 0.0, NEG).T
+    )(*[fixed(x) for x in (cache_len, path, parents, queries, kv)])
+
+
+def prepare_kernel(
+    cache_hbm, routes_hbm, router_hbm, out_ref, bias_ref, route_w_ref,
+    packed, kv_f, routes_ref, router_ref, sems,
+):
+    requests, _, cells, _ = out_ref.shape
+    copies = [
+        pltpu.make_async_copy(cache_hbm.at[r], packed.at[r], sems.at[r]) for r in range(requests)
+    ]
+    copies.append(pltpu.make_async_copy(routes_hbm, routes_ref, sems.at[requests]))
+    copies.append(pltpu.make_async_copy(router_hbm, router_ref, sems.at[requests + 1]))
+    for copy in copies:
+        copy.start()
+    for r in range(requests):
+        copies[r].wait()
+        kv_f[...] = packed[r].astype(F32)
+        for j in range(2 * PAIRS):
+            out_ref[r, j] = kv_f[pl.ds(j, cells, stride=2 * PAIRS), :].astype(BF)
+    copies[requests].wait()
+    copies[requests + 1].wait()
+    experts = router_ref.shape[0]
+    router = router_ref[...]
+    high = router.astype(BF)
+    route_w_ref[:experts, :] = high
+    route_w_ref[experts:, :] = (router - high.astype(F32)).astype(BF)
+    for d in range(routes_ref.shape[0]):
+        chosen = routes_ref[d]
+        expert = lax.broadcasted_iota(jnp.int32, (experts, chosen.shape[1]), 0)
+        hit = expert == chosen[0:1, :]
+        for k in range(1, chosen.shape[0]):
+            hit = hit | (expert == chosen[k : k + 1, :])
+        bias_ref[d] = jnp.where(hit, 0.0, NEG).T
 
 
 def prepare(cache, routes, router):
@@ -190,36 +230,34 @@
             jax.ShapeDtypeStruct((blocks, n, experts), F32),
             jax.ShapeDtypeStruct((2 * experts, width), BF),
         ),
-        grid=(requests,),
-        in_specs=[
-            pl.BlockSpec((1, span, LANES), lambda r: (r, 0, 0)),
-            pl.BlockSpec((blocks, top, n), lambda r: (0, 0, 0)),
-            pl.BlockSpec((experts, width), lambda r: (0, 0)),
+        in_specs=[in_hbm()] * 3,
+        out_specs=(whole(),) * 3,
+        scratch_shapes=[
+            pltpu.VMEM(cache.shape, BF),
+            pltpu.VMEM((span, LANES), F32),
+            pltpu.VMEM(routes.shape, jnp.int32),
+            pltpu.VMEM(router.shape, F32),
+            pltpu.SemaphoreType.DMA((requests + 2,)),
         ],
-        out_specs=(
-            pl.BlockSpec((1, 2 * PAIRS, cells, LANES), lambda r: (r, 0, 0, 0)),
-            pl.BlockSpec((blocks, n, experts), lambda r: (0, 0, 0)),
-            pl.BlockSpec((2 * experts, width), lambda r: (0, 0)),
-        ),
-        scratch_shapes=[pltpu.VMEM((span, LANES), F32)],
-        compiler_params=params(12),
+        compiler_params=params(16),
+        cost_estimate=cost(1e8),
         name="prepare",
-    )(cache, routes, router)
+    )(*[fixed(x) for x in (cache, routes, router)])
 
 
 def attend_kernel(
-    step, near, where_ref, len_ref, pay_ref, kv_ref, key_ref, val_ref, anc_ref, pos_ref, out_ref
+    step, near, pay_ref, kv_ref, key_ref, val_ref, anc_ref, pos_ref, lim_ref, out_ref
 ):
     draft = anc_ref.shape[0]
     n = key_ref.shape[0]
     cells = kv_ref.shape[2]
-    me = where_ref[0]
+    me = lax.axis_index("tensor")
     start = (me ^ step) * n
     request = start // draft
     key_start = me * cells
     place = pos_ref[pl.ds(pl.multiple_of(start, 8), n), :][:, :1]
     key_pos = (lane_index((n, cells)) + key_start).astype(F32)
-    far_ok = (key_pos < len_ref[request].astype(F32)) & (
+    far_ok = (key_pos < lim_ref[request][:1, :1]) & (
         (key_pos < SINKS) | (place - key_pos < WINDOW)
     )
     bias = jnp.where(far_ok, 0.0, NEG)
@@ -295,33 +333,33 @@
     out_ref[:, QH * HD :] = stats.astype(BF)
 
 
-def attend(step, near, where, cache_len, payload, cache, keys, vals, ancestry, pos):
+def attend(step, near, payload, cache, keys, vals, ancestry, pos, limit):
     n = keys.shape[0]
     return pl.pallas_call(
         functools.partial(attend_kernel, step, near),
         out_shape=jax.ShapeDtypeStruct((n, QH * HD + LANES), BF),
-        in_specs=[scalars(), scalars()] + [whole()] * 6,
+        in_specs=[whole()] * 7,
         out_specs=whole(),
         compiler_params=params(12),
         name="attend",
-    )(where, cache_len, payload, cache, keys, vals, ancestry, pos)
+    )(payload, cache, keys, vals, ancestry, pos, limit)
 
 
 SPAN = 2 * GROUPS
 
 
 def attend_split_kernel(
-    step, near, count, where_ref, len_ref, pay_ref, kv_ref, key_ref, val_ref, anc_ref, pos_ref, *refs
+    step, near, count, pay_ref, kv_ref, key_ref, val_ref, anc_ref, pos_ref, lim_ref, *refs
 ):
     out_refs = refs[-count:]
     n = key_ref.shape[0]
     cells = kv_ref.shape[2]
-    me = where_ref[0]
+    me = lax.axis_index("tensor")
     start = (me ^ step) * n
     request = me ^ step
     place = pos_ref[pl.ds(pl.multiple_of(start, 8), n), :][:, :1]
     key_pos = (lane_index((n, cells)) + me * cells).astype(F32)
-    far_ok = (key_pos < len_ref[request].astype(F32)) & (
+    far_ok = (key_pos < lim_ref[request][:1, :1]) & (
         (key_pos < SINKS) | (place - key_pos < WINDOW)
     )
     bias = jnp.where(far_ok, 0.0, NEG)
@@ -382,18 +420,19 @@
         out_refs[j][count * GROUPS] = stats.astype(BF)
 
 
-def attend_split(step, count, where, cache_len, payload, cache, keys, vals, ancestry, pos, outs):
+def attend_split(step, count, payload, cache, keys, vals, ancestry, pos, limit, outs):
     n = keys.shape[0]
     shape = jax.ShapeDtypeStruct((count * GROUPS + 1, n, LANES), BF)
     return pl.pallas_call(
         functools.partial(attend_split_kernel, step, step == 0, count),
         out_shape=(shape,) * count,
-        in_specs=[scalars(), scalars()] + [whole()] * (6 + len(outs)),
+        in_specs=[whole()] * (7 + len(outs)),
         out_specs=(whole(),) * count,
-        input_output_aliases={8 + j: j for j in range(len(outs))},
+        input_output_aliases={7 + j: j for j in range(len(outs))},
         compiler_params=params(12),
+        cost_estimate=cost(4e8),
         name="attend",
-    )(where, cache_len, payload, cache, keys, vals, ancestry, pos, *outs)
+    )(payload, cache, keys, vals, ancestry, pos, limit, *outs)
 
 
 def join_split_kernel(count, weight_ref, *refs):
@@ -449,6 +488,7 @@
         out_specs=(whole(),) * count,
         scratch_shapes=[pltpu.VMEM((count * n, weight.shape[0]), BF)],
         compiler_params=params(12),
+        cost_estimate=cost(4e8),
         name="join",
     )(weight, *parts)
 
@@ -473,11 +513,12 @@
         in_specs=[whole()] * (3 + len(others)),
         out_specs=(whole(), whole()),
         compiler_params=params(4),
+        cost_estimate=cost(1e6),
         name="norm",
     )(hidden_in, gain, own, *others)
 
 
-def join_kernel(count, where_ref, *refs):
+def join_kernel(count, *refs):
     parts, rest = refs[:count], refs[count:]
     shares = 2 * count - 1
     pieces, rest = rest[:shares], rest[shares:]
@@ -486,8 +527,8 @@
     depth = pieces[0].shape[0]
     half = depth // CORES
     width = QH * HD
-    me = where_ref[0]
-    core = where_ref[1] % CORES
+    me = lax.axis_index("tensor")
+    core = lax.axis_index("dp") % CORES
     starts = [me * depth]
     for k in range(1, count):
         starts += [(me ^ k) * depth + core * half, (me ^ k) * depth + (1 - core) * half]
@@ -538,7 +579,7 @@
     normed_ref[...] = (mixed * lax.rsqrt(square + 1e-06) * gain_ref[...]).astype(BF)
 
 
-def join(where, parts, pieces, hidden_in, gain):
+def join(parts, pieces, hidden_in, gain):
     n, width = hidden_in.shape
     count = len(parts)
     inner = QH * HD
@@ -548,8 +589,7 @@
             jax.ShapeDtypeStruct((n, width), F32),
             jax.ShapeDtypeStruct((n, width), BF),
         ),
-        in_specs=[scalars()]
-        + [whole()] * count
+        in_specs=[whole()] * count
         + [pl.BlockSpec(memory_space=pl.ANY)] * len(pieces)
         + [whole(), whole()],
         out_specs=(whole(), whole()),
@@ -560,16 +600,16 @@
         ],
         compiler_params=params(14),
         name="join",
-    )(where, *parts, *pieces, hidden_in, gain)
+    )(*parts, *pieces, hidden_in, gain)
 
 
 def experts_kernel(
-    step, where_ref, bias_ref, route_ref, wg, wu, wd, a_ref, b_ref, own_ref, other_ref
+    step, bias_ref, route_ref, wg, wu, wd, a_ref, b_ref, own_ref, other_ref
 ):
     n, width = a_ref.shape
     local = wg.shape[0]
     experts = bias_ref.shape[2]
-    me = where_ref[1]
+    me = lax.axis_index("dp")
     x = jnp.concatenate([a_ref[...], b_ref[...]], axis=0)
     logits = lax.dot_general(
         x, route_ref[...], (((1,), (1,)), ((), ())), preferred_element_type=F32
@@ -592,7 +632,7 @@
     other_ref[...] = acc[n:].astype(BF)
 
 
-def experts_part(step, where, bias, route, w_gate, w_up, w_down, a, b):
+def experts_part(step, bias, route, w_gate, w_up, w_down, a, b):
     n, width = a.shape
     return pl.pallas_call(
         functools.partial(experts_kernel, step),
@@ -600,35 +640,37 @@
             jax.ShapeDtypeStruct((n, width), F32),
             jax.ShapeDtypeStruct((n, width), BF),
         ),
-        in_specs=[scalars()] + [whole()] * 7,
+        in_specs=[whole()] * 7,
         out_specs=(whole(), whole()),
         compiler_params=params(12),
+        cost_estimate=cost(12e8),
         name="experts",
-    )(where, bias, route, w_gate, w_up, w_down, a, b)
-
-
-def accepted_kernel(count, n, where_ref, *refs):
+    )(bias, route, w_gate, w_up, w_down, a, b)
+
+
+def accepted_kernel(count, n, *refs):
     out_ref = refs[count]
     requests = out_ref.shape[0]
     draft = count * n // requests
     out_ref[...] = jnp.zeros(out_ref.shape, out_ref.dtype)
     for k in range(count):
-        request = (where_ref[0] ^ k) * n // draft
+        request = (lax.axis_index("tensor") ^ k) * n // draft
         out_ref[request] = out_ref[request] + refs[k][:, : out_ref.shape[2]]
 
 
-def accepted(where, payloads, requests, entries, n):
+def accepted(payloads, requests, entries, n):
     count = len(payloads)
     block = pl.BlockSpec((entries, payloads[0].shape[1]), lambda i: (n // entries, 0))
     return pl.pallas_call(
         functools.partial(accepted_kernel, count, n),
         out_shape=jax.ShapeDtypeStruct((requests, entries, 2 * KVH * HD), BF),
         grid=(1,),
-        in_specs=[scalars()] + [block] * count,
+        in_specs=[block] * count,
         out_specs=pl.BlockSpec((requests, entries, 2 * KVH * HD), lambda i: (0, 0, 0)),
         compiler_params=params(4),
+        cost_estimate=cost(1e6),
         name="accepted",
-    )(where, *payloads)
+    )(*payloads)
 
 
 def rows_by_lane_block(kv):
@@ -645,9 +687,8 @@
     data = lax.axis_size("dp")
     n = queries.shape[0]
     requests, draft = parents.shape
-    where = jnp.stack([lax.axis_index("tensor"), lax.axis_index("dp")]).astype(jnp.int32)
-    payload, keys, vals, ancestry, pos = prelude(
-        where, cache_len, path, parents, queries, rows_by_lane_block(draft_kv)
+    payload, keys, vals, ancestry, pos, limit = prelude(
+        cache_len, path, parents, queries, rows_by_lane_block(draft_kv)
     )
     cache = rows_by_lane_block(cache_kv)
     payloads = [payload] + [exchange(payload, "tensor", tensor, k) for k in range(1, tensor)]
@@ -657,7 +698,7 @@
         parts = ()
         for k in range(tensor):
             parts = attend_split(
-                k, tensor, where, cache_len, payloads[k], unpacked, keys, vals, ancestry, pos, parts
+                k, tensor, payloads[k], unpacked, keys, vals, ancestry, pos, limit, parts
             )
         parts = [parts[0]] + [exchange(parts[j], "tensor", tensor, j) for j in range(1, tensor)]
         products = join_split(w_out, parts)
@@ -671,13 +712,13 @@
         parts = []
         for k in range(tensor):
             near = k < max(1, draft // n)
-            part = attend(k, near, where, cache_len, payloads[k], unpacked, keys, vals, ancestry, pos)
+            part = attend(k, near, payloads[k], unpacked, keys, vals, ancestry, pos, limit)
             parts.append(part if k == 0 else exchange(part, "tensor", tensor, k))
         pieces = [w_out]
         for piece in fetched:
             pieces += [piece, exchange(piece, "dp", data, 1)]
-        mixed, normed = join(where, parts, pieces, hidden_in, gain)
-    compacted = accepted(where, payloads, requests, path.shape[1], n)
+        mixed, normed = join(parts, pieces, hidden_in, gain)
+    compacted = accepted(payloads, requests, path.shape[1], n)
 
     steps = data // CORES
     lines = {0: normed}
@@ -686,14 +727,17 @@
         for k in [k for k in lines if k % (2 * reach) == 0]:
             lines[k + reach] = exchange(lines[k], "dp", data, CORES * reach)
         reach //= 2
+    single = [k for k in lines if k and k & (k - 1) == 0]
     total = mixed
     last = None
-    for k in sorted(lines, key=lambda k: (bin(k).count("1"), k)):
+    for k in sorted(lines, key=lambda k: (bin(k).count("1"), -k)):
+        if k == max(single) or (k and k not in single):
+            names = single if k in single else [k]
+            tied = lax.optimization_barrier([lines[name] for name in names] + [last])
+            lines.update(zip(names, tied))
         line = lines[k]
-        if last is not None:
-            line = lax.optimization_barrier((line, last))[0]
         twin = exchange(line, "dp", data, 1)
-        own, other = experts_part(k, where, bias, route, w_gate, w_up, w_down, line, twin)
+        own, other = experts_part(k, bias, route, w_gate, w_up, w_down, line, twin)
         last = own
         chip = own + exchange(other, "dp", data, 1).astype(F32)
         if k:

time: 104 us -> 84.6 us (0.81)
  the two profiles are of different devices: /device:TPU:16 before, /device:TPU:0 now
where the time goes in v3:
time: 84.6 us; the launch traced here: 84.4 us
  waiting for transfers between devices  36.5 us (43%)
  Pallas kernels  23.3 us (28%)
  starting transfers between devices  22.8 us (27%)
  other arithmetic  0.91 us (1%)
    ppermute x23, waiting for transfers between devices, exchange(): return lax.ppermute(x, axis, [(i, i ^ step) for i in range(size)])  36.5 us
    ppermute x23, starting transfers between devices, exchange(): return lax.ppermute(x, axis, [(i, i ^ step) for i in range(size)])  22.8 us
    pallas_call x4, Pallas kernels, experts_part(): pl.pallas_call(functools.partial(experts_kernel, step), out_shape=(jax.Sh...  7.29 us
    pallas_call x4, Pallas kernels, attend_split(): pl.pallas_call(functools.partial(attend_split_kernel, step, step == 0, co...  6.45 us
    pallas_call x1, Pallas kernels, prepare(): pl.pallas_call(prepare_kernel, out_shape=(jax.ShapeDtypeStruct((requests,...  3.82 us
    pallas_call x1, Pallas kernels, prelude(): pl.pallas_call(prelude_kernel, out_shape=(jax.ShapeDtypeStruct((n + path....  2.51 us
    pallas_call x1, Pallas kernels, join_split(): pl.pallas_call(functools.partial(join_split_kernel, count), out_shape=tup...  2.34 us
  transfers between devices with their start and end apart: 23, of which 12 were waited for; matrix products, arithmetic and copies ran while one was open for 0% of the time, Pallas kernels for 20%

profile of v3, /device:TPU:0, one launch (start us, length us, event | category | flops | bytes accessed | tf_op | source)
XLA Modules:
  0.0 84.4 jit_solution(2013111047492049785)
XLA Ops:
  0.6 2.5 %prelude.1 = (bf16[72,1536]{1,0:T(8,128)(2,1)S(1)}, bf16[64,512]{1,0:T(8,128)(2,1)S(1)}, bf16[64,512]{1,0:T(8,128)(2,1)S(1)}, f32[64,64]{1,0:T(8,128)S(1)}, f32[...) custom-call(s32[4]{0:T(128)} %len_hbm.1, s32[4,8]{1,0:T(4,128)} %path_hbm.1, s32[4,64]{1,0:T(4,128)} %par_hbm.1, ...), custom_call_target="tpu_custom_call" | custom-call | flops 10000000 | tf_op jit(solution)/shard_map/prelude/pallas_call | solution.py:160
  3.2 3.0 %collective-permute-start.2 = (bf16[72,1536]{1,0:T(8,128)(2,1)S(1)}, bf16[72,1536]{1,0:T(8,128)(2,1)S(1)}, u32[]{:S(2)}, u32[]{:S(2)}) collective-permute-start(bf16[72,1536]{1,0:T(8,128)(2,1)S(1)} %get-tuple-element.44.pay_ref.refs_0_), channel_id=1, source_target_pairs={{0,1},{1,0},{2,3},{3,2},{4,5},{5,4},{6,7},{7,6},{8,9},{9,8},{10,11... | collective-permute-start | bytes 663560 | tf_op jit(solution)/shard_map/ppermute | solution.py:56
  6.2 1.5 %collective-permute-start.1 = (bf16[72,1536]{1,0:T(8,128)(2,1)S(1)}, bf16[72,1536]{1,0:T(8,128)(2,1)S(1)}, u32[]{:S(2)}, u32[]{:S(2)}) collective-permute-start(bf16[72,1536]{1,0:T(8,128)(2,1)S(1)} %get-tuple-element.44.pay_ref.refs_0_), channel_id=1, source_target_pairs={{0,2},{1,3},{2,0},{3,1},{4,6},{5,7},{6,4},{7,5},{8,10},{9,11},{10,... | collective-permute-start | bytes 663560 | tf_op jit(solution)/shard_map/ppermute | solution.py:56
  7.7 0.0 collective-permute-start
  7.7 3.8 %prepare.1 = (bf16[4,8,512,128]{3,2,1,0:T(8,128)(2,1)S(1)}, f32[8,64,16]{2,1,0:T(8,128)S(1)}, bf16[32,1536]{1,0:T(8,128)(2,1)S(1)}) custom-call(bf16[4,4096,128]{2,1,0:T(8,128)(2,1)} %bitcast.12, s32[8,8,64]{2,1,0:T(8,128)} %bitcast.15, f32[16,1536]{1,0:T(8,128)} %bitcast.14), custom_call_target="tpu_custom_call" | custom-call | flops 100000000 | tf_op jit(solution)/shard_map/prepare/pallas_call | solution.py:226
  11.5 2.2 %attend.4 = (bf16[13,64,128]{2,1,0:T(8,128)(2,1)S(1)}, bf16[13,64,128]{2,1,0:T(8,128)(2,1)S(1)}, bf16[13,64,128]{2,1,0:T(8,128)(2,1)S(1)}, bf16[13,64,128]{2,1,0:T(8,128)(2,1)S(1)}) custom-call(bf16[72,1536]{1,0:T(8,128)(2,1)S(1)} %get-tuple-element.44.pay_ref.refs_0_, bf16[4,8,512,128]{3,2,1,0:T(8,128)(2,1)S(1)} %get-tuple-element.45.kv_ref, ...), custom_call_target="tpu_custom_call" | custom-call | flops 400000000 | tf_op jit(solution)/shard_map/attend/pallas_call | solution.py:426
  13.7 0.0 collective-permute-done.2.pay_ref.refs_1_
  13.7 1.4 %attend.5 = (bf16[13,64,128]{2,1,0:T(8,128)(2,1)S(1)}, bf16[13,64,128]{2,1,0:T(8,128)(2,1)S(1)}, bf16[13,64,128]{2,1,0:T(8,128)(2,1)S(1)}, bf16[13,64,128]{2,1,0:T(8,128)(2,1)S(1)}) custom-call(bf16[72,1536]{1,0:T(8,128)(2,1)S(1)} %collective-permute-done.2.pay_ref.refs_1_, ...), custom_call_target="tpu_custom_call", output_to_operand_aliasing={{0}: (7, {}), {1}: (8, {}), {2}: (9, {}), {3}: (10, {})} | custom-call | flops 400000000 | tf_op jit(solution)/shard_map/attend/pallas_call | solution.py:426
  15.2 2.6 %collective-permute-done.1.pay_ref.refs_2_ = bf16[72,1536]{1,0:T(8,128)(2,1)S(1)} collective-permute-done((bf16[72,1536]{1,0:T(8,128)(2,1)S(1)}, bf16[72,1536]{1,0:T(8,128)(2,1)S(1)}, u32[]{:S(2)}, u32[]{:S(2)}) %collective-permute-start.1) | collective-permute-done | bytes 221216 | tf_op jit(solution)/shard_map/ppermute | solution.py:56
  17.8 1.4 %attend.6 = (bf16[13,64,128]{2,1,0:T(8,128)(2,1)S(1)}, bf16[13,64,128]{2,1,0:T(8,128)(2,1)S(1)}, bf16[13,64,128]{2,1,0:T(8,128)(2,1)S(1)}, bf16[13,64,128]{2,1,0:T(8,128)(2,1)S(1)}) custom-call(bf16[72,1536]{1,0:T(8,128)(2,1)S(1)} %collective-permute-done.1.pay_ref.refs_2_, ...), custom_call_target="tpu_custom_call", output_to_operand_aliasing={{0}: (7, {}), {1}: (8, {}), {2}: (9, {}), {3}: (10, {})} | custom-call | flops 400000000 | tf_op jit(solution)/shard_map/attend/pallas_call | solution.py:426
  19.2 0.0 copy-start.3
  19.2 0.0 collective-permute-done.pay_ref.refs_3_
  19.2 0.0 copy-start.5
  19.2 0.0 copy-start
  19.2 0.0 copy-start.1
  19.2 1.4 %attend.7 = (bf16[13,64,128]{2,1,0:T(8,128)(2,1)S(1)}, bf16[13,64,128]{2,1,0:T(8,128)(2,1)S(1)}, bf16[13,64,128]{2,1,0:T(8,128)(2,1)S(1)}, bf16[13,64,128]{2,1,0:T(8,128)(2,1)S(1)}) custom-call(bf16[72,1536]{1,0:T(8,128)(2,1)S(1)} %collective-permute-done.pay_ref.refs_3_, ...), custom_call_target="tpu_custom_call", output_to_operand_aliasing={{0}: (7, {}), {1}: (8, {}), {2}: (9, {}), {3}: (10, {})} | custom-call | flops 400000000 | tf_op jit(solution)/shard_map/attend/pallas_call | solution.py:426
  20.7 0.1 collective-permute-start.3
  20.7 2.0 %collective-permute-start.4 = (bf16[13,64,128]{2,1,0:T(8,128)(2,1)S(1)}, bf16[13,64,128]{2,1,0:T(8,128)(2,1)S(1)}, u32[]{:S(2)}, u32[]{:S(2)}) collective-permute-start(bf16[13,64,128]{2,1,0:T(8,128)(2,1)S(1)} %get-tuple-element.65), channel_id=1, source_target_pairs={{0,2},{1,3},{2,0},{3,1},{4,6},{5,7},{6,4},{7,5},{8,10},{9,11},{10,... | collective-permute-start | bytes 638984 | tf_op jit(solution)/shard_map/ppermute | solution.py:56
  22.8 1.4 %collective-permute-start.5 = (bf16[13,64,128]{2,1,0:T(8,128)(2,1)S(1)}, bf16[13,64,128]{2,1,0:T(8,128)(2,1)S(1)}, u32[]{:S(2)}, u32[]{:S(2)}) collective-permute-start(bf16[13,64,128]{2,1,0:T(8,128)(2,1)S(1)} %get-tuple-element.66), channel_id=1, source_target_pairs={{0,3},{1,2},{2,1},{3,0},{4,7},{5,6},{6,5},{7,4},{8,11},{9,10},{10,... | collective-permute-start | bytes 638984 | tf_op jit(solution)/shard_map/ppermute | solution.py:56
  24.2 3.4 %collective-permute-done.3.refs_1_ = bf16[13,64,128]{2,1,0:T(8,128)(2,1)S(1)} collective-permute-done((bf16[13,64,128]{2,1,0:T(8,128)(2,1)S(1)}, bf16[13,64,128]{2,1,0:T(8,128)(2,1)S(1)}, u32[]{:S(2)}, u32[]{:S(2)}) %collective-permute-start.3) | collective-permute-done | bytes 213024 | tf_op jit(solution)/shard_map/ppermute | solution.py:56
  27.6 3.3 %collective-permute-done.4.refs_2_ = bf16[13,64,128]{2,1,0:T(8,128)(2,1)S(1)} collective-permute-done((bf16[13,64,128]{2,1,0:T(8,128)(2,1)S(1)}, bf16[13,64,128]{2,1,0:T(8,128)(2,1)S(1)}, u32[]{:S(2)}, u32[]{:S(2)}) %collective-permute-start.4) | collective-permute-done | bytes 213024 | tf_op jit(solution)/shard_map/ppermute | solution.py:56
  30.9 0.0 collective-permute-done.5.refs_3_
  30.9 2.3 %join.1 = (f32[64,1536]{1,0:T(8,128)S(1)}, bf16[64,1536]{1,0:T(8,128)(2,1)S(1)}, bf16[64,1536]{1,0:T(8,128)(2,1)S(1)}, bf16[64,1536]{1,0:T(8,128)(2,1)S(1)}) custom-call(bf16[384,1536]{1,0:T(8,128)(2,1)S(1)} %copy-done.3, bf16[13,64,128]{2,1,0:T(8,128)(2,1)S(1)} %get-tuple-element.63.refs_0_, bf16[13,64,128]{2,1,0:T(8,128)(2,1)S(1)} %collective-permute-done.3.refs_1_, ...), custom_call_target="tpu_custom_call" | custom-call | flops 400000000 | tf_op jit(solution)/shard_map/join/pallas_call | solution.py:482
  33.3 1.1 %collective-permute-start.6 = (bf16[64,1536]{1,0:T(8,128)(2,1)S(1)}, bf16[64,1536]{1,0:T(8,128)(2,1)S(1)}, u32[]{:S(2)}, u32[]{:S(2)}) collective-permute-start(bf16[64,1536]{1,0:T(8,128)(2,1)S(1)} %get-tuple-element.68), channel_id=1, source_target_pairs={{0,1},{1,0},{2,3},{3,2},{4,5},{5,4},{6,7},{7,6},{8,9},{9,8},{10,11... | collective-permute-start | bytes 589832 | tf_op jit(solution)/shard_map/ppermute | solution.py:56
  34.4 1.7 %collective-permute-start.7 = (bf16[64,1536]{1,0:T(8,128)(2,1)S(1)}, bf16[64,1536]{1,0:T(8,128)(2,1)S(1)}, u32[]{:S(2)}, u32[]{:S(2)}) collective-permute-start(bf16[64,1536]{1,0:T(8,128)(2,1)S(1)} %get-tuple-element.69), channel_id=1, source_target_pairs={{0,2},{1,3},{2,0},{3,1},{4,6},{5,7},{6,4},{7,5},{8,10},{9,11},{10,... | collective-permute-start | bytes 589832 | tf_op jit(solution)/shard_map/ppermute | solution.py:56
  36.1 0.7 collective-permute-start.8
  36.8 2.2 %collective-permute-done.6.refs_0_ = bf16[64,1536]{1,0:T(8,128)(2,1)S(1)} collective-permute-done((bf16[64,1536]{1,0:T(8,128)(2,1)S(1)}, bf16[64,1536]{1,0:T(8,128)(2,1)S(1)}, u32[]{:S(2)}, u32[]{:S(2)}) %collective-permute-start.6) | collective-permute-done | bytes 196640 | tf_op jit(solution)/shard_map/ppermute | solution.py:56
  39.0 2.4 %collective-permute-done.7.refs_1_ = bf16[64,1536]{1,0:T(8,128)(2,1)S(1)} collective-permute-done((bf16[64,1536]{1,0:T(8,128)(2,1)S(1)}, bf16[64,1536]{1,0:T(8,128)(2,1)S(1)}, u32[]{:S(2)}, u32[]{:S(2)}) %collective-permute-start.7) | collective-permute-done | bytes 196640 | tf_op jit(solution)/shard_map/ppermute | solution.py:56
  41.4 1.3 %collective-permute-done.8.refs_2_ = bf16[64,1536]{1,0:T(8,128)(2,1)S(1)} collective-permute-done((bf16[64,1536]{1,0:T(8,128)(2,1)S(1)}, bf16[64,1536]{1,0:T(8,128)(2,1)S(1)}, u32[]{:S(2)}, u32[]{:S(2)}) %collective-permute-start.8) | collective-permute-done | bytes 196640 | tf_op jit(solution)/shard_map/ppermute | solution.py:56
  42.7 0.2 norm.1
  42.9 0.1 collective-permute-start.9
  43.0 1.6 %collective-permute-start.12 = (bf16[64,1536]{1,0:T(8,128)(2,1)S(1)}, bf16[64,1536]{1,0:T(8,128)(2,1)S(1)}, u32[]{:S(2)}, u32[]{:S(2)}) collective-permute-start(bf16[64,1536]{1,0:T(8,128)(2,1)S(1)} %get-tuple-element.74.a_ref), channel_id=1, source_target_pairs={{0,8},{4,12},{8,0},{12,4},{16,24},{20,28},{24,16},{28,20},{1,9},{5... | collective-permute-start | bytes 589832 | tf_op jit(solution)/shard_map/ppermute | solution.py:56
  44.6 2.6 %collective-permute-start.11 = (bf16[64,1536]{1,0:T(8,128)(2,1)S(1)}, bf16[64,1536]{1,0:T(8,128)(2,1)S(1)}, u32[]{:S(2)}, u32[]{:S(2)}) collective-permute-start(bf16[64,1536]{1,0:T(8,128)(2,1)S(1)} %get-tuple-element.74.a_ref), channel_id=1, source_target_pairs={{0,16},{4,20},{8,24},{12,28},{16,0},{20,4},{24,8},{28,12},{1,17},{... | collective-permute-start | bytes 589832 | tf_op jit(solution)/shard_map/ppermute | solution.py:56
  47.2 0.0 collective-permute-done.9.b_ref
  47.2 1.8 %experts.4 = (f32[64,1536]{1,0:T(8,128)S(1)}, bf16[64,1536]{1,0:T(8,128)(2,1)S(1)}) custom-call(f32[8,64,16]{2,1,0:T(8,128)S(1)} %get-tuple-element.72.bias_ref, bf16[32,1536]{1,0:T(8,128)(2,1)S(1)} %get-tuple-element.73.route_ref, bf16[2,1536,512]{2,1,0:T(8,128)(2,1)S(1)} %copy-done, bf16[2,1536,512]{2,1,0:T(8,128)(2,1)S(1)} %copy-done.1, ...), custom_call_target="tpu_custom_call" | custom-call | flops 1200000000 | tf_op jit(solution)/shard_map/experts/pallas_call | solution.py:637
  49.0 5.4 %collective-permute-done.12.a_ref = bf16[64,1536]{1,0:T(8,128)(2,1)S(1)} collective-permute-done((bf16[64,1536]{1,0:T(8,128)(2,1)S(1)}, bf16[64,1536]{1,0:T(8,128)(2,1)S(1)}, u32[]{:S(2)}, u32[]{:S(2)}) %collective-permute-start.12) | collective-permute-done | bytes 196640 | tf_op jit(solution)/shard_map/ppermute | solution.py:56
  54.4 2.3 %collective-permute-done.11.a_ref = bf16[64,1536]{1,0:T(8,128)(2,1)S(1)} collective-permute-done((bf16[64,1536]{1,0:T(8,128)(2,1)S(1)}, bf16[64,1536]{1,0:T(8,128)(2,1)S(1)}, u32[]{:S(2)}, u32[]{:S(2)}) %collective-permute-start.11) | collective-permute-done | bytes 196640 | tf_op jit(solution)/shard_map/ppermute | solution.py:56
  56.7 0.0 collective-permute-start.13
  56.7 0.5 collective-permute-start.16
  57.2 0.5 collective-permute-start.19
  57.7 0.5 collective-permute-done.13.b_ref
  58.2 1.8 %experts.5 = (f32[64,1536]{1,0:T(8,128)S(1)}, bf16[64,1536]{1,0:T(8,128)(2,1)S(1)}) custom-call(f32[8,64,16]{2,1,0:T(8,128)S(1)} %get-tuple-element.72.bias_ref, bf16[32,1536]{1,0:T(8,128)(2,1)S(1)} %get-tuple-element.73.route_ref, bf16[2,1536,512]{2,1,0:T(8,128)(2,1)S(1)} %copy-done, bf16[2,1536,512]{2,1,0:T(8,128)(2,1)S(1)} %copy-done.1, ...), custom_call_target="tpu_custom_call" | custom-call | flops 1200000000 | tf_op jit(solution)/shard_map/experts/pallas_call | solution.py:637
  60.0 0.2 collective-permute-start.14
  60.2 0.4 collective-permute-start.10
  60.6 0.0 collective-permute-done.16.b_ref
  60.6 1.8 %experts.6 = (f32[64,1536]{1,0:T(8,128)S(1)}, bf16[64,1536]{1,0:T(8,128)(2,1)S(1)}) custom-call(f32[8,64,16]{2,1,0:T(8,128)S(1)} %get-tuple-element.72.bias_ref, bf16[32,1536]{1,0:T(8,128)(2,1)S(1)} %get-tuple-element.73.route_ref, bf16[2,1536,512]{2,1,0:T(8,128)(2,1)S(1)} %copy-done, bf16[2,1536,512]{2,1,0:T(8,128)(2,1)S(1)} %copy-done.1, ...), custom_call_target="tpu_custom_call" | custom-call | flops 1200000000 | tf_op jit(solution)/shard_map/experts/pallas_call | solution.py:637
  62.4 1.6 %collective-permute-done.19.a_ref = bf16[64,1536]{1,0:T(8,128)(2,1)S(1)} collective-permute-done((bf16[64,1536]{1,0:T(8,128)(2,1)S(1)}, bf16[64,1536]{1,0:T(8,128)(2,1)S(1)}, u32[]{:S(2)}, u32[]{:S(2)}) %collective-permute-start.19) | collective-permute-done | bytes 196640 | tf_op jit(solution)/shard_map/ppermute | solution.py:56
  64.0 0.0 collective-permute-start.20
  64.0 0.5 collective-permute-start.17
  64.5 0.0 collective-permute-done.14
  64.6 1.4 %collective-permute-start.15 = (bf16[64,1536]{1,0:T(8,128)(2,1)S(1)}, bf16[64,1536]{1,0:T(8,128)(2,1)S(1)}, u32[]{:S(2)}, u32[]{:S(2)}) collective-permute-start(bf16[64,1536]{1,0:T(8,128)(2,1)S(1)} %add_convert_fusion.3), channel_id=1, source_target_pairs={{0,16},{4,20},{8,24},{12,28},{16,0},{20,4},{24,8},{28,12},{1,17},{... | collective-permute-start | bytes 589832 | tf_op jit(solution)/shard_map/ppermute | solution.py:56
  66.0 0.0 collective-permute-done.20.b_ref
  66.0 1.8 %experts.7 = (f32[64,1536]{1,0:T(8,128)S(1)}, bf16[64,1536]{1,0:T(8,128)(2,1)S(1)}) custom-call(f32[8,64,16]{2,1,0:T(8,128)S(1)} %get-tuple-element.72.bias_ref, bf16[32,1536]{1,0:T(8,128)(2,1)S(1)} %get-tuple-element.73.route_ref, bf16[2,1536,512]{2,1,0:T(8,128)(2,1)S(1)} %copy-done, bf16[2,1536,512]{2,1,0:T(8,128)(2,1)S(1)} %copy-done.1, ...), custom_call_target="tpu_custom_call" | custom-call | flops 1200000000 | tf_op jit(solution)/shard_map/experts/pallas_call | solution.py:637
  67.8 0.1 collective-permute-start.21
  67.9 0.0 collective-permute-done.17
  67.9 1.8 %collective-permute-start.18 = (bf16[64,1536]{1,0:T(8,128)(2,1)S(1)}, bf16[64,1536]{1,0:T(8,128)(2,1)S(1)}, u32[]{:S(2)}, u32[]{:S(2)}) collective-permute-start(bf16[64,1536]{1,0:T(8,128)(2,1)S(1)} %add_convert_fusion.2), channel_id=1, source_target_pairs={{0,8},{4,12},{8,0},{12,4},{16,24},{20,28},{24,16},{28,20},{1,9},{5... | collective-permute-start | bytes 589832 | tf_op jit(solution)/shard_map/ppermute | solution.py:56
  69.7 0.0 collective-permute-done.21
  69.8 1.6 %collective-permute-start.22 = (bf16[64,1536]{1,0:T(8,128)(2,1)S(1)}, bf16[64,1536]{1,0:T(8,128)(2,1)S(1)}, u32[]{:S(2)}, u32[]{:S(2)}) collective-permute-start(bf16[64,1536]{1,0:T(8,128)(2,1)S(1)} %add_convert_fusion.1), channel_id=1, source_target_pairs={{0,24},{4,28},{8,16},{12,20},{16,8},{20,12},{24,0},{28,4},{1,25},{... | collective-permute-start | bytes 589832 | tf_op jit(solution)/shard_map/ppermute | solution.py:56
  71.4 0.6 accepted.1
  72.0 0.0 collective-permute-done.10
  72.0 4.9 %collective-permute-done.15 = bf16[64,1536]{1,0:T(8,128)(2,1)S(1)} collective-permute-done((bf16[64,1536]{1,0:T(8,128)(2,1)S(1)}, bf16[64,1536]{1,0:T(8,128)(2,1)S(1)}, u32[]{:S(2)}, u32[]{:S(2)}) %collective-permute-start.15) | collective-permute-done | bytes 196640 | tf_op jit(solution)/shard_map/ppermute | solution.py:56
  76.9 6.7 %collective-permute-done.18 = bf16[64,1536]{1,0:T(8,128)(2,1)S(1)} collective-permute-done((bf16[64,1536]{1,0:T(8,128)(2,1)S(1)}, bf16[64,1536]{1,0:T(8,128)(2,1)S(1)}, u32[]{:S(2)}, u32[]{:S(2)}) %collective-permute-start.18) | collective-permute-done | bytes 196640 | tf_op jit(solution)/shard_map/ppermute | solution.py:56
  83.6 0.0 collective-permute-done.22
  83.6 0.8 add_convert_fusion
  (12 shorter events, 0.1 us)
Async XLA Ops:
  3.2 10.6 %collective-permute-start.2 = (bf16[72,1536]{1,0:T(8,128)(2,1)S(1)}, bf16[72,1536]{1,0:T(8,128)(2,1)S(1)}, u32[]{:S(2)}, u32[]{:S(2)}) collective-permute-start(bf16[72,1536]{1,0:T(8,128)(2,1)S(1)} %get-tuple-element.44.pay_ref.refs_0_), channel_id=1, source_target_pairs={{0,1},{1,0},{2,3},{3,2},{4,5},{5,4},{6,7},{7,6},{8,9},{9,8},{10,11... | collective-permute-start | bytes 663560 | tf_op jit(solution)/shard_map/ppermute | solution.py:56
  6.2 11.6 %collective-permute-start.1 = (bf16[72,1536]{1,0:T(8,128)(2,1)S(1)}, bf16[72,1536]{1,0:T(8,128)(2,1)S(1)}, u32[]{:S(2)}, u32[]{:S(2)}) collective-permute-start(bf16[72,1536]{1,0:T(8,128)(2,1)S(1)} %get-tuple-element.44.pay_ref.refs_0_), channel_id=1, source_target_pairs={{0,2},{1,3},{2,0},{3,1},{4,6},{5,7},{6,4},{7,5},{8,10},{9,11},{10,... | collective-permute-start | bytes 663560 | tf_op jit(solution)/shard_map/ppermute | solution.py:56
  7.7 11.5 %collective-permute-start = (bf16[72,1536]{1,0:T(8,128)(2,1)S(1)}, bf16[72,1536]{1,0:T(8,128)(2,1)S(1)}, u32[]{:S(2)}, u32[]{:S(2)}) collective-permute-start(bf16[72,1536]{1,0:T(8,128)(2,1)S(1)} %get-tuple-element.44.pay_ref.refs_0_), channel_id=1, source_target_pairs={{0,3},{1,2},{2,1},{3,0},{4,7},{5,6},{6,5},{7,4},{8,11},{9,10},{10,... | collective-permute-start | bytes 663560 | tf_op jit(solution)/shard_map/ppermute | solution.py:56
  17.8 24.9 %copy-start.4 = (bf16[64,1536]{1,0:T(8,128)(2,1)S(1)}, bf16[64,1536]{1,0:T(8,128)(2,1)}, u32[]{:S(2)}) copy-start(bf16[64,1536]{1,0:T(8,128)(2,1)} %hidden_ref.1) | copy-start | bytes 589828
  17.8 29.4 %copy-start.2 = (bf16[2,512,1536]{2,1,0:T(8,128)(2,1)S(1)}, bf16[2,512,1536]{2,1,0:T(8,128)(2,1)}, u32[]{:S(2)}) copy-start(bf16[2,512,1536]{2,1,0:T(8,128)(2,1)} %wd.7) | copy-start | bytes 9437188
  19.2 11.7 %copy-start.3 = (bf16[384,1536]{1,0:T(8,128)(2,1)S(1)}, bf16[384,1536]{1,0:T(8,128)(2,1)}, u32[]{:S(2)}) copy-start(bf16[384,1536]{1,0:T(8,128)(2,1)} %weight_ref.1) | copy-start | bytes 3538948
  19.2 17.6 %copy-start.5 = (f32[1536]{0:T(1024)S(1)}, f32[1536]{0:T(1024)}, u32[]{:S(2)}) copy-start(f32[1536]{0:T(1024)} %param.24) | copy-start | bytes 18436
  19.2 28.0 %copy-start = (bf16[2,1536,512]{2,1,0:T(8,128)(2,1)S(1)}, bf16[2,1536,512]{2,1,0:T(8,128)(2,1)}, u32[]{:S(2)}) copy-start(bf16[2,1536,512]{2,1,0:T(8,128)(2,1)} %wg.7) | copy-start | bytes 9437188
  19.2 28.0 %copy-start.1 = (bf16[2,1536,512]{2,1,0:T(8,128)(2,1)S(1)}, bf16[2,1536,512]{2,1,0:T(8,128)(2,1)}, u32[]{:S(2)}) copy-start(bf16[2,1536,512]{2,1,0:T(8,128)(2,1)} %wu.7) | copy-start | bytes 9437188
  20.7 6.9 %collective-permute-start.3 = (bf16[13,64,128]{2,1,0:T(8,128)(2,1)S(1)}, bf16[13,64,128]{2,1,0:T(8,128)(2,1)S(1)}, u32[]{:S(2)}, u32[]{:S(2)}) collective-permute-start(bf16[13,64,128]{2,1,0:T(8,128)(2,1)S(1)} %get-tuple-element.64), channel_id=1, source_target_pairs={{0,1},{1,0},{2,3},{3,2},{4,5},{5,4},{6,7},{7,6},{8,9},{9,8},{10,11... | collective-permute-start | bytes 638984 | tf_op jit(solution)/shard_map/ppermute | solution.py:56
  20.7 10.2 %collective-permute-start.4 = (bf16[13,64,128]{2,1,0:T(8,128)(2,1)S(1)}, bf16[13,64,128]{2,1,0:T(8,128)(2,1)S(1)}, u32[]{:S(2)}, u32[]{:S(2)}) collective-permute-start(bf16[13,64,128]{2,1,0:T(8,128)(2,1)S(1)} %get-tuple-element.65), channel_id=1, source_target_pairs={{0,2},{1,3},{2,0},{3,1},{4,6},{5,7},{6,4},{7,5},{8,10},{9,11},{10,... | collective-permute-start | bytes 638984 | tf_op jit(solution)/shard_map/ppermute | solution.py:56
  22.8 8.1 %collective-permute-start.5 = (bf16[13,64,128]{2,1,0:T(8,128)(2,1)S(1)}, bf16[13,64,128]{2,1,0:T(8,128)(2,1)S(1)}, u32[]{:S(2)}, u32[]{:S(2)}) collective-permute-start(bf16[13,64,128]{2,1,0:T(8,128)(2,1)S(1)} %get-tuple-element.66), channel_id=1, source_target_pairs={{0,3},{1,2},{2,1},{3,0},{4,7},{5,6},{6,5},{7,4},{8,11},{9,10},{10,... | collective-permute-start | bytes 638984 | tf_op jit(solution)/shard_map/ppermute | solution.py:56
  33.3 5.7 %collective-permute-start.6 = (bf16[64,1536]{1,0:T(8,128)(2,1)S(1)}, bf16[64,1536]{1,0:T(8,128)(2,1)S(1)}, u32[]{:S(2)}, u32[]{:S(2)}) collective-permute-start(bf16[64,1536]{1,0:T(8,128)(2,1)S(1)} %get-tuple-element.68), channel_id=1, source_target_pairs={{0,1},{1,0},{2,3},{3,2},{4,5},{5,4},{6,7},{7,6},{8,9},{9,8},{10,11... | collective-permute-start | bytes 589832 | tf_op jit(solution)/shard_map/ppermute | solution.py:56
  34.4 7.0 %collective-permute-start.7 = (bf16[64,1536]{1,0:T(8,128)(2,1)S(1)}, bf16[64,1536]{1,0:T(8,128)(2,1)S(1)}, u32[]{:S(2)}, u32[]{:S(2)}) collective-permute-start(bf16[64,1536]{1,0:T(8,128)(2,1)S(1)} %get-tuple-element.69), channel_id=1, source_target_pairs={{0,2},{1,3},{2,0},{3,1},{4,6},{5,7},{6,4},{7,5},{8,10},{9,11},{10,... | collective-permute-start | bytes 589832 | tf_op jit(solution)/shard_map/ppermute | solution.py:56
  36.1 6.6 %collective-permute-start.8 = (bf16[64,1536]{1,0:T(8,128)(2,1)S(1)}, bf16[64,1536]{1,0:T(8,128)(2,1)S(1)}, u32[]{:S(2)}, u32[]{:S(2)}) collective-permute-start(bf16[64,1536]{1,0:T(8,128)(2,1)S(1)} %get-tuple-element.70), channel_id=1, source_target_pairs={{0,3},{1,2},{2,1},{3,0},{4,7},{5,6},{6,5},{7,4},{8,11},{9,10},{10,... | collective-permute-start | bytes 589832 | tf_op jit(solution)/shard_map/ppermute | solution.py:56
  42.9 4.3 %collective-permute-start.9 = (bf16[64,1536]{1,0:T(8,128)(2,1)S(1)}, bf16[64,1536]{1,0:T(8,128)(2,1)S(1)}, u32[]{:S(2)}, u32[]{:S(2)}) collective-permute-start(bf16[64,1536]{1,0:T(8,128)(2,1)S(1)} %get-tuple-element.74.a_ref), channel_id=1, source_target_pairs={{0,4},{4,0},{8,12},{12,8},{16,20},{20,16},{24,28},{28,24},{1,5},{5... | collective-permute-start | bytes 589832 | tf_op jit(solution)/shard_map/ppermute | solution.py:56
  43.0 11.4 %collective-permute-start.12 = (bf16[64,1536]{1,0:T(8,128)(2,1)S(1)}, bf16[64,1536]{1,0:T(8,128)(2,1)S(1)}, u32[]{:S(2)}, u32[]{:S(2)}) collective-permute-start(bf16[64,1536]{1,0:T(8,128)(2,1)S(1)} %get-tuple-element.74.a_ref), channel_id=1, source_target_pairs={{0,8},{4,12},{8,0},{12,4},{16,24},{20,28},{24,16},{28,20},{1,9},{5... | collective-permute-start | bytes 589832 | tf_op jit(solution)/shard_map/ppermute | solution.py:56
  44.6 12.1 %collective-permute-start.11 = (bf16[64,1536]{1,0:T(8,128)(2,1)S(1)}, bf16[64,1536]{1,0:T(8,128)(2,1)S(1)}, u32[]{:S(2)}, u32[]{:S(2)}) collective-permute-start(bf16[64,1536]{1,0:T(8,128)(2,1)S(1)} %get-tuple-element.74.a_ref), channel_id=1, source_target_pairs={{0,16},{4,20},{8,24},{12,28},{16,0},{20,4},{24,8},{28,12},{1,17},{... | collective-permute-start | bytes 589832 | tf_op jit(solution)/shard_map/ppermute | solution.py:56
  56.7 1.4 %collective-permute-start.13 = (bf16[64,1536]{1,0:T(8,128)(2,1)S(1)}, bf16[64,1536]{1,0:T(8,128)(2,1)S(1)}, u32[]{:S(2)}, u32[]{:S(2)}) collective-permute-start(bf16[64,1536]{1,0:T(8,128)(2,1)S(1)} %collective-permute-done.11.a_ref), channel_id=1, source_target_pairs={{0,4},{4,0},{8,12},{12,8},{16,20},{20,16},{24,28},{28,24},{1,5},{5... | collective-permute-start | bytes 589832 | tf_op jit(solution)/shard_map/ppermute | solution.py:56
  56.7 3.9 %collective-permute-start.16 = (bf16[64,1536]{1,0:T(8,128)(2,1)S(1)}, bf16[64,1536]{1,0:T(8,128)(2,1)S(1)}, u32[]{:S(2)}, u32[]{:S(2)}) collective-permute-start(bf16[64,1536]{1,0:T(8,128)(2,1)S(1)} %collective-permute-done.12.a_ref), channel_id=1, source_target_pairs={{0,4},{4,0},{8,12},{12,8},{16,20},{20,16},{24,28},{28,24},{1,5},{5... | collective-permute-start | bytes 589832 | tf_op jit(solution)/shard_map/ppermute | solution.py:56
  57.2 6.8 %collective-permute-start.19 = (bf16[64,1536]{1,0:T(8,128)(2,1)S(1)}, bf16[64,1536]{1,0:T(8,128)(2,1)S(1)}, u32[]{:S(2)}, u32[]{:S(2)}) collective-permute-start(bf16[64,1536]{1,0:T(8,128)(2,1)S(1)} %collective-permute-done.11.a_ref), channel_id=1, source_target_pairs={{0,8},{4,12},{8,0},{12,4},{16,24},{20,28},{24,16},{28,20},{1,9},{5... | collective-permute-start | bytes 589832 | tf_op jit(solution)/shard_map/ppermute | solution.py:56
  60.0 4.6 %collective-permute-start.14 = (bf16[64,1536]{1,0:T(8,128)(2,1)S(1)}, bf16[64,1536]{1,0:T(8,128)(2,1)S(1)}, u32[]{:S(2)}, u32[]{:S(2)}) collective-permute-start(bf16[64,1536]{1,0:T(8,128)(2,1)S(1)} %get-tuple-element.79), channel_id=1, source_target_pairs={{0,4},{4,0},{8,12},{12,8},{16,20},{20,16},{24,28},{28,24},{1,5},{5... | collective-permute-start | bytes 589832 | tf_op jit(solution)/shard_map/ppermute | solution.py:56
  60.2 11.9 %collective-permute-start.10 = (bf16[64,1536]{1,0:T(8,128)(2,1)S(1)}, bf16[64,1536]{1,0:T(8,128)(2,1)S(1)}, u32[]{:S(2)}, u32[]{:S(2)}) collective-permute-start(bf16[64,1536]{1,0:T(8,128)(2,1)S(1)} %get-tuple-element.76), channel_id=1, source_target_pairs={{0,4},{4,0},{8,12},{12,8},{16,20},{20,16},{24,28},{28,24},{1,5},{5... | collective-permute-start | bytes 589832 | tf_op jit(solution)/shard_map/ppermute | solution.py:56
  64.0 1.9 %collective-permute-start.20 = (bf16[64,1536]{1,0:T(8,128)(2,1)S(1)}, bf16[64,1536]{1,0:T(8,128)(2,1)S(1)}, u32[]{:S(2)}, u32[]{:S(2)}) collective-permute-start(bf16[64,1536]{1,0:T(8,128)(2,1)S(1)} %collective-permute-done.19.a_ref), channel_id=1, source_target_pairs={{0,4},{4,0},{8,12},{12,8},{16,20},{20,16},{24,28},{28,24},{1,5},{5... | collective-permute-start | bytes 589832 | tf_op jit(solution)/shard_map/ppermute | solution.py:56
  64.0 3.8 %collective-permute-start.17 = (bf16[64,1536]{1,0:T(8,128)(2,1)S(1)}, bf16[64,1536]{1,0:T(8,128)(2,1)S(1)}, u32[]{:S(2)}, u32[]{:S(2)}) collective-permute-start(bf16[64,1536]{1,0:T(8,128)(2,1)S(1)} %get-tuple-element.82), channel_id=1, source_target_pairs={{0,4},{4,0},{8,12},{12,8},{16,20},{20,16},{24,28},{28,24},{1,5},{5... | collective-permute-start | bytes 589832 | tf_op jit(solution)/shard_map/ppermute | solution.py:56
  64.6 12.3 %collective-permute-start.15 = (bf16[64,1536]{1,0:T(8,128)(2,1)S(1)}, bf16[64,1536]{1,0:T(8,128)(2,1)S(1)}, u32[]{:S(2)}, u32[]{:S(2)}) collective-permute-start(bf16[64,1536]{1,0:T(8,128)(2,1)S(1)} %add_convert_fusion.3), channel_id=1, source_target_pairs={{0,16},{4,20},{8,24},{12,28},{16,0},{20,4},{24,8},{28,12},{1,17},{... | collective-permute-start | bytes 589832 | tf_op jit(solution)/shard_map/ppermute | solution.py:56
  67.8 1.9 %collective-permute-start.21 = (bf16[64,1536]{1,0:T(8,128)(2,1)S(1)}, bf16[64,1536]{1,0:T(8,128)(2,1)S(1)}, u32[]{:S(2)}, u32[]{:S(2)}) collective-permute-start(bf16[64,1536]{1,0:T(8,128)(2,1)S(1)} %get-tuple-element.85), channel_id=1, source_target_pairs={{0,4},{4,0},{8,12},{12,8},{16,20},{20,16},{24,28},{28,24},{1,5},{5... | collective-permute-start | bytes 589832 | tf_op jit(solution)/shard_map/ppermute | solution.py:56
  67.9 15.7 %collective-permute-start.18 = (bf16[64,1536]{1,0:T(8,128)(2,1)S(1)}, bf16[64,1536]{1,0:T(8,128)(2,1)S(1)}, u32[]{:S(2)}, u32[]{:S(2)}) collective-permute-start(bf16[64,1536]{1,0:T(8,128)(2,1)S(1)} %add_convert_fusion.2), channel_id=1, source_target_pairs={{0,8},{4,12},{8,0},{12,4},{16,24},{20,28},{24,16},{28,20},{1,9},{5... | collective-permute-start | bytes 589832 | tf_op jit(solution)/shard_map/ppermute | solution.py:56
  69.8 13.8 %collective-permute-start.22 = (bf16[64,1536]{1,0:T(8,128)(2,1)S(1)}, bf16[64,1536]{1,0:T(8,128)(2,1)S(1)}, u32[]{:S(2)}, u32[]{:S(2)}) collective-permute-start(bf16[64,1536]{1,0:T(8,128)(2,1)S(1)} %add_convert_fusion.1), channel_id=1, source_target_pairs={{0,24},{4,28},{8,16},{12,20},{16,8},{20,12},{24,0},{28,4},{1,25},{... | collective-permute-start | bytes 589832 | tf_op jit(solution)/shard_map/ppermute | solution.py:56

commit v4 on v3

--- a/solution.py
+++ b/solution.py
@@ -61,8 +61,8 @@
 
 
 def prelude_kernel(
-    len_hbm, path_hbm, par_hbm, q_hbm, kv_hbm,
-    pay_ref, key_ref, val_ref, anc_ref, pos_ref, lim_ref,
+    len_hbm, path_hbm, par_hbm, q_hbm, kv_hbm, cache_hbm,
+    pay_ref, key_ref, val_ref, anc_ref, pos_ref, lim_ref, packed_ref,
     len_ref, path_ref, par_ref, q_ref, kv_ref, kv_f, anc_all, sems,
 ):
     copies = [
@@ -70,7 +70,7 @@
         for j, (src, dst) in enumerate(
             (
                 (par_hbm, par_ref), (len_hbm, len_ref), (path_hbm, path_ref),
-                (kv_hbm, kv_ref), (q_hbm, q_ref),
+                (kv_hbm, kv_ref), (q_hbm, q_ref), (cache_hbm, packed_ref),
             )
         )
     ]
@@ -151,9 +151,10 @@
         y2 = jnp.where(low, x1, x2)
         for i, y in enumerate((y0, y1, y2)):
             pay_ref[:n, (GROUPS * b + i) * LANES : (GROUPS * b + i + 1) * LANES] = y.astype(BF)
-
-
-def prelude(cache_len, path, parents, queries, kv):
+    copies[5].wait()
+
+
+def prelude(cache_len, path, parents, queries, kv, cache):
     requests, draft = parents.shape
     n, width = queries.shape
     kv_width = KVH * HD
@@ -166,9 +167,10 @@
             jax.ShapeDtypeStruct((draft, draft), F32),
             jax.ShapeDtypeStruct((requests * draft, LANES), F32),
             jax.ShapeDtypeStruct((requests, 8, LANES), F32),
+            jax.ShapeDtypeStruct(cache.shape, BF),
         ),
-        in_specs=[in_hbm()] * 5,
-        out_specs=(whole(),) * 6,
+        in_specs=[in_hbm()] * 6,
+        out_specs=(whole(),) * 7,
         scratch_shapes=[
             pltpu.SMEM(cache_len.shape, jnp.int32),
             pltpu.SMEM(path.shape, jnp.int32),
@@ -177,33 +179,47 @@
             pltpu.VMEM(kv.shape, BF),
             pltpu.VMEM(kv.shape, F32),
             pltpu.VMEM((requests, draft, draft), F32),
-            pltpu.SemaphoreType.DMA((5,)),
+            pltpu.SemaphoreType.DMA((6,)),
         ],
         compiler_params=params(8),
         cost_estimate=cost(1e7),
         name="prelude",
-    )(*[fixed(x) for x in (cache_len, path, parents, queries, kv)])
-
-
-def prepare_kernel(
-    cache_hbm, routes_hbm, router_hbm, out_ref, bias_ref, route_w_ref,
-    packed, kv_f, routes_ref, router_ref, sems,
-):
+    )(*[fixed(x) for x in (cache_len, path, parents, queries, kv, cache)])
+
+
+def unpack_kernel(packed_ref, out_ref, kv_f):
     requests, _, cells, _ = out_ref.shape
+    for r in range(requests):
+        kv_f[r % 2] = packed_ref[r].astype(F32)
+        for j in range(2 * PAIRS):
+            out_ref[r, j] = kv_f[r % 2, pl.ds(j, cells, stride=2 * PAIRS), :].astype(BF)
+
+
+def unpack(packed):
+    requests, span, _ = packed.shape
+    return pl.pallas_call(
+        unpack_kernel,
+        out_shape=jax.ShapeDtypeStruct(
+            (requests, 2 * PAIRS, span // (2 * PAIRS), LANES), BF
+        ),
+        in_specs=[whole()],
+        out_specs=whole(),
+        scratch_shapes=[pltpu.VMEM((2, span, LANES), F32)],
+        compiler_params=params(8),
+        cost_estimate=cost(1e8),
+        name="unpack",
+    )(packed)
+
+
+def routing_kernel(routes_hbm, router_hbm, bias_ref, route_w_ref, routes_ref, router_ref, sems):
     copies = [
-        pltpu.make_async_copy(cache_hbm.at[r], packed.at[r], sems.at[r]) for r in range(requests)
+        pltpu.make_async_copy(routes_hbm, routes_ref, sems.at[0]),
+        pltpu.make_async_copy(router_hbm, router_ref, sems.at[1]),
     ]
-    copies.append(pltpu.make_async_copy(routes_hbm, routes_ref, sems.at[requests]))
-    copies.append(pltpu.make_async_copy(router_hbm, router_ref, sems.at[requests + 1]))
     for copy in copies:
         copy.start()
-    for r in range(requests):
-        copies[r].wait()
-        kv_f[...] = packed[r].astype(F32)
-        for j in range(2 * PAIRS):
-            out_ref[r, j] = kv_f[pl.ds(j, cells, stride=2 * PAIRS), :].astype(BF)
-    copies[requests].wait()
-    copies[requests + 1].wait()
+    for copy in copies:
+        copy.wait()
     experts = router_ref.shape[0]
     router = router_ref[...]
     high = router.astype(BF)
@@ -218,31 +234,26 @@
         bias_ref[d] = jnp.where(hit, 0.0, NEG).T
 
 
-def prepare(cache, routes, router):
-    requests, span, _ = cache.shape
-    cells = span // (2 * PAIRS)
+def routing(routes, router):
     experts, width = router.shape
     blocks, top, n = routes.shape
     return pl.pallas_call(
-        prepare_kernel,
+        routing_kernel,
         out_shape=(
-            jax.ShapeDtypeStruct((requests, 2 * PAIRS, cells, LANES), BF),
             jax.ShapeDtypeStruct((blocks, n, experts), F32),
             jax.ShapeDtypeStruct((2 * experts, width), BF),
         ),
-        in_specs=[in_hbm()] * 3,
-        out_specs=(whole(),) * 3,
+        in_specs=[in_hbm()] * 2,
+        out_specs=(whole(),) * 2,
         scratch_shapes=[
-            pltpu.VMEM(cache.shape, BF),
-            pltpu.VMEM((span, LANES), F32),
             pltpu.VMEM(routes.shape, jnp.int32),
             pltpu.VMEM(router.shape, F32),
-            pltpu.SemaphoreType.DMA((requests + 2,)),
+            pltpu.SemaphoreType.DMA((2,)),
         ],
-        compiler_params=params(16),
-        cost_estimate=cost(1e8),
-        name="prepare",
-    )(*[fixed(x) for x in (cache, routes, router)])
+        compiler_params=params(8),
+        cost_estimate=cost(1e6),
+        name="routing",
+    )(fixed(routes), fixed(router))
 
 
 def attend_kernel(
@@ -687,12 +698,17 @@
     data = lax.axis_size("dp")
     n = queries.shape[0]
     requests, draft = parents.shape
-    payload, keys, vals, ancestry, pos, limit = prelude(
-        cache_len, path, parents, queries, rows_by_lane_block(draft_kv)
+    payload, keys, vals, ancestry, pos, limit, packed = prelude(
+        cache_len,
+        path,
+        parents,
+        queries,
+        rows_by_lane_block(draft_kv),
+        rows_by_lane_block(cache_kv),
     )
-    cache = rows_by_lane_block(cache_kv)
     payloads = [payload] + [exchange(payload, "tensor", tensor, k) for k in range(1, tensor)]
-    unpacked, bias, route = prepare(cache, jnp.swapaxes(routes, 1, 2), router.T)
+    unpacked = unpack(packed)
+    tables = jnp.swapaxes(routes, 1, 2), router.T
     gain = norm_gain.reshape(1, -1)
     if n == draft and tensor == PAIRS:
         parts = ()
@@ -700,7 +716,10 @@
             parts = attend_split(
                 k, tensor, payloads[k], unpacked, keys, vals, ancestry, pos, limit, parts
             )
+        tables = lax.optimization_barrier((*tables, parts[0]))[:2]
         parts = [parts[0]] + [exchange(parts[j], "tensor", tensor, j) for j in range(1, tensor)]
+        bias, route = routing(*tables)
+        parts, bias, route = lax.optimization_barrier((parts, bias, route))
         products = join_split(w_out, parts)
         others = [exchange(products[k], "tensor", tensor, k) for k in range(1, tensor)]
         mixed, normed = norm(hidden_in, gain, products[0], others)
@@ -718,6 +737,7 @@
         for piece in fetched:
             pieces += [piece, exchange(piece, "dp", data, 1)]
         mixed, normed = join(parts, pieces, hidden_in, gain)
+        bias, route = routing(*tables)
     compacted = accepted(payloads, requests, path.shape[1], n)
 
     steps = data // CORES

time: 84.6 us -> 83.3 us (0.985)
  waiting for transfers between devices: 36.5 us -> 33.2 us
  starting transfers between devices: 22.8 us -> 24.8 us
    ppermute x23, waiting for transfers between devices: 36.5 us -> 33.2 us  [exchange(): return lax.ppermute(x, axis, [(i, i ^ step) for i in range(size)])]
    ppermute x23, starting transfers between devices: 22.8 us -> 24.8 us  [exchange(): return lax.ppermute(x, axis, [(i, i ^ step) for i in range(size)])]
    pallas_call x1 -> x2, Pallas kernels: 3.82 us -> 3.47 us  [the longest x1 2.38 us: unpack(): pl.pallas_call(unpack_kernel, out_shape=jax.ShapeDtypeStruct((requests, 2...]
where the time goes in v4:
time: 83.3 us; the launch traced here: 82.8 us
  waiting for transfers between devices  33.2 us (40%)
  starting transfers between devices  24.8 us (30%)
  Pallas kernels  23 us (28%)
  other arithmetic  0.92 us (1%)
    ppermute x23, waiting for transfers between devices, exchange(): return lax.ppermute(x, axis, [(i, i ^ step) for i in range(size)])  33.2 us
    ppermute x23, starting transfers between devices, exchange(): return lax.ppermute(x, axis, [(i, i ^ step) for i in range(size)])  24.8 us
    pallas_call x4, Pallas kernels, experts_part(): pl.pallas_call(functools.partial(experts_kernel, step), out_shape=(jax.Sh...  7.29 us
    pallas_call x4, Pallas kernels, attend_split(): pl.pallas_call(functools.partial(attend_split_kernel, step, step == 0, co...  6.53 us
    pallas_call x1, Pallas kernels, prelude(): pl.pallas_call(prelude_kernel, out_shape=(jax.ShapeDtypeStruct((n + path....  2.52 us
    pallas_call x1, Pallas kernels, unpack(): pl.pallas_call(unpack_kernel, out_shape=jax.ShapeDtypeStruct((requests, 2...  2.38 us
    pallas_call x1, Pallas kernels, join_split(): pl.pallas_call(functools.partial(join_split_kernel, count), out_shape=tup...  2.35 us
  transfers between devices with their start and end apart: 23, of which 12 were waited for; matrix products, arithmetic and copies ran while one was open for 0% of the time, Pallas kernels for 20%

profile of v4, /device:TPU:0, one launch (start us, length us, event | category | flops | bytes accessed | tf_op | source)
XLA Modules:
  0.0 82.8 jit_solution(15744751738506676520)
XLA Ops:
  0.6 2.5 %prelude.1 = (bf16[72,1536]{1,0:T(8,128)(2,1)S(1)}, bf16[64,512]{1,0:T(8,128)(2,1)S(1)}, bf16[64,512]{1,0:T(8,128)(2,1)S(1)}, f32[64,64]{1,0:T(8,128)S(1)}, f32[...) custom-call(s32[4]{0:T(128)} %len_hbm.1, s32[4,8]{1,0:T(4,128)} %path_hbm.1, ...), custom_call_target="tpu_custom_call" | custom-call | flops 10000000 | tf_op jit(solution)/shard_map/prelude/pallas_call | solution.py:161
  3.2 3.0 %collective-permute-start.2 = (bf16[72,1536]{1,0:T(8,128)(2,1)S(1)}, bf16[72,1536]{1,0:T(8,128)(2,1)S(1)}, u32[]{:S(2)}, u32[]{:S(2)}) collective-permute-start(bf16[72,1536]{1,0:T(8,128)(2,1)S(1)} %get-tuple-element.52.pay_ref.refs_0_), channel_id=1, source_target_pairs={{0,1},{1,0},{2,3},{3,2},{4,5},{5,4},{6,7},{7,6},{8,9},{9,8},{10,11... | collective-permute-start | bytes 663560 | tf_op jit(solution)/shard_map/ppermute | solution.py:56
  6.2 1.5 %collective-permute-start.1 = (bf16[72,1536]{1,0:T(8,128)(2,1)S(1)}, bf16[72,1536]{1,0:T(8,128)(2,1)S(1)}, u32[]{:S(2)}, u32[]{:S(2)}) collective-permute-start(bf16[72,1536]{1,0:T(8,128)(2,1)S(1)} %get-tuple-element.52.pay_ref.refs_0_), channel_id=1, source_target_pairs={{0,2},{1,3},{2,0},{3,1},{4,6},{5,7},{6,4},{7,5},{8,10},{9,11},{10,... | collective-permute-start | bytes 663560 | tf_op jit(solution)/shard_map/ppermute | solution.py:56
  7.7 0.0 collective-permute-start
  7.7 2.4 %unpack.1.kv_ref = bf16[4,8,512,128]{3,2,1,0:T(8,128)(2,1)S(1)} custom-call(bf16[4,4096,128]{2,1,0:T(8,128)(2,1)S(1)} %get-tuple-element.53.packed_ref), custom_call_target="tpu_custom_call" | custom-call | flops 100000000 | tf_op jit(solution)/shard_map/unpack/pallas_call | solution.py:200
  10.1 2.2 %attend.4 = (bf16[13,64,128]{2,1,0:T(8,128)(2,1)S(1)}, bf16[13,64,128]{2,1,0:T(8,128)(2,1)S(1)}, bf16[13,64,128]{2,1,0:T(8,128)(2,1)S(1)}, bf16[13,64,128]{2,1,0:T(8,128)(2,1)S(1)}) custom-call(bf16[72,1536]{1,0:T(8,128)(2,1)S(1)} %get-tuple-element.52.pay_ref.refs_0_, bf16[4,8,512,128]{3,2,1,0:T(8,128)(2,1)S(1)} %unpack.1.kv_ref, ...), custom_call_target="tpu_custom_call" | custom-call | flops 400000000 | tf_op jit(solution)/shard_map/attend/pallas_call | solution.py:437
  12.3 0.1 collective-permute-done.2.pay_ref.refs_1_
  12.4 1.4 %attend.5 = (bf16[13,64,128]{2,1,0:T(8,128)(2,1)S(1)}, bf16[13,64,128]{2,1,0:T(8,128)(2,1)S(1)}, bf16[13,64,128]{2,1,0:T(8,128)(2,1)S(1)}, bf16[13,64,128]{2,1,0:T(8,128)(2,1)S(1)}) custom-call(bf16[72,1536]{1,0:T(8,128)(2,1)S(1)} %collective-permute-done.2.pay_ref.refs_1_, ...), custom_call_target="tpu_custom_call", output_to_operand_aliasing={{0}: (7, {}), {1}: (8, {}), {2}: (9, {}), {3}: (10, {})} | custom-call | flops 400000000 | tf_op jit(solution)/shard_map/attend/pallas_call | solution.py:437
  13.9 3.9 %collective-permute-done.1.pay_ref.refs_2_ = bf16[72,1536]{1,0:T(8,128)(2,1)S(1)} collective-permute-done((bf16[72,1536]{1,0:T(8,128)(2,1)S(1)}, bf16[72,1536]{1,0:T(8,128)(2,1)S(1)}, u32[]{:S(2)}, u32[]{:S(2)}) %collective-permute-start.1) | collective-permute-done | bytes 221216 | tf_op jit(solution)/shard_map/ppermute | solution.py:56
  17.8 1.4 %attend.6 = (bf16[13,64,128]{2,1,0:T(8,128)(2,1)S(1)}, bf16[13,64,128]{2,1,0:T(8,128)(2,1)S(1)}, bf16[13,64,128]{2,1,0:T(8,128)(2,1)S(1)}, bf16[13,64,128]{2,1,0:T(8,128)(2,1)S(1)}) custom-call(bf16[72,1536]{1,0:T(8,128)(2,1)S(1)} %collective-permute-done.1.pay_ref.refs_2_, ...), custom_call_target="tpu_custom_call", output_to_operand_aliasing={{0}: (7, {}), {1}: (8, {}), {2}: (9, {}), {3}: (10, {})} | custom-call | flops 400000000 | tf_op jit(solution)/shard_map/attend/pallas_call | solution.py:437
  19.2 0.0 copy-start.3
  19.2 0.0 collective-permute-done.pay_ref.refs_3_
  19.3 0.0 copy-start.5
  19.3 0.0 copy-start.4
  19.3 0.0 copy-start
  19.3 0.0 copy-start.1
  19.3 1.4 %attend.7 = (bf16[13,64,128]{2,1,0:T(8,128)(2,1)S(1)}, bf16[13,64,128]{2,1,0:T(8,128)(2,1)S(1)}, bf16[13,64,128]{2,1,0:T(8,128)(2,1)S(1)}, bf16[13,64,128]{2,1,0:T(8,128)(2,1)S(1)}) custom-call(bf16[72,1536]{1,0:T(8,128)(2,1)S(1)} %collective-permute-done.pay_ref.refs_3_, ...), custom_call_target="tpu_custom_call", output_to_operand_aliasing={{0}: (7, {}), {1}: (8, {}), {2}: (9, {}), {3}: (10, {})} | custom-call | flops 400000000 | tf_op jit(solution)/shard_map/attend/pallas_call | solution.py:437
  20.8 0.1 collective-permute-start.3
  20.8 2.0 %collective-permute-start.4 = (bf16[13,64,128]{2,1,0:T(8,128)(2,1)S(1)}, bf16[13,64,128]{2,1,0:T(8,128)(2,1)S(1)}, u32[]{:S(2)}, u32[]{:S(2)}) collective-permute-start(bf16[13,64,128]{2,1,0:T(8,128)(2,1)S(1)} %get-tuple-element.73), channel_id=1, source_target_pairs={{0,2},{1,3},{2,0},{3,1},{4,6},{5,7},{6,4},{7,5},{8,10},{9,11},{10,... | collective-permute-start | bytes 638984 | tf_op jit(solution)/shard_map/ppermute | solution.py:56
  22.9 1.4 %collective-permute-start.5 = (bf16[13,64,128]{2,1,0:T(8,128)(2,1)S(1)}, bf16[13,64,128]{2,1,0:T(8,128)(2,1)S(1)}, u32[]{:S(2)}, u32[]{:S(2)}) collective-permute-start(bf16[13,64,128]{2,1,0:T(8,128)(2,1)S(1)} %get-tuple-element.74), channel_id=1, source_target_pairs={{0,3},{1,2},{2,1},{3,0},{4,7},{5,6},{6,5},{7,4},{8,11},{9,10},{10,... | collective-permute-start | bytes 638984 | tf_op jit(solution)/shard_map/ppermute | solution.py:56
  24.3 1.1 %routing.1 = (f32[8,64,16]{2,1,0:T(8,128)S(1)}, bf16[32,1536]{1,0:T(8,128)(2,1)S(1)}) custom-call(s32[8,8,64]{2,1,0:T(8,128)} %bitcast.15, f32[16,1536]{1,0:T(8,128)} %bitcast.14), custom_call_target="tpu_custom_call" | custom-call | flops 1000000 | tf_op jit(solution)/shard_map/routing/pallas_call | solution.py:240
  25.4 2.2 %collective-permute-done.3.refs_1_ = bf16[13,64,128]{2,1,0:T(8,128)(2,1)S(1)} collective-permute-done((bf16[13,64,128]{2,1,0:T(8,128)(2,1)S(1)}, bf16[13,64,128]{2,1,0:T(8,128)(2,1)S(1)}, u32[]{:S(2)}, u32[]{:S(2)}) %collective-permute-start.3) | collective-permute-done | bytes 213024 | tf_op jit(solution)/shard_map/ppermute | solution.py:56
  27.6 3.3 %collective-permute-done.4.refs_2_ = bf16[13,64,128]{2,1,0:T(8,128)(2,1)S(1)} collective-permute-done((bf16[13,64,128]{2,1,0:T(8,128)(2,1)S(1)}, bf16[13,64,128]{2,1,0:T(8,128)(2,1)S(1)}, u32[]{:S(2)}, u32[]{:S(2)}) %collective-permute-start.4) | collective-permute-done | bytes 213024 | tf_op jit(solution)/shard_map/ppermute | solution.py:56
  31.0 0.0 collective-permute-done.5.refs_3_
  31.0 2.4 %join.1 = (f32[64,1536]{1,0:T(8,128)S(1)}, bf16[64,1536]{1,0:T(8,128)(2,1)S(1)}, bf16[64,1536]{1,0:T(8,128)(2,1)S(1)}, bf16[64,1536]{1,0:T(8,128)(2,1)S(1)}) custom-call(bf16[384,1536]{1,0:T(8,128)(2,1)S(1)} %copy-done.3, bf16[13,64,128]{2,1,0:T(8,128)(2,1)S(1)} %get-tuple-element.79.refs_0_, bf16[13,64,128]{2,1,0:T(8,128)(2,1)S(1)} %collective-permute-done.3.refs_1_, ...), custom_call_target="tpu_custom_call" | custom-call | flops 400000000 | tf_op jit(solution)/shard_map/join/pallas_call | solution.py:493
  33.3 0.6 collective-permute-start.6
  34.0 2.2 %collective-permute-start.7 = (bf16[64,1536]{1,0:T(8,128)(2,1)S(1)}, bf16[64,1536]{1,0:T(8,128)(2,1)S(1)}, u32[]{:S(2)}, u32[]{:S(2)}) collective-permute-start(bf16[64,1536]{1,0:T(8,128)(2,1)S(1)} %get-tuple-element.85), channel_id=1, source_target_pairs={{0,2},{1,3},{2,0},{3,1},{4,6},{5,7},{6,4},{7,5},{8,10},{9,11},{10,... | collective-permute-start | bytes 589832 | tf_op jit(solution)/shard_map/ppermute | solution.py:56
  36.1 0.7 collective-permute-start.8
  36.9 2.2 %collective-permute-done.6.refs_0_ = bf16[64,1536]{1,0:T(8,128)(2,1)S(1)} collective-permute-done((bf16[64,1536]{1,0:T(8,128)(2,1)S(1)}, bf16[64,1536]{1,0:T(8,128)(2,1)S(1)}, u32[]{:S(2)}, u32[]{:S(2)}) %collective-permute-start.6) | collective-permute-done | bytes 196640 | tf_op jit(solution)/shard_map/ppermute | solution.py:56
  39.1 2.4 %collective-permute-done.7.refs_1_ = bf16[64,1536]{1,0:T(8,128)(2,1)S(1)} collective-permute-done((bf16[64,1536]{1,0:T(8,128)(2,1)S(1)}, bf16[64,1536]{1,0:T(8,128)(2,1)S(1)}, u32[]{:S(2)}, u32[]{:S(2)}) %collective-permute-start.7) | collective-permute-done | bytes 196640 | tf_op jit(solution)/shard_map/ppermute | solution.py:56
  41.4 1.3 %collective-permute-done.8.refs_2_ = bf16[64,1536]{1,0:T(8,128)(2,1)S(1)} collective-permute-done((bf16[64,1536]{1,0:T(8,128)(2,1)S(1)}, bf16[64,1536]{1,0:T(8,128)(2,1)S(1)}, u32[]{:S(2)}, u32[]{:S(2)}) %collective-permute-start.8) | collective-permute-done | bytes 196640 | tf_op jit(solution)/shard_map/ppermute | solution.py:56
  42.7 0.2 norm.1
  42.9 0.1 collective-permute-start.9
  43.0 2.6 %collective-permute-start.11 = (bf16[64,1536]{1,0:T(8,128)(2,1)S(1)}, bf16[64,1536]{1,0:T(8,128)(2,1)S(1)}, u32[]{:S(2)}, u32[]{:S(2)}) collective-permute-start(bf16[64,1536]{1,0:T(8,128)(2,1)S(1)} %get-tuple-element.90.a_ref), channel_id=1, source_target_pairs={{0,16},{4,20},{8,24},{12,28},{16,0},{20,4},{24,8},{28,12},{1,17},{... | collective-permute-start | bytes 589832 | tf_op jit(solution)/shard_map/ppermute | solution.py:56
  45.7 1.6 %collective-permute-start.12 = (bf16[64,1536]{1,0:T(8,128)(2,1)S(1)}, bf16[64,1536]{1,0:T(8,128)(2,1)S(1)}, u32[]{:S(2)}, u32[]{:S(2)}) collective-permute-start(bf16[64,1536]{1,0:T(8,128)(2,1)S(1)} %get-tuple-element.90.a_ref), channel_id=1, source_target_pairs={{0,8},{4,12},{8,0},{12,4},{16,24},{20,28},{24,16},{28,20},{1,9},{5... | collective-permute-start | bytes 589832 | tf_op jit(solution)/shard_map/ppermute | solution.py:56
  47.2 0.0 collective-permute-done.9.b_ref
  47.3 1.8 %experts.4 = (f32[64,1536]{1,0:T(8,128)S(1)}, bf16[64,1536]{1,0:T(8,128)(2,1)S(1)}) custom-call(f32[8,64,16]{2,1,0:T(8,128)S(1)} %get-tuple-element.88.bias_ref, bf16[32,1536]{1,0:T(8,128)(2,1)S(1)} %get-tuple-element.89.route_ref, bf16[2,1536,512]{2,1,0:T(8,128)(2,1)S(1)} %copy-done, bf16[2,1536,512]{2,1,0:T(8,128)(2,1)S(1)} %copy-done.1, ...), custom_call_target="tpu_custom_call" | custom-call | flops 1200000000 | tf_op jit(solution)/shard_map/experts/pallas_call | solution.py:648
  49.1 6.5 %collective-permute-done.11.a_ref = bf16[64,1536]{1,0:T(8,128)(2,1)S(1)} collective-permute-done((bf16[64,1536]{1,0:T(8,128)(2,1)S(1)}, bf16[64,1536]{1,0:T(8,128)(2,1)S(1)}, u32[]{:S(2)}, u32[]{:S(2)}) %collective-permute-start.11) | collective-permute-done | bytes 196640 | tf_op jit(solution)/shard_map/ppermute | solution.py:56
  55.6 0.2 collective-permute-done.12.a_ref
  55.7 0.0 collective-permute-start.13
  55.7 0.5 collective-permute-start.16
  56.2 1.4 %collective-permute-start.19 = (bf16[64,1536]{1,0:T(8,128)(2,1)S(1)}, bf16[64,1536]{1,0:T(8,128)(2,1)S(1)}, u32[]{:S(2)}, u32[]{:S(2)}) collective-permute-start(bf16[64,1536]{1,0:T(8,128)(2,1)S(1)} %collective-permute-done.11.a_ref), channel_id=1, source_target_pairs={{0,8},{4,12},{8,0},{12,4},{16,24},{20,28},{24,16},{28,20},{1,9},{5... | collective-permute-start | bytes 589832 | tf_op jit(solution)/shard_map/ppermute | solution.py:56
  57.7 0.0 collective-permute-done.13.b_ref
  57.7 1.8 %experts.5 = (f32[64,1536]{1,0:T(8,128)S(1)}, bf16[64,1536]{1,0:T(8,128)(2,1)S(1)}) custom-call(f32[8,64,16]{2,1,0:T(8,128)S(1)} %get-tuple-element.88.bias_ref, bf16[32,1536]{1,0:T(8,128)(2,1)S(1)} %get-tuple-element.89.route_ref, bf16[2,1536,512]{2,1,0:T(8,128)(2,1)S(1)} %copy-done, bf16[2,1536,512]{2,1,0:T(8,128)(2,1)S(1)} %copy-done.1, ...), custom_call_target="tpu_custom_call" | custom-call | flops 1200000000 | tf_op jit(solution)/shard_map/experts/pallas_call | solution.py:648
  59.5 0.1 collective-permute-start.14
  59.6 0.5 collective-permute-start.10
  60.1 0.0 collective-permute-done.16.b_ref
  60.1 1.8 %experts.6 = (f32[64,1536]{1,0:T(8,128)S(1)}, bf16[64,1536]{1,0:T(8,128)(2,1)S(1)}) custom-call(f32[8,64,16]{2,1,0:T(8,128)S(1)} %get-tuple-element.88.bias_ref, bf16[32,1536]{1,0:T(8,128)(2,1)S(1)} %get-tuple-element.89.route_ref, bf16[2,1536,512]{2,1,0:T(8,128)(2,1)S(1)} %copy-done, bf16[2,1536,512]{2,1,0:T(8,128)(2,1)S(1)} %copy-done.1, ...), custom_call_target="tpu_custom_call" | custom-call | flops 1200000000 | tf_op jit(solution)/shard_map/experts/pallas_call | solution.py:648
  61.9 0.1 collective-permute-start.17
  62.1 1.0 %collective-permute-done.19.a_ref = bf16[64,1536]{1,0:T(8,128)(2,1)S(1)} collective-permute-done((bf16[64,1536]{1,0:T(8,128)(2,1)S(1)}, bf16[64,1536]{1,0:T(8,128)(2,1)S(1)}, u32[]{:S(2)}, u32[]{:S(2)}) %collective-permute-start.19) | collective-permute-done | bytes 196640 | tf_op jit(solution)/shard_map/ppermute | solution.py:56
  63.0 0.0 collective-permute-start.20
  63.0 0.0 collective-permute-done.14
  63.1 2.2 %collective-permute-start.15 = (bf16[64,1536]{1,0:T(8,128)(2,1)S(1)}, bf16[64,1536]{1,0:T(8,128)(2,1)S(1)}, u32[]{:S(2)}, u32[]{:S(2)}) collective-permute-start(bf16[64,1536]{1,0:T(8,128)(2,1)S(1)} %add_convert_fusion.3), channel_id=1, source_target_pairs={{0,16},{4,20},{8,24},{12,28},{16,0},{20,4},{24,8},{28,12},{1,17},{... | collective-permute-start | bytes 589832 | tf_op jit(solution)/shard_map/ppermute | solution.py:56
  65.2 1.8 %experts.7 = (f32[64,1536]{1,0:T(8,128)S(1)}, bf16[64,1536]{1,0:T(8,128)(2,1)S(1)}) custom-call(f32[8,64,16]{2,1,0:T(8,128)S(1)} %get-tuple-element.88.bias_ref, bf16[32,1536]{1,0:T(8,128)(2,1)S(1)} %get-tuple-element.89.route_ref, bf16[2,1536,512]{2,1,0:T(8,128)(2,1)S(1)} %copy-done, bf16[2,1536,512]{2,1,0:T(8,128)(2,1)S(1)} %copy-done.1, ...), custom_call_target="tpu_custom_call" | custom-call | flops 1200000000 | tf_op jit(solution)/shard_map/experts/pallas_call | solution.py:648
  67.1 0.3 collective-permute-start.21
  67.4 0.0 collective-permute-done.17
  67.4 1.8 %collective-permute-start.18 = (bf16[64,1536]{1,0:T(8,128)(2,1)S(1)}, bf16[64,1536]{1,0:T(8,128)(2,1)S(1)}, u32[]{:S(2)}, u32[]{:S(2)}) collective-permute-start(bf16[64,1536]{1,0:T(8,128)(2,1)S(1)} %add_convert_fusion.2), channel_id=1, source_target_pairs={{0,8},{4,12},{8,0},{12,4},{16,24},{20,28},{24,16},{28,20},{1,9},{5... | collective-permute-start | bytes 589832 | tf_op jit(solution)/shard_map/ppermute | solution.py:56
  69.2 0.0 collective-permute-done.21
  69.3 1.9 %collective-permute-start.22 = (bf16[64,1536]{1,0:T(8,128)(2,1)S(1)}, bf16[64,1536]{1,0:T(8,128)(2,1)S(1)}, u32[]{:S(2)}, u32[]{:S(2)}) collective-permute-start(bf16[64,1536]{1,0:T(8,128)(2,1)S(1)} %add_convert_fusion.1), channel_id=1, source_target_pairs={{0,24},{4,28},{8,16},{12,20},{16,8},{20,12},{24,0},{28,4},{1,25},{... | collective-permute-start | bytes 589832 | tf_op jit(solution)/shard_map/ppermute | solution.py:56
  71.2 0.6 accepted.1
  71.8 4.2 %collective-permute-done.15 = bf16[64,1536]{1,0:T(8,128)(2,1)S(1)} collective-permute-done((bf16[64,1536]{1,0:T(8,128)(2,1)S(1)}, bf16[64,1536]{1,0:T(8,128)(2,1)S(1)}, u32[]{:S(2)}, u32[]{:S(2)}) %collective-permute-start.15) | collective-permute-done | bytes 196640 | tf_op jit(solution)/shard_map/ppermute | solution.py:56
  76.0 6.0 %collective-permute-done.18 = bf16[64,1536]{1,0:T(8,128)(2,1)S(1)} collective-permute-done((bf16[64,1536]{1,0:T(8,128)(2,1)S(1)}, bf16[64,1536]{1,0:T(8,128)(2,1)S(1)}, u32[]{:S(2)}, u32[]{:S(2)}) %collective-permute-start.18) | collective-permute-done | bytes 196640 | tf_op jit(solution)/shard_map/ppermute | solution.py:56
  82.0 0.0 collective-permute-done.22
  82.0 0.8 add_convert_fusion
  (13 shorter events, 0.1 us)
Async XLA Ops:
  3.2 9.3 %collective-permute-start.2 = (bf16[72,1536]{1,0:T(8,128)(2,1)S(1)}, bf16[72,1536]{1,0:T(8,128)(2,1)S(1)}, u32[]{:S(2)}, u32[]{:S(2)}) collective-permute-start(bf16[72,1536]{1,0:T(8,128)(2,1)S(1)} %get-tuple-element.52.pay_ref.refs_0_), channel_id=1, source_target_pairs={{0,1},{1,0},{2,3},{3,2},{4,5},{5,4},{6,7},{7,6},{8,9},{9,8},{10,11... | collective-permute-start | bytes 663560 | tf_op jit(solution)/shard_map/ppermute | solution.py:56
  6.2 11.6 %collective-permute-start.1 = (bf16[72,1536]{1,0:T(8,128)(2,1)S(1)}, bf16[72,1536]{1,0:T(8,128)(2,1)S(1)}, u32[]{:S(2)}, u32[]{:S(2)}) collective-permute-start(bf16[72,1536]{1,0:T(8,128)(2,1)S(1)} %get-tuple-element.52.pay_ref.refs_0_), channel_id=1, source_target_pairs={{0,2},{1,3},{2,0},{3,1},{4,6},{5,7},{6,4},{7,5},{8,10},{9,11},{10,... | collective-permute-start | bytes 663560 | tf_op jit(solution)/shard_map/ppermute | solution.py:56
  7.7 11.6 %collective-permute-start = (bf16[72,1536]{1,0:T(8,128)(2,1)S(1)}, bf16[72,1536]{1,0:T(8,128)(2,1)S(1)}, u32[]{:S(2)}, u32[]{:S(2)}) collective-permute-start(bf16[72,1536]{1,0:T(8,128)(2,1)S(1)} %get-tuple-element.52.pay_ref.refs_0_), channel_id=1, source_target_pairs={{0,3},{1,2},{2,1},{3,0},{4,7},{5,6},{6,5},{7,4},{8,11},{9,10},{10,... | collective-permute-start | bytes 663560 | tf_op jit(solution)/shard_map/ppermute | solution.py:56
  17.8 29.4 %copy-start.2 = (bf16[2,512,1536]{2,1,0:T(8,128)(2,1)S(1)}, bf16[2,512,1536]{2,1,0:T(8,128)(2,1)}, u32[]{:S(2)}) copy-start(bf16[2,512,1536]{2,1,0:T(8,128)(2,1)} %wd.7) | copy-start | bytes 9437188
  19.2 11.7 %copy-start.3 = (bf16[384,1536]{1,0:T(8,128)(2,1)S(1)}, bf16[384,1536]{1,0:T(8,128)(2,1)}, u32[]{:S(2)}) copy-start(bf16[384,1536]{1,0:T(8,128)(2,1)} %weight_ref.1) | copy-start | bytes 3538948
  19.3 17.6 %copy-start.5 = (f32[1536]{0:T(1024)S(1)}, f32[1536]{0:T(1024)}, u32[]{:S(2)}) copy-start(f32[1536]{0:T(1024)} %param.24) | copy-start | bytes 18436
  19.3 23.4 %copy-start.4 = (bf16[64,1536]{1,0:T(8,128)(2,1)S(1)}, bf16[64,1536]{1,0:T(8,128)(2,1)}, u32[]{:S(2)}) copy-start(bf16[64,1536]{1,0:T(8,128)(2,1)} %hidden_ref.1) | copy-start | bytes 589828
  19.3 28.0 %copy-start = (bf16[2,1536,512]{2,1,0:T(8,128)(2,1)S(1)}, bf16[2,1536,512]{2,1,0:T(8,128)(2,1)}, u32[]{:S(2)}) copy-start(bf16[2,1536,512]{2,1,0:T(8,128)(2,1)} %wg.7) | copy-start | bytes 9437188
  19.3 28.0 %copy-start.1 = (bf16[2,1536,512]{2,1,0:T(8,128)(2,1)S(1)}, bf16[2,1536,512]{2,1,0:T(8,128)(2,1)}, u32[]{:S(2)}) copy-start(bf16[2,1536,512]{2,1,0:T(8,128)(2,1)} %wu.7) | copy-start | bytes 9437188
  20.8 6.9 %collective-permute-start.3 = (bf16[13,64,128]{2,1,0:T(8,128)(2,1)S(1)}, bf16[13,64,128]{2,1,0:T(8,128)(2,1)S(1)}, u32[]{:S(2)}, u32[]{:S(2)}) collective-permute-start(bf16[13,64,128]{2,1,0:T(8,128)(2,1)S(1)} %get-tuple-element.72), channel_id=1, source_target_pairs={{0,1},{1,0},{2,3},{3,2},{4,5},{5,4},{6,7},{7,6},{8,9},{9,8},{10,11... | collective-permute-start | bytes 638984 | tf_op jit(solution)/shard_map/ppermute | solution.py:56
  20.8 10.1 %collective-permute-start.4 = (bf16[13,64,128]{2,1,0:T(8,128)(2,1)S(1)}, bf16[13,64,128]{2,1,0:T(8,128)(2,1)S(1)}, u32[]{:S(2)}, u32[]{:S(2)}) collective-permute-start(bf16[13,64,128]{2,1,0:T(8,128)(2,1)S(1)} %get-tuple-element.73), channel_id=1, source_target_pairs={{0,2},{1,3},{2,0},{3,1},{4,6},{5,7},{6,4},{7,5},{8,10},{9,11},{10,... | collective-permute-start | bytes 638984 | tf_op jit(solution)/shard_map/ppermute | solution.py:56
  22.9 8.1 %collective-permute-start.5 = (bf16[13,64,128]{2,1,0:T(8,128)(2,1)S(1)}, bf16[13,64,128]{2,1,0:T(8,128)(2,1)S(1)}, u32[]{:S(2)}, u32[]{:S(2)}) collective-permute-start(bf16[13,64,128]{2,1,0:T(8,128)(2,1)S(1)} %get-tuple-element.74), channel_id=1, source_target_pairs={{0,3},{1,2},{2,1},{3,0},{4,7},{5,6},{6,5},{7,4},{8,11},{9,10},{10,... | collective-permute-start | bytes 638984 | tf_op jit(solution)/shard_map/ppermute | solution.py:56
  33.3 5.7 %collective-permute-start.6 = (bf16[64,1536]{1,0:T(8,128)(2,1)S(1)}, bf16[64,1536]{1,0:T(8,128)(2,1)S(1)}, u32[]{:S(2)}, u32[]{:S(2)}) collective-permute-start(bf16[64,1536]{1,0:T(8,128)(2,1)S(1)} %get-tuple-element.84), channel_id=1, source_target_pairs={{0,1},{1,0},{2,3},{3,2},{4,5},{5,4},{6,7},{7,6},{8,9},{9,8},{10,11... | collective-permute-start | bytes 589832 | tf_op jit(solution)/shard_map/ppermute | solution.py:56
  34.0 7.5 %collective-permute-start.7 = (bf16[64,1536]{1,0:T(8,128)(2,1)S(1)}, bf16[64,1536]{1,0:T(8,128)(2,1)S(1)}, u32[]{:S(2)}, u32[]{:S(2)}) collective-permute-start(bf16[64,1536]{1,0:T(8,128)(2,1)S(1)} %get-tuple-element.85), channel_id=1, source_target_pairs={{0,2},{1,3},{2,0},{3,1},{4,6},{5,7},{6,4},{7,5},{8,10},{9,11},{10,... | collective-permute-start | bytes 589832 | tf_op jit(solution)/shard_map/ppermute | solution.py:56
  36.1 6.6 %collective-permute-start.8 = (bf16[64,1536]{1,0:T(8,128)(2,1)S(1)}, bf16[64,1536]{1,0:T(8,128)(2,1)S(1)}, u32[]{:S(2)}, u32[]{:S(2)}) collective-permute-start(bf16[64,1536]{1,0:T(8,128)(2,1)S(1)} %get-tuple-element.86), channel_id=1, source_target_pairs={{0,3},{1,2},{2,1},{3,0},{4,7},{5,6},{6,5},{7,4},{8,11},{9,10},{10,... | collective-permute-start | bytes 589832 | tf_op jit(solution)/shard_map/ppermute | solution.py:56
  42.9 4.3 %collective-permute-start.9 = (bf16[64,1536]{1,0:T(8,128)(2,1)S(1)}, bf16[64,1536]{1,0:T(8,128)(2,1)S(1)}, u32[]{:S(2)}, u32[]{:S(2)}) collective-permute-start(bf16[64,1536]{1,0:T(8,128)(2,1)S(1)} %get-tuple-element.90.a_ref), channel_id=1, source_target_pairs={{0,4},{4,0},{8,12},{12,8},{16,20},{20,16},{24,28},{28,24},{1,5},{5... | collective-permute-start | bytes 589832 | tf_op jit(solution)/shard_map/ppermute | solution.py:56
  43.0 12.5 %collective-permute-start.11 = (bf16[64,1536]{1,0:T(8,128)(2,1)S(1)}, bf16[64,1536]{1,0:T(8,128)(2,1)S(1)}, u32[]{:S(2)}, u32[]{:S(2)}) collective-permute-start(bf16[64,1536]{1,0:T(8,128)(2,1)S(1)} %get-tuple-element.90.a_ref), channel_id=1, source_target_pairs={{0,16},{4,20},{8,24},{12,28},{16,0},{20,4},{24,8},{28,12},{1,17},{... | collective-permute-start | bytes 589832 | tf_op jit(solution)/shard_map/ppermute | solution.py:56
  45.7 10.1 %collective-permute-start.12 = (bf16[64,1536]{1,0:T(8,128)(2,1)S(1)}, bf16[64,1536]{1,0:T(8,128)(2,1)S(1)}, u32[]{:S(2)}, u32[]{:S(2)}) collective-permute-start(bf16[64,1536]{1,0:T(8,128)(2,1)S(1)} %get-tuple-element.90.a_ref), channel_id=1, source_target_pairs={{0,8},{4,12},{8,0},{12,4},{16,24},{20,28},{24,16},{28,20},{1,9},{5... | collective-permute-start | bytes 589832 | tf_op jit(solution)/shard_map/ppermute | solution.py:56
  55.7 2.0 %collective-permute-start.13 = (bf16[64,1536]{1,0:T(8,128)(2,1)S(1)}, bf16[64,1536]{1,0:T(8,128)(2,1)S(1)}, u32[]{:S(2)}, u32[]{:S(2)}) collective-permute-start(bf16[64,1536]{1,0:T(8,128)(2,1)S(1)} %collective-permute-done.11.a_ref), channel_id=1, source_target_pairs={{0,4},{4,0},{8,12},{12,8},{16,20},{20,16},{24,28},{28,24},{1,5},{5... | collective-permute-start | bytes 589832 | tf_op jit(solution)/shard_map/ppermute | solution.py:56
  55.7 4.4 %collective-permute-start.16 = (bf16[64,1536]{1,0:T(8,128)(2,1)S(1)}, bf16[64,1536]{1,0:T(8,128)(2,1)S(1)}, u32[]{:S(2)}, u32[]{:S(2)}) collective-permute-start(bf16[64,1536]{1,0:T(8,128)(2,1)S(1)} %collective-permute-done.12.a_ref), channel_id=1, source_target_pairs={{0,4},{4,0},{8,12},{12,8},{16,20},{20,16},{24,28},{28,24},{1,5},{5... | collective-permute-start | bytes 589832 | tf_op jit(solution)/shard_map/ppermute | solution.py:56
  56.2 6.8 %collective-permute-start.19 = (bf16[64,1536]{1,0:T(8,128)(2,1)S(1)}, bf16[64,1536]{1,0:T(8,128)(2,1)S(1)}, u32[]{:S(2)}, u32[]{:S(2)}) collective-permute-start(bf16[64,1536]{1,0:T(8,128)(2,1)S(1)} %collective-permute-done.11.a_ref), channel_id=1, source_target_pairs={{0,8},{4,12},{8,0},{12,4},{16,24},{20,28},{24,16},{28,20},{1,9},{5... | collective-permute-start | bytes 589832 | tf_op jit(solution)/shard_map/ppermute | solution.py:56
  59.5 3.5 %collective-permute-start.14 = (bf16[64,1536]{1,0:T(8,128)(2,1)S(1)}, bf16[64,1536]{1,0:T(8,128)(2,1)S(1)}, u32[]{:S(2)}, u32[]{:S(2)}) collective-permute-start(bf16[64,1536]{1,0:T(8,128)(2,1)S(1)} %get-tuple-element.95), channel_id=1, source_target_pairs={{0,4},{4,0},{8,12},{12,8},{16,20},{20,16},{24,28},{28,24},{1,5},{5... | collective-permute-start | bytes 589832 | tf_op jit(solution)/shard_map/ppermute | solution.py:56
  59.6 12.3 %collective-permute-start.10 = (bf16[64,1536]{1,0:T(8,128)(2,1)S(1)}, bf16[64,1536]{1,0:T(8,128)(2,1)S(1)}, u32[]{:S(2)}, u32[]{:S(2)}) collective-permute-start(bf16[64,1536]{1,0:T(8,128)(2,1)S(1)} %get-tuple-element.92), channel_id=1, source_target_pairs={{0,4},{4,0},{8,12},{12,8},{16,20},{20,16},{24,28},{28,24},{1,5},{5... | collective-permute-start | bytes 589832 | tf_op jit(solution)/shard_map/ppermute | solution.py:56
  61.9 5.5 %collective-permute-start.17 = (bf16[64,1536]{1,0:T(8,128)(2,1)S(1)}, bf16[64,1536]{1,0:T(8,128)(2,1)S(1)}, u32[]{:S(2)}, u32[]{:S(2)}) collective-permute-start(bf16[64,1536]{1,0:T(8,128)(2,1)S(1)} %get-tuple-element.98), channel_id=1, source_target_pairs={{0,4},{4,0},{8,12},{12,8},{16,20},{20,16},{24,28},{28,24},{1,5},{5... | collective-permute-start | bytes 589832 | tf_op jit(solution)/shard_map/ppermute | solution.py:56
  63.0 2.2 %collective-permute-start.20 = (bf16[64,1536]{1,0:T(8,128)(2,1)S(1)}, bf16[64,1536]{1,0:T(8,128)(2,1)S(1)}, u32[]{:S(2)}, u32[]{:S(2)}) collective-permute-start(bf16[64,1536]{1,0:T(8,128)(2,1)S(1)} %collective-permute-done.19.a_ref), channel_id=1, source_target_pairs={{0,4},{4,0},{8,12},{12,8},{16,20},{20,16},{24,28},{28,24},{1,5},{5... | collective-permute-start | bytes 589832 | tf_op jit(solution)/shard_map/ppermute | solution.py:56
  63.1 12.9 %collective-permute-start.15 = (bf16[64,1536]{1,0:T(8,128)(2,1)S(1)}, bf16[64,1536]{1,0:T(8,128)(2,1)S(1)}, u32[]{:S(2)}, u32[]{:S(2)}) collective-permute-start(bf16[64,1536]{1,0:T(8,128)(2,1)S(1)} %add_convert_fusion.3), channel_id=1, source_target_pairs={{0,16},{4,20},{8,24},{12,28},{16,0},{20,4},{24,8},{28,12},{1,17},{... | collective-permute-start | bytes 589832 | tf_op jit(solution)/shard_map/ppermute | solution.py:56
  67.1 2.2 %collective-permute-start.21 = (bf16[64,1536]{1,0:T(8,128)(2,1)S(1)}, bf16[64,1536]{1,0:T(8,128)(2,1)S(1)}, u32[]{:S(2)}, u32[]{:S(2)}) collective-permute-start(bf16[64,1536]{1,0:T(8,128)(2,1)S(1)} %get-tuple-element.101), channel_id=1, source_target_pairs={{0,4},{4,0},{8,12},{12,8},{16,20},{20,16},{24,28},{28,24},{1,5},{5... | collective-permute-start | bytes 589832 | tf_op jit(solution)/shard_map/ppermute | solution.py:56
  67.4 14.6 %collective-permute-start.18 = (bf16[64,1536]{1,0:T(8,128)(2,1)S(1)}, bf16[64,1536]{1,0:T(8,128)(2,1)S(1)}, u32[]{:S(2)}, u32[]{:S(2)}) collective-permute-start(bf16[64,1536]{1,0:T(8,128)(2,1)S(1)} %add_convert_fusion.2), channel_id=1, source_target_pairs={{0,8},{4,12},{8,0},{12,4},{16,24},{20,28},{24,16},{28,20},{1,9},{5... | collective-permute-start | bytes 589832 | tf_op jit(solution)/shard_map/ppermute | solution.py:56
  69.3 12.7 %collective-permute-start.22 = (bf16[64,1536]{1,0:T(8,128)(2,1)S(1)}, bf16[64,1536]{1,0:T(8,128)(2,1)S(1)}, u32[]{:S(2)}, u32[]{:S(2)}) collective-permute-start(bf16[64,1536]{1,0:T(8,128)(2,1)S(1)} %add_convert_fusion.1), channel_id=1, source_target_pairs={{0,24},{4,28},{8,16},{12,20},{16,8},{20,12},{24,0},{28,4},{1,25},{... | collective-permute-start | bytes 589832 | tf_op jit(solution)/shard_map/ppermute | solution.py:56

commit v5 on v4

--- a/solution.py
+++ b/solution.py
@@ -62,7 +62,7 @@
 
 def prelude_kernel(
     len_hbm, path_hbm, par_hbm, q_hbm, kv_hbm, cache_hbm,
-    pay_ref, key_ref, val_ref, anc_ref, pos_ref, lim_ref, packed_ref,
+    pay_ref, key_ref, val_ref, anc_ref, pos_ref, lim_ref, packed_ref, pick_ref,
     len_ref, path_ref, par_ref, q_ref, kv_ref, kv_f, anc_all, sems,
 ):
     copies = [
@@ -136,11 +136,7 @@
         val_ref[:, b * LANES : (b + 1) * LANES] = vals[b]
     copies[4].wait()
     packed = jnp.concatenate(keys + vals, axis=1)
-    picked = jnp.dot(chooser, packed, preferred_element_type=F32).astype(BF)
-    pay_ref[n:, : packed.shape[1]] = picked
-    pay_ref[n:, packed.shape[1] :] = jnp.zeros(
-        (path_ref.shape[1], pay_ref.shape[1] - packed.shape[1]), BF
-    )
+    pick_ref[...] = jnp.dot(chooser, packed, preferred_element_type=F32).astype(BF)
     for b in range(PAIRS):
         x0, x1, x2 = [
             turned(q_ref[:, (GROUPS * b + i) * LANES : (GROUPS * b + i + 1) * LANES].astype(F32))
@@ -150,7 +146,7 @@
         y1 = jnp.where(low, pltpu.roll(x0, HD, axis=1), pltpu.roll(x2, HD, axis=1))
         y2 = jnp.where(low, x1, x2)
         for i, y in enumerate((y0, y1, y2)):
-            pay_ref[:n, (GROUPS * b + i) * LANES : (GROUPS * b + i + 1) * LANES] = y.astype(BF)
+            pay_ref[:, (GROUPS * b + i) * LANES : (GROUPS * b + i + 1) * LANES] = y.astype(BF)
     copies[5].wait()
 
 
@@ -161,16 +157,17 @@
     return pl.pallas_call(
         prelude_kernel,
         out_shape=(
-            jax.ShapeDtypeStruct((n + path.shape[1], width), BF),
+            jax.ShapeDtypeStruct((n, width), BF),
             jax.ShapeDtypeStruct((n, kv_width), BF),
             jax.ShapeDtypeStruct((n, kv_width), BF),
             jax.ShapeDtypeStruct((draft, draft), F32),
             jax.ShapeDtypeStruct((requests * draft, LANES), F32),
             jax.ShapeDtypeStruct((requests, 8, LANES), F32),
             jax.ShapeDtypeStruct(cache.shape, BF),
+            jax.ShapeDtypeStruct((path.shape[1], 2 * kv_width), BF),
         ),
         in_specs=[in_hbm()] * 6,
-        out_specs=(whole(),) * 7,
+        out_specs=(whole(),) * 8,
         scratch_shapes=[
             pltpu.SMEM(cache_len.shape, jnp.int32),
             pltpu.SMEM(path.shape, jnp.int32),
@@ -659,29 +656,26 @@
     )(bias, route, w_gate, w_up, w_down, a, b)
 
 
-def accepted_kernel(count, n, *refs):
-    out_ref = refs[count]
-    requests = out_ref.shape[0]
+def accepted_kernel(n, picks_ref, out_ref):
+    requests, entries, _ = out_ref.shape
+    count = picks_ref.shape[0] // entries
     draft = count * n // requests
     out_ref[...] = jnp.zeros(out_ref.shape, out_ref.dtype)
     for k in range(count):
         request = (lax.axis_index("tensor") ^ k) * n // draft
-        out_ref[request] = out_ref[request] + refs[k][:, : out_ref.shape[2]]
-
-
-def accepted(payloads, requests, entries, n):
-    count = len(payloads)
-    block = pl.BlockSpec((entries, payloads[0].shape[1]), lambda i: (n // entries, 0))
-    return pl.pallas_call(
-        functools.partial(accepted_kernel, count, n),
-        out_shape=jax.ShapeDtypeStruct((requests, entries, 2 * KVH * HD), BF),
-        grid=(1,),
-        in_specs=[block] * count,
-        out_specs=pl.BlockSpec((requests, entries, 2 * KVH * HD), lambda i: (0, 0, 0)),
+        out_ref[request] = out_ref[request] + picks_ref[k * entries : (k + 1) * entries, :]
+
+
+def accepted(picks, requests, entries, n):
+    return pl.pallas_call(
+        functools.partial(accepted_kernel, n),
+        out_shape=jax.ShapeDtypeStruct((requests, entries, picks.shape[1]), BF),
+        in_specs=[whole()],
+        out_specs=whole(),
         compiler_params=params(4),
         cost_estimate=cost(1e6),
         name="accepted",
-    )(*payloads)
+    )(picks)
 
 
 def rows_by_lane_block(kv):
@@ -698,7 +692,7 @@
     data = lax.axis_size("dp")
     n = queries.shape[0]
     requests, draft = parents.shape
-    payload, keys, vals, ancestry, pos, limit, packed = prelude(
+    payload, keys, vals, ancestry, pos, limit, packed, picks = prelude(
         cache_len,
         path,
         parents,
@@ -738,7 +732,6 @@
             pieces += [piece, exchange(piece, "dp", data, 1)]
         mixed, normed = join(parts, pieces, hidden_in, gain)
         bias, route = routing(*tables)
-    compacted = accepted(payloads, requests, path.shape[1], n)
 
     steps = data // CORES
     lines = {0: normed}
@@ -759,10 +752,18 @@
         twin = exchange(line, "dp", data, 1)
         own, other = experts_part(k, bias, route, w_gate, w_up, w_down, line, twin)
         last = own
+        if k == 1:
+            picks = lax.optimization_barrier((picks, own))[0]
         chip = own + exchange(other, "dp", data, 1).astype(F32)
         if k:
-            chip = exchange(chip.astype(BF), "dp", data, CORES * k).astype(F32)
+            chip = chip.astype(BF)
+            chip = exchange(chip, "dp", data, CORES * k).astype(F32)
         total = total + chip
+    reach = 1
+    while reach < tensor:
+        picks = jnp.concatenate([picks, exchange(picks, "tensor", tensor, reach)], axis=0)
+        reach *= 2
+    compacted = accepted(picks, requests, path.shape[1], n)
     return total.astype(BF), compacted
 
 

time: 83.3 us -> 82.3 us (0.988)
  waiting for transfers between devices: 33.2 us -> 30.8 us
  starting transfers between devices: 24.8 us -> 26.5 us
    ppermute x23 -> x25, waiting for transfers between devices: 33.2 us -> 30.8 us  [exchange(): return lax.ppermute(x, axis, [(i, i ^ step) for i in range(size)])]
    ppermute x23 -> x25, starting transfers between devices: 24.8 us -> 26.5 us  [exchange(): return lax.ppermute(x, axis, [(i, i ^ step) for i in range(size)])]
  transfers between devices with their start and end apart: 23 -> 25, of which waited for: 12 -> 12; matrix products, arithmetic and copies ran while one was open for 0% -> 0% of each run, Pallas kernels for 20% -> 20%
where the time goes in v5:
time: 82.3 us; the launch traced here: 82.1 us
  waiting for transfers between devices  30.8 us (37%)
  starting transfers between devices  26.5 us (32%)
  Pallas kernels  22.9 us (28%)
  other arithmetic  0.92 us (1%)
  between operations  0.86 us (1%)
    ppermute x25, waiting for transfers between devices, exchange(): return lax.ppermute(x, axis, [(i, i ^ step) for i in range(size)])  30.8 us
    ppermute x25, starting transfers between devices, exchange(): return lax.ppermute(x, axis, [(i, i ^ step) for i in range(size)])  26.5 us
    pallas_call x4, Pallas kernels, experts_part(): pl.pallas_call(functools.partial(experts_kernel, step), out_shape=(jax.Sh...  7.29 us
    pallas_call x4, Pallas kernels, attend_split(): pl.pallas_call(functools.partial(attend_split_kernel, step, step == 0, co...  6.41 us
    pallas_call x1, Pallas kernels, prelude(): pl.pallas_call(prelude_kernel, out_shape=(jax.ShapeDtypeStruct((n, width)...  2.52 us
    pallas_call x1, Pallas kernels, unpack(): pl.pallas_call(unpack_kernel, out_shape=jax.ShapeDtypeStruct((requests, 2...  2.37 us
    pallas_call x1, Pallas kernels, join_split(): pl.pallas_call(functools.partial(join_split_kernel, count), out_shape=tup...  2.34 us
  transfers between devices with their start and end apart: 25, of which 12 were waited for; matrix products, arithmetic and copies ran while one was open for 0% of the time, Pallas kernels for 20%

profile of v5, /device:TPU:0, one launch (start us, length us, event | category | flops | bytes accessed | tf_op | source)
XLA Modules:
  0.0 82.1 jit_solution(9467819347415264902)
XLA Ops:
  0.6 2.5 %prelude.1 = (bf16[64,1536]{1,0:T(8,128)(2,1)S(1)}, bf16[64,512]{1,0:T(8,128)(2,1)S(1)}, bf16[64,512]{1,0:T(8,128)(2,1)S(1)}, f32[64,64]{1,0:T(8,128)S(1)}, f32[...) custom-call(s32[4]{0:T(128)} %len_hbm.1, ...), custom_call_target="tpu_custom_call" | custom-call | flops 10000000 | tf_op jit(solution)/shard_map/prelude/pallas_call | solution.py:157
  3.2 3.0 %collective-permute-start.2 = (bf16[64,1536]{1,0:T(8,128)(2,1)S(1)}, bf16[64,1536]{1,0:T(8,128)(2,1)S(1)}, u32[]{:S(2)}, u32[]{:S(2)}) collective-permute-start(bf16[64,1536]{1,0:T(8,128)(2,1)S(1)} %get-tuple-element.54.pay_ref), channel_id=1, source_target_pairs={{0,1},{1,0},{2,3},{3,2},{4,5},{5,4},{6,7},{7,6},{8,9},{9,8},{10,11... | collective-permute-start | bytes 589832 | tf_op jit(solution)/shard_map/ppermute | solution.py:56
  6.2 1.5 %collective-permute-start.1 = (bf16[64,1536]{1,0:T(8,128)(2,1)S(1)}, bf16[64,1536]{1,0:T(8,128)(2,1)S(1)}, u32[]{:S(2)}, u32[]{:S(2)}) collective-permute-start(bf16[64,1536]{1,0:T(8,128)(2,1)S(1)} %get-tuple-element.54.pay_ref), channel_id=1, source_target_pairs={{0,2},{1,3},{2,0},{3,1},{4,6},{5,7},{6,4},{7,5},{8,10},{9,11},{10,... | collective-permute-start | bytes 589832 | tf_op jit(solution)/shard_map/ppermute | solution.py:56
  7.7 0.0 collective-permute-start
  7.7 2.4 %unpack.1.kv_ref = bf16[4,8,512,128]{3,2,1,0:T(8,128)(2,1)S(1)} custom-call(bf16[4,4096,128]{2,1,0:T(8,128)(2,1)S(1)} %get-tuple-element.55.packed_ref), custom_call_target="tpu_custom_call" | custom-call | flops 100000000 | tf_op jit(solution)/shard_map/unpack/pallas_call | solution.py:197
  10.1 2.2 %attend.4 = (bf16[13,64,128]{2,1,0:T(8,128)(2,1)S(1)}, bf16[13,64,128]{2,1,0:T(8,128)(2,1)S(1)}, bf16[13,64,128]{2,1,0:T(8,128)(2,1)S(1)}, bf16[13,64,128]{2,1,0:T(8,128)(2,1)S(1)}) custom-call(bf16[64,1536]{1,0:T(8,128)(2,1)S(1)} %get-tuple-element.54.pay_ref, bf16[4,8,512,128]{3,2,1,0:T(8,128)(2,1)S(1)} %unpack.1.kv_ref, ...), custom_call_target="tpu_custom_call" | custom-call | flops 400000000 | tf_op jit(solution)/shard_map/attend/pallas_call | solution.py:434
  12.3 0.0 collective-permute-done.2.pay_ref
  12.3 1.4 %attend.5 = (bf16[13,64,128]{2,1,0:T(8,128)(2,1)S(1)}, bf16[13,64,128]{2,1,0:T(8,128)(2,1)S(1)}, bf16[13,64,128]{2,1,0:T(8,128)(2,1)S(1)}, bf16[13,64,128]{2,1,0:T(8,128)(2,1)S(1)}) custom-call(bf16[64,1536]{1,0:T(8,128)(2,1)S(1)} %collective-permute-done.2.pay_ref, ...), custom_call_target="tpu_custom_call", output_to_operand_aliasing={{0}: (7, {}), {1}: (8, {}), {2}: (9, {}), {3}: (10, {})} | custom-call | flops 400000000 | tf_op jit(solution)/shard_map/attend/pallas_call | solution.py:434
  13.7 3.0 %collective-permute-done.1.pay_ref = bf16[64,1536]{1,0:T(8,128)(2,1)S(1)} collective-permute-done((bf16[64,1536]{1,0:T(8,128)(2,1)S(1)}, bf16[64,1536]{1,0:T(8,128)(2,1)S(1)}, u32[]{:S(2)}, u32[]{:S(2)}) %collective-permute-start.1) | collective-permute-done | bytes 196640 | tf_op jit(solution)/shard_map/ppermute | solution.py:56
  16.7 1.4 %attend.6 = (bf16[13,64,128]{2,1,0:T(8,128)(2,1)S(1)}, bf16[13,64,128]{2,1,0:T(8,128)(2,1)S(1)}, bf16[13,64,128]{2,1,0:T(8,128)(2,1)S(1)}, bf16[13,64,128]{2,1,0:T(8,128)(2,1)S(1)}) custom-call(bf16[64,1536]{1,0:T(8,128)(2,1)S(1)} %collective-permute-done.1.pay_ref, ...), custom_call_target="tpu_custom_call", output_to_operand_aliasing={{0}: (7, {}), {1}: (8, {}), {2}: (9, {}), {3}: (10, {})} | custom-call | flops 400000000 | tf_op jit(solution)/shard_map/attend/pallas_call | solution.py:434
  18.1 0.0 copy-start.3
  18.2 0.0 collective-permute-done.pay_ref
  18.2 0.0 copy-start.5
  18.2 0.0 copy-start.4
  18.2 0.0 copy-start
  18.2 0.0 copy-start.1
  18.2 1.4 %attend.7 = (bf16[13,64,128]{2,1,0:T(8,128)(2,1)S(1)}, bf16[13,64,128]{2,1,0:T(8,128)(2,1)S(1)}, bf16[13,64,128]{2,1,0:T(8,128)(2,1)S(1)}, bf16[13,64,128]{2,1,0:T(8,128)(2,1)S(1)}) custom-call(bf16[64,1536]{1,0:T(8,128)(2,1)S(1)} %collective-permute-done.pay_ref, ...), custom_call_target="tpu_custom_call", output_to_operand_aliasing={{0}: (7, {}), {1}: (8, {}), {2}: (9, {}), {3}: (10, {})} | custom-call | flops 400000000 | tf_op jit(solution)/shard_map/attend/pallas_call | solution.py:434
  19.6 0.1 collective-permute-start.3
  19.7 2.0 %collective-permute-start.4 = (bf16[13,64,128]{2,1,0:T(8,128)(2,1)S(1)}, bf16[13,64,128]{2,1,0:T(8,128)(2,1)S(1)}, u32[]{:S(2)}, u32[]{:S(2)}) collective-permute-start(bf16[13,64,128]{2,1,0:T(8,128)(2,1)S(1)} %get-tuple-element.75), channel_id=1, source_target_pairs={{0,2},{1,3},{2,0},{3,1},{4,6},{5,7},{6,4},{7,5},{8,10},{9,11},{10,... | collective-permute-start | bytes 638984 | tf_op jit(solution)/shard_map/ppermute | solution.py:56
  21.7 1.4 %collective-permute-start.5 = (bf16[13,64,128]{2,1,0:T(8,128)(2,1)S(1)}, bf16[13,64,128]{2,1,0:T(8,128)(2,1)S(1)}, u32[]{:S(2)}, u32[]{:S(2)}) collective-permute-start(bf16[13,64,128]{2,1,0:T(8,128)(2,1)S(1)} %get-tuple-element.76), channel_id=1, source_target_pairs={{0,3},{1,2},{2,1},{3,0},{4,7},{5,6},{6,5},{7,4},{8,11},{9,10},{10,... | collective-permute-start | bytes 638984 | tf_op jit(solution)/shard_map/ppermute | solution.py:56
  23.2 1.1 %routing.1 = (f32[8,64,16]{2,1,0:T(8,128)S(1)}, bf16[32,1536]{1,0:T(8,128)(2,1)S(1)}) custom-call(s32[8,8,64]{2,1,0:T(8,128)} %bitcast.15, f32[16,1536]{1,0:T(8,128)} %bitcast.14), custom_call_target="tpu_custom_call" | custom-call | flops 1000000 | tf_op jit(solution)/shard_map/routing/pallas_call | solution.py:237
  24.3 2.3 %collective-permute-done.3.refs_1_ = bf16[13,64,128]{2,1,0:T(8,128)(2,1)S(1)} collective-permute-done((bf16[13,64,128]{2,1,0:T(8,128)(2,1)S(1)}, bf16[13,64,128]{2,1,0:T(8,128)(2,1)S(1)}, u32[]{:S(2)}, u32[]{:S(2)}) %collective-permute-start.3) | collective-permute-done | bytes 213024 | tf_op jit(solution)/shard_map/ppermute | solution.py:56
  26.5 3.3 %collective-permute-done.4.refs_2_ = bf16[13,64,128]{2,1,0:T(8,128)(2,1)S(1)} collective-permute-done((bf16[13,64,128]{2,1,0:T(8,128)(2,1)S(1)}, bf16[13,64,128]{2,1,0:T(8,128)(2,1)S(1)}, u32[]{:S(2)}, u32[]{:S(2)}) %collective-permute-start.4) | collective-permute-done | bytes 213024 | tf_op jit(solution)/shard_map/ppermute | solution.py:56
  29.9 0.0 collective-permute-done.5.refs_3_
  29.9 2.3 %join.1 = (f32[64,1536]{1,0:T(8,128)S(1)}, bf16[64,1536]{1,0:T(8,128)(2,1)S(1)}, bf16[64,1536]{1,0:T(8,128)(2,1)S(1)}, bf16[64,1536]{1,0:T(8,128)(2,1)S(1)}) custom-call(bf16[384,1536]{1,0:T(8,128)(2,1)S(1)} %copy-done.3, bf16[13,64,128]{2,1,0:T(8,128)(2,1)S(1)} %get-tuple-element.81.refs_0_, bf16[13,64,128]{2,1,0:T(8,128)(2,1)S(1)} %collective-permute-done.3.refs_1_, ...), custom_call_target="tpu_custom_call" | custom-call | flops 400000000 | tf_op jit(solution)/shard_map/join/pallas_call | solution.py:490
  32.2 0.8 collective-permute-start.6
  33.0 2.1 %collective-permute-start.7 = (bf16[64,1536]{1,0:T(8,128)(2,1)S(1)}, bf16[64,1536]{1,0:T(8,128)(2,1)S(1)}, u32[]{:S(2)}, u32[]{:S(2)}) collective-permute-start(bf16[64,1536]{1,0:T(8,128)(2,1)S(1)} %get-tuple-element.87), channel_id=1, source_target_pairs={{0,2},{1,3},{2,0},{3,1},{4,6},{5,7},{6,4},{7,5},{8,10},{9,11},{10,... | collective-permute-start | bytes 589832 | tf_op jit(solution)/shard_map/ppermute | solution.py:56
  35.1 0.7 collective-permute-start.8
  35.8 2.2 %collective-permute-done.6.refs_0_ = bf16[64,1536]{1,0:T(8,128)(2,1)S(1)} collective-permute-done((bf16[64,1536]{1,0:T(8,128)(2,1)S(1)}, bf16[64,1536]{1,0:T(8,128)(2,1)S(1)}, u32[]{:S(2)}, u32[]{:S(2)}) %collective-permute-start.6) | collective-permute-done | bytes 196640 | tf_op jit(solution)/shard_map/ppermute | solution.py:56
  38.0 2.4 %collective-permute-done.7.refs_1_ = bf16[64,1536]{1,0:T(8,128)(2,1)S(1)} collective-permute-done((bf16[64,1536]{1,0:T(8,128)(2,1)S(1)}, bf16[64,1536]{1,0:T(8,128)(2,1)S(1)}, u32[]{:S(2)}, u32[]{:S(2)}) %collective-permute-start.7) | collective-permute-done | bytes 196640 | tf_op jit(solution)/shard_map/ppermute | solution.py:56
  40.4 1.3 %collective-permute-done.8.refs_2_ = bf16[64,1536]{1,0:T(8,128)(2,1)S(1)} collective-permute-done((bf16[64,1536]{1,0:T(8,128)(2,1)S(1)}, bf16[64,1536]{1,0:T(8,128)(2,1)S(1)}, u32[]{:S(2)}, u32[]{:S(2)}) %collective-permute-start.8) | collective-permute-done | bytes 196640 | tf_op jit(solution)/shard_map/ppermute | solution.py:56
  41.6 0.2 norm.1
  41.9 0.1 collective-permute-start.9
  41.9 2.6 %collective-permute-start.11 = (bf16[64,1536]{1,0:T(8,128)(2,1)S(1)}, bf16[64,1536]{1,0:T(8,128)(2,1)S(1)}, u32[]{:S(2)}, u32[]{:S(2)}) collective-permute-start(bf16[64,1536]{1,0:T(8,128)(2,1)S(1)} %get-tuple-element.92.a_ref), channel_id=1, source_target_pairs={{0,16},{4,20},{8,24},{12,28},{16,0},{20,4},{24,8},{28,12},{1,17},{... | collective-permute-start | bytes 589832 | tf_op jit(solution)/shard_map/ppermute | solution.py:56
  44.6 1.6 %collective-permute-start.12 = (bf16[64,1536]{1,0:T(8,128)(2,1)S(1)}, bf16[64,1536]{1,0:T(8,128)(2,1)S(1)}, u32[]{:S(2)}, u32[]{:S(2)}) collective-permute-start(bf16[64,1536]{1,0:T(8,128)(2,1)S(1)} %get-tuple-element.92.a_ref), channel_id=1, source_target_pairs={{0,8},{4,12},{8,0},{12,4},{16,24},{20,28},{24,16},{28,20},{1,9},{5... | collective-permute-start | bytes 589832 | tf_op jit(solution)/shard_map/ppermute | solution.py:56
  46.2 0.0 collective-permute-done.9.b_ref
  46.2 1.8 %experts.4 = (f32[64,1536]{1,0:T(8,128)S(1)}, bf16[64,1536]{1,0:T(8,128)(2,1)S(1)}) custom-call(f32[8,64,16]{2,1,0:T(8,128)S(1)} %get-tuple-element.90.bias_ref, bf16[32,1536]{1,0:T(8,128)(2,1)S(1)} %get-tuple-element.91.route_ref, bf16[2,1536,512]{2,1,0:T(8,128)(2,1)S(1)} %copy-done, bf16[2,1536,512]{2,1,0:T(8,128)(2,1)S(1)} %copy-done.1, ...), custom_call_target="tpu_custom_call" | custom-call | flops 1200000000 | tf_op jit(solution)/shard_map/experts/pallas_call | solution.py:645
  48.0 6.5 %collective-permute-done.11.a_ref = bf16[64,1536]{1,0:T(8,128)(2,1)S(1)} collective-permute-done((bf16[64,1536]{1,0:T(8,128)(2,1)S(1)}, bf16[64,1536]{1,0:T(8,128)(2,1)S(1)}, u32[]{:S(2)}, u32[]{:S(2)}) %collective-permute-start.11) | collective-permute-done | bytes 196640 | tf_op jit(solution)/shard_map/ppermute | solution.py:56
  54.5 0.2 collective-permute-done.12.a_ref
  54.6 0.0 collective-permute-start.13
  54.7 0.5 collective-permute-start.16
  55.2 1.4 %collective-permute-start.19 = (bf16[64,1536]{1,0:T(8,128)(2,1)S(1)}, bf16[64,1536]{1,0:T(8,128)(2,1)S(1)}, u32[]{:S(2)}, u32[]{:S(2)}) collective-permute-start(bf16[64,1536]{1,0:T(8,128)(2,1)S(1)} %collective-permute-done.11.a_ref), channel_id=1, source_target_pairs={{0,8},{4,12},{8,0},{12,4},{16,24},{20,28},{24,16},{28,20},{1,9},{5... | collective-permute-start | bytes 589832 | tf_op jit(solution)/shard_map/ppermute | solution.py:56
  56.6 0.0 collective-permute-done.13.b_ref
  56.6 1.8 %experts.5 = (f32[64,1536]{1,0:T(8,128)S(1)}, bf16[64,1536]{1,0:T(8,128)(2,1)S(1)}) custom-call(f32[8,64,16]{2,1,0:T(8,128)S(1)} %get-tuple-element.90.bias_ref, bf16[32,1536]{1,0:T(8,128)(2,1)S(1)} %get-tuple-element.91.route_ref, bf16[2,1536,512]{2,1,0:T(8,128)(2,1)S(1)} %copy-done, bf16[2,1536,512]{2,1,0:T(8,128)(2,1)S(1)} %copy-done.1, ...), custom_call_target="tpu_custom_call" | custom-call | flops 1200000000 | tf_op jit(solution)/shard_map/experts/pallas_call | solution.py:645
  58.4 0.1 collective-permute-start.14
  58.5 0.5 collective-permute-start.10
  59.0 1.8 %experts.6 = (f32[64,1536]{1,0:T(8,128)S(1)}, bf16[64,1536]{1,0:T(8,128)(2,1)S(1)}) custom-call(f32[8,64,16]{2,1,0:T(8,128)S(1)} %get-tuple-element.90.bias_ref, bf16[32,1536]{1,0:T(8,128)(2,1)S(1)} %get-tuple-element.91.route_ref, bf16[2,1536,512]{2,1,0:T(8,128)(2,1)S(1)} %copy-done, bf16[2,1536,512]{2,1,0:T(8,128)(2,1)S(1)} %copy-done.1, ...), custom_call_target="tpu_custom_call" | custom-call | flops 1200000000 | tf_op jit(solution)/shard_map/experts/pallas_call | solution.py:645
  60.8 0.7 collective-permute-start.23
  61.5 0.4 collective-permute-done.19.a_ref
  62.0 0.1 collective-permute-start.20
  62.1 0.0 collective-permute-done.14
  62.1 2.4 %collective-permute-start.15 = (bf16[64,1536]{1,0:T(8,128)(2,1)S(1)}, bf16[64,1536]{1,0:T(8,128)(2,1)S(1)}, u32[]{:S(2)}, u32[]{:S(2)}) collective-permute-start(bf16[64,1536]{1,0:T(8,128)(2,1)S(1)} %add_convert_fusion.3), channel_id=1, source_target_pairs={{0,16},{4,20},{8,24},{12,28},{16,0},{20,4},{24,8},{28,12},{1,17},{... | collective-permute-start | bytes 589832 | tf_op jit(solution)/shard_map/ppermute | solution.py:56
  64.5 1.8 %experts.7 = (f32[64,1536]{1,0:T(8,128)S(1)}, bf16[64,1536]{1,0:T(8,128)(2,1)S(1)}) custom-call(f32[8,64,16]{2,1,0:T(8,128)S(1)} %get-tuple-element.90.bias_ref, bf16[32,1536]{1,0:T(8,128)(2,1)S(1)} %get-tuple-element.91.route_ref, bf16[2,1536,512]{2,1,0:T(8,128)(2,1)S(1)} %copy-done, bf16[2,1536,512]{2,1,0:T(8,128)(2,1)S(1)} %copy-done.1, ...), custom_call_target="tpu_custom_call" | custom-call | flops 1200000000 | tf_op jit(solution)/shard_map/experts/pallas_call | solution.py:645
  66.3 0.1 collective-permute-start.21
  66.4 0.0 collective-permute-done.17
  66.5 1.7 %collective-permute-start.18 = (bf16[64,1536]{1,0:T(8,128)(2,1)S(1)}, bf16[64,1536]{1,0:T(8,128)(2,1)S(1)}, u32[]{:S(2)}, u32[]{:S(2)}) collective-permute-start(bf16[64,1536]{1,0:T(8,128)(2,1)S(1)} %add_convert_fusion.2), channel_id=1, source_target_pairs={{0,8},{4,12},{8,0},{12,4},{16,24},{20,28},{24,16},{28,20},{1,9},{5... | collective-permute-start | bytes 589832 | tf_op jit(solution)/shard_map/ppermute | solution.py:56
  68.2 1.9 %collective-permute-start.22 = (bf16[64,1536]{1,0:T(8,128)(2,1)S(1)}, bf16[64,1536]{1,0:T(8,128)(2,1)S(1)}, u32[]{:S(2)}, u32[]{:S(2)}) collective-permute-start(bf16[64,1536]{1,0:T(8,128)(2,1)S(1)} %add_convert_fusion.1), channel_id=1, source_target_pairs={{0,24},{4,28},{8,16},{12,20},{16,8},{20,12},{24,0},{28,4},{1,25},{... | collective-permute-start | bytes 589832 | tf_op jit(solution)/shard_map/ppermute | solution.py:56
  70.1 1.2 %collective-permute-start.24 = (bf16[16,1024]{1,0:T(8,128)(2,1)S(1)}, bf16[16,1024]{1,0:T(8,128)(2,1)S(1)}, u32[]{:S(2)}, u32[]{:S(2)}) collective-permute-start(bf16[16,1024]{1,0:T(8,128)(2,1)S(1)} %pad_maximum_fusion.1), channel_id=1, source_target_pairs={{0,2},{1,3},{2,0},{3,1},{4,6},{5,7},{6,4},{7,5},{8,10},{9,11},{10,... | collective-permute-start | bytes 98312 | tf_op jit(solution)/shard_map/ppermute | solution.py:56
  71.3 2.7 %collective-permute-done.24 = bf16[16,1024]{1,0:T(8,128)(2,1)S(1)} collective-permute-done((bf16[16,1024]{1,0:T(8,128)(2,1)S(1)}, bf16[16,1024]{1,0:T(8,128)(2,1)S(1)}, u32[]{:S(2)}, u32[]{:S(2)}) %collective-permute-start.24) | collective-permute-done | bytes 32800 | tf_op jit(solution)/shard_map/ppermute | solution.py:56
  74.0 0.7 accepted.1
  74.7 0.0 collective-permute-done.10
  74.7 0.3 collective-permute-done.15
  75.0 6.2 %collective-permute-done.18 = bf16[64,1536]{1,0:T(8,128)(2,1)S(1)} collective-permute-done((bf16[64,1536]{1,0:T(8,128)(2,1)S(1)}, bf16[64,1536]{1,0:T(8,128)(2,1)S(1)}, u32[]{:S(2)}, u32[]{:S(2)}) %collective-permute-start.18) | collective-permute-done | bytes 196640 | tf_op jit(solution)/shard_map/ppermute | solution.py:56
  81.3 0.8 add_convert_fusion
  (19 shorter events, 0.1 us)
Async XLA Ops:
  3.2 9.1 %collective-permute-start.2 = (bf16[64,1536]{1,0:T(8,128)(2,1)S(1)}, bf16[64,1536]{1,0:T(8,128)(2,1)S(1)}, u32[]{:S(2)}, u32[]{:S(2)}) collective-permute-start(bf16[64,1536]{1,0:T(8,128)(2,1)S(1)} %get-tuple-element.54.pay_ref), channel_id=1, source_target_pairs={{0,1},{1,0},{2,3},{3,2},{4,5},{5,4},{6,7},{7,6},{8,9},{9,8},{10,11... | collective-permute-start | bytes 589832 | tf_op jit(solution)/shard_map/ppermute | solution.py:56
  6.2 10.6 %collective-permute-start.1 = (bf16[64,1536]{1,0:T(8,128)(2,1)S(1)}, bf16[64,1536]{1,0:T(8,128)(2,1)S(1)}, u32[]{:S(2)}, u32[]{:S(2)}) collective-permute-start(bf16[64,1536]{1,0:T(8,128)(2,1)S(1)} %get-tuple-element.54.pay_ref), channel_id=1, source_target_pairs={{0,2},{1,3},{2,0},{3,1},{4,6},{5,7},{6,4},{7,5},{8,10},{9,11},{10,... | collective-permute-start | bytes 589832 | tf_op jit(solution)/shard_map/ppermute | solution.py:56
  7.7 10.5 %collective-permute-start = (bf16[64,1536]{1,0:T(8,128)(2,1)S(1)}, bf16[64,1536]{1,0:T(8,128)(2,1)S(1)}, u32[]{:S(2)}, u32[]{:S(2)}) collective-permute-start(bf16[64,1536]{1,0:T(8,128)(2,1)S(1)} %get-tuple-element.54.pay_ref), channel_id=1, source_target_pairs={{0,3},{1,2},{2,1},{3,0},{4,7},{5,6},{6,5},{7,4},{8,11},{9,10},{10,... | collective-permute-start | bytes 589832 | tf_op jit(solution)/shard_map/ppermute | solution.py:56
  16.7 29.4 %copy-start.2 = (bf16[2,512,1536]{2,1,0:T(8,128)(2,1)S(1)}, bf16[2,512,1536]{2,1,0:T(8,128)(2,1)}, u32[]{:S(2)}) copy-start(bf16[2,512,1536]{2,1,0:T(8,128)(2,1)} %wd.7) | copy-start | bytes 9437188
  18.1 11.7 %copy-start.3 = (bf16[384,1536]{1,0:T(8,128)(2,1)S(1)}, bf16[384,1536]{1,0:T(8,128)(2,1)}, u32[]{:S(2)}) copy-start(bf16[384,1536]{1,0:T(8,128)(2,1)} %weight_ref.1) | copy-start | bytes 3538948
  18.2 17.6 %copy-start.5 = (f32[1536]{0:T(1024)S(1)}, f32[1536]{0:T(1024)}, u32[]{:S(2)}) copy-start(f32[1536]{0:T(1024)} %param.24) | copy-start | bytes 18436
  18.2 23.5 %copy-start.4 = (bf16[64,1536]{1,0:T(8,128)(2,1)S(1)}, bf16[64,1536]{1,0:T(8,128)(2,1)}, u32[]{:S(2)}) copy-start(bf16[64,1536]{1,0:T(8,128)(2,1)} %hidden_ref.1) | copy-start | bytes 589828
  18.2 28.0 %copy-start = (bf16[2,1536,512]{2,1,0:T(8,128)(2,1)S(1)}, bf16[2,1536,512]{2,1,0:T(8,128)(2,1)}, u32[]{:S(2)}) copy-start(bf16[2,1536,512]{2,1,0:T(8,128)(2,1)} %wg.7) | copy-start | bytes 9437188
  18.2 28.0 %copy-start.1 = (bf16[2,1536,512]{2,1,0:T(8,128)(2,1)S(1)}, bf16[2,1536,512]{2,1,0:T(8,128)(2,1)}, u32[]{:S(2)}) copy-start(bf16[2,1536,512]{2,1,0:T(8,128)(2,1)} %wu.7) | copy-start | bytes 9437188
  19.6 6.9 %collective-permute-start.3 = (bf16[13,64,128]{2,1,0:T(8,128)(2,1)S(1)}, bf16[13,64,128]{2,1,0:T(8,128)(2,1)S(1)}, u32[]{:S(2)}, u32[]{:S(2)}) collective-permute-start(bf16[13,64,128]{2,1,0:T(8,128)(2,1)S(1)} %get-tuple-element.74), channel_id=1, source_target_pairs={{0,1},{1,0},{2,3},{3,2},{4,5},{5,4},{6,7},{7,6},{8,9},{9,8},{10,11... | collective-permute-start | bytes 638984 | tf_op jit(solution)/shard_map/ppermute | solution.py:56
  19.7 10.2 %collective-permute-start.4 = (bf16[13,64,128]{2,1,0:T(8,128)(2,1)S(1)}, bf16[13,64,128]{2,1,0:T(8,128)(2,1)S(1)}, u32[]{:S(2)}, u32[]{:S(2)}) collective-permute-start(bf16[13,64,128]{2,1,0:T(8,128)(2,1)S(1)} %get-tuple-element.75), channel_id=1, source_target_pairs={{0,2},{1,3},{2,0},{3,1},{4,6},{5,7},{6,4},{7,5},{8,10},{9,11},{10,... | collective-permute-start | bytes 638984 | tf_op jit(solution)/shard_map/ppermute | solution.py:56
  21.7 8.1 %collective-permute-start.5 = (bf16[13,64,128]{2,1,0:T(8,128)(2,1)S(1)}, bf16[13,64,128]{2,1,0:T(8,128)(2,1)S(1)}, u32[]{:S(2)}, u32[]{:S(2)}) collective-permute-start(bf16[13,64,128]{2,1,0:T(8,128)(2,1)S(1)} %get-tuple-element.76), channel_id=1, source_target_pairs={{0,3},{1,2},{2,1},{3,0},{4,7},{5,6},{6,5},{7,4},{8,11},{9,10},{10,... | collective-permute-start | bytes 638984 | tf_op jit(solution)/shard_map/ppermute | solution.py:56
  32.2 5.7 %collective-permute-start.6 = (bf16[64,1536]{1,0:T(8,128)(2,1)S(1)}, bf16[64,1536]{1,0:T(8,128)(2,1)S(1)}, u32[]{:S(2)}, u32[]{:S(2)}) collective-permute-start(bf16[64,1536]{1,0:T(8,128)(2,1)S(1)} %get-tuple-element.86), channel_id=1, source_target_pairs={{0,1},{1,0},{2,3},{3,2},{4,5},{5,4},{6,7},{7,6},{8,9},{9,8},{10,11... | collective-permute-start | bytes 589832 | tf_op jit(solution)/shard_map/ppermute | solution.py:56
  33.0 7.4 %collective-permute-start.7 = (bf16[64,1536]{1,0:T(8,128)(2,1)S(1)}, bf16[64,1536]{1,0:T(8,128)(2,1)S(1)}, u32[]{:S(2)}, u32[]{:S(2)}) collective-permute-start(bf16[64,1536]{1,0:T(8,128)(2,1)S(1)} %get-tuple-element.87), channel_id=1, source_target_pairs={{0,2},{1,3},{2,0},{3,1},{4,6},{5,7},{6,4},{7,5},{8,10},{9,11},{10,... | collective-permute-start | bytes 589832 | tf_op jit(solution)/shard_map/ppermute | solution.py:56
  35.1 6.6 %collective-permute-start.8 = (bf16[64,1536]{1,0:T(8,128)(2,1)S(1)}, bf16[64,1536]{1,0:T(8,128)(2,1)S(1)}, u32[]{:S(2)}, u32[]{:S(2)}) collective-permute-start(bf16[64,1536]{1,0:T(8,128)(2,1)S(1)} %get-tuple-element.88), channel_id=1, source_target_pairs={{0,3},{1,2},{2,1},{3,0},{4,7},{5,6},{6,5},{7,4},{8,11},{9,10},{10,... | collective-permute-start | bytes 589832 | tf_op jit(solution)/shard_map/ppermute | solution.py:56
  41.9 4.3 %collective-permute-start.9 = (bf16[64,1536]{1,0:T(8,128)(2,1)S(1)}, bf16[64,1536]{1,0:T(8,128)(2,1)S(1)}, u32[]{:S(2)}, u32[]{:S(2)}) collective-permute-start(bf16[64,1536]{1,0:T(8,128)(2,1)S(1)} %get-tuple-element.92.a_ref), channel_id=1, source_target_pairs={{0,4},{4,0},{8,12},{12,8},{16,20},{20,16},{24,28},{28,24},{1,5},{5... | collective-permute-start | bytes 589832 | tf_op jit(solution)/shard_map/ppermute | solution.py:56
  41.9 12.5 %collective-permute-start.11 = (bf16[64,1536]{1,0:T(8,128)(2,1)S(1)}, bf16[64,1536]{1,0:T(8,128)(2,1)S(1)}, u32[]{:S(2)}, u32[]{:S(2)}) collective-permute-start(bf16[64,1536]{1,0:T(8,128)(2,1)S(1)} %get-tuple-element.92.a_ref), channel_id=1, source_target_pairs={{0,16},{4,20},{8,24},{12,28},{16,0},{20,4},{24,8},{28,12},{1,17},{... | collective-permute-start | bytes 589832 | tf_op jit(solution)/shard_map/ppermute | solution.py:56
  44.6 10.1 %collective-permute-start.12 = (bf16[64,1536]{1,0:T(8,128)(2,1)S(1)}, bf16[64,1536]{1,0:T(8,128)(2,1)S(1)}, u32[]{:S(2)}, u32[]{:S(2)}) collective-permute-start(bf16[64,1536]{1,0:T(8,128)(2,1)S(1)} %get-tuple-element.92.a_ref), channel_id=1, source_target_pairs={{0,8},{4,12},{8,0},{12,4},{16,24},{20,28},{24,16},{28,20},{1,9},{5... | collective-permute-start | bytes 589832 | tf_op jit(solution)/shard_map/ppermute | solution.py:56
  54.6 2.0 %collective-permute-start.13 = (bf16[64,1536]{1,0:T(8,128)(2,1)S(1)}, bf16[64,1536]{1,0:T(8,128)(2,1)S(1)}, u32[]{:S(2)}, u32[]{:S(2)}) collective-permute-start(bf16[64,1536]{1,0:T(8,128)(2,1)S(1)} %collective-permute-done.11.a_ref), channel_id=1, source_target_pairs={{0,4},{4,0},{8,12},{12,8},{16,20},{20,16},{24,28},{28,24},{1,5},{5... | collective-permute-start | bytes 589832 | tf_op jit(solution)/shard_map/ppermute | solution.py:56
  54.7 4.4 %collective-permute-start.16 = (bf16[64,1536]{1,0:T(8,128)(2,1)S(1)}, bf16[64,1536]{1,0:T(8,128)(2,1)S(1)}, u32[]{:S(2)}, u32[]{:S(2)}) collective-permute-start(bf16[64,1536]{1,0:T(8,128)(2,1)S(1)} %collective-permute-done.12.a_ref), channel_id=1, source_target_pairs={{0,4},{4,0},{8,12},{12,8},{16,20},{20,16},{24,28},{28,24},{1,5},{5... | collective-permute-start | bytes 589832 | tf_op jit(solution)/shard_map/ppermute | solution.py:56
  55.2 6.8 %collective-permute-start.19 = (bf16[64,1536]{1,0:T(8,128)(2,1)S(1)}, bf16[64,1536]{1,0:T(8,128)(2,1)S(1)}, u32[]{:S(2)}, u32[]{:S(2)}) collective-permute-start(bf16[64,1536]{1,0:T(8,128)(2,1)S(1)} %collective-permute-done.11.a_ref), channel_id=1, source_target_pairs={{0,8},{4,12},{8,0},{12,4},{16,24},{20,28},{24,16},{28,20},{1,9},{5... | collective-permute-start | bytes 589832 | tf_op jit(solution)/shard_map/ppermute | solution.py:56
  58.4 3.6 %collective-permute-start.14 = (bf16[64,1536]{1,0:T(8,128)(2,1)S(1)}, bf16[64,1536]{1,0:T(8,128)(2,1)S(1)}, u32[]{:S(2)}, u32[]{:S(2)}) collective-permute-start(bf16[64,1536]{1,0:T(8,128)(2,1)S(1)} %get-tuple-element.97), channel_id=1, source_target_pairs={{0,4},{4,0},{8,12},{12,8},{16,20},{20,16},{24,28},{28,24},{1,5},{5... | collective-permute-start | bytes 589832 | tf_op jit(solution)/shard_map/ppermute | solution.py:56
  58.5 16.2 %collective-permute-start.10 = (bf16[64,1536]{1,0:T(8,128)(2,1)S(1)}, bf16[64,1536]{1,0:T(8,128)(2,1)S(1)}, u32[]{:S(2)}, u32[]{:S(2)}) collective-permute-start(bf16[64,1536]{1,0:T(8,128)(2,1)S(1)} %get-tuple-element.94), channel_id=1, source_target_pairs={{0,4},{4,0},{8,12},{12,8},{16,20},{20,16},{24,28},{28,24},{1,5},{5... | collective-permute-start | bytes 589832 | tf_op jit(solution)/shard_map/ppermute | solution.py:56
  60.8 9.3 %collective-permute-start.23 = (bf16[8,1024]{1,0:T(8,128)(2,1)S(1)}, bf16[8,1024]{1,0:T(8,128)(2,1)S(1)}, u32[]{:S(2)}, u32[]{:S(2)}) collective-permute-start(bf16[8,1024]{1,0:T(8,128)(2,1)S(1)} %get-tuple-element.105), channel_id=1, source_target_pairs={{0,1},{1,0},{2,3},{3,2},{4,5},{5,4},{6,7},{7,6},{8,9},{9,8},{10,11... | collective-permute-start | bytes 49160 | tf_op jit(solution)/shard_map/ppermute | solution.py:56
  61.5 4.9 %collective-permute-start.17 = (bf16[64,1536]{1,0:T(8,128)(2,1)S(1)}, bf16[64,1536]{1,0:T(8,128)(2,1)S(1)}, u32[]{:S(2)}, u32[]{:S(2)}) collective-permute-start(bf16[64,1536]{1,0:T(8,128)(2,1)S(1)} %get-tuple-element.100), channel_id=1, source_target_pairs={{0,4},{4,0},{8,12},{12,8},{16,20},{20,16},{24,28},{28,24},{1,5},{5... | collective-permute-start | bytes 589832 | tf_op jit(solution)/shard_map/ppermute | solution.py:56
  62.0 2.5 %collective-permute-start.20 = (bf16[64,1536]{1,0:T(8,128)(2,1)S(1)}, bf16[64,1536]{1,0:T(8,128)(2,1)S(1)}, u32[]{:S(2)}, u32[]{:S(2)}) collective-permute-start(bf16[64,1536]{1,0:T(8,128)(2,1)S(1)} %collective-permute-done.19.a_ref), channel_id=1, source_target_pairs={{0,4},{4,0},{8,12},{12,8},{16,20},{20,16},{24,28},{28,24},{1,5},{5... | collective-permute-start | bytes 589832 | tf_op jit(solution)/shard_map/ppermute | solution.py:56
  62.1 12.9 %collective-permute-start.15 = (bf16[64,1536]{1,0:T(8,128)(2,1)S(1)}, bf16[64,1536]{1,0:T(8,128)(2,1)S(1)}, u32[]{:S(2)}, u32[]{:S(2)}) collective-permute-start(bf16[64,1536]{1,0:T(8,128)(2,1)S(1)} %add_convert_fusion.3), channel_id=1, source_target_pairs={{0,16},{4,20},{8,24},{12,28},{16,0},{20,4},{24,8},{28,12},{1,17},{... | collective-permute-start | bytes 589832 | tf_op jit(solution)/shard_map/ppermute | solution.py:56
  66.3 1.8 %collective-permute-start.21 = (bf16[64,1536]{1,0:T(8,128)(2,1)S(1)}, bf16[64,1536]{1,0:T(8,128)(2,1)S(1)}, u32[]{:S(2)}, u32[]{:S(2)}) collective-permute-start(bf16[64,1536]{1,0:T(8,128)(2,1)S(1)} %get-tuple-element.103), channel_id=1, source_target_pairs={{0,4},{4,0},{8,12},{12,8},{16,20},{20,16},{24,28},{28,24},{1,5},{5... | collective-permute-start | bytes 589832 | tf_op jit(solution)/shard_map/ppermute | solution.py:56
  66.5 14.8 %collective-permute-start.18 = (bf16[64,1536]{1,0:T(8,128)(2,1)S(1)}, bf16[64,1536]{1,0:T(8,128)(2,1)S(1)}, u32[]{:S(2)}, u32[]{:S(2)}) collective-permute-start(bf16[64,1536]{1,0:T(8,128)(2,1)S(1)} %add_convert_fusion.2), channel_id=1, source_target_pairs={{0,8},{4,12},{8,0},{12,4},{16,24},{20,28},{24,16},{28,20},{1,9},{5... | collective-permute-start | bytes 589832 | tf_op jit(solution)/shard_map/ppermute | solution.py:56
  68.2 13.1 %collective-permute-start.22 = (bf16[64,1536]{1,0:T(8,128)(2,1)S(1)}, bf16[64,1536]{1,0:T(8,128)(2,1)S(1)}, u32[]{:S(2)}, u32[]{:S(2)}) collective-permute-start(bf16[64,1536]{1,0:T(8,128)(2,1)S(1)} %add_convert_fusion.1), channel_id=1, source_target_pairs={{0,24},{4,28},{8,16},{12,20},{16,8},{20,12},{24,0},{28,4},{1,25},{... | collective-permute-start | bytes 589832 | tf_op jit(solution)/shard_map/ppermute | solution.py:56
  70.1 3.9 %collective-permute-start.24 = (bf16[16,1024]{1,0:T(8,128)(2,1)S(1)}, bf16[16,1024]{1,0:T(8,128)(2,1)S(1)}, u32[]{:S(2)}, u32[]{:S(2)}) collective-permute-start(bf16[16,1024]{1,0:T(8,128)(2,1)S(1)} %pad_maximum_fusion.1), channel_id=1, source_target_pairs={{0,2},{1,3},{2,0},{3,1},{4,6},{5,7},{6,4},{7,5},{8,10},{9,11},{10,... | collective-permute-start | bytes 98312 | tf_op jit(solution)/shard_map/ppermute | solution.py:56

commit v6 on v5

--- a/solution.py
+++ b/solution.py
@@ -741,13 +741,16 @@
             lines[k + reach] = exchange(lines[k], "dp", data, CORES * reach)
         reach //= 2
     single = [k for k in lines if k and k & (k - 1) == 0]
-    total = mixed
+    far = []
     last = None
     for k in sorted(lines, key=lambda k: (bin(k).count("1"), -k)):
         if k == max(single) or (k and k not in single):
             names = single if k in single else [k]
-            tied = lax.optimization_barrier([lines[name] for name in names] + [last])
+            held = [last] if k in single else [last, base]
+            tied = lax.optimization_barrier([lines[name] for name in names] + held)
             lines.update(zip(names, tied))
+            if k not in single:
+                base = tied[-1]
         line = lines[k]
         twin = exchange(line, "dp", data, 1)
         own, other = experts_part(k, bias, route, w_gate, w_up, w_down, line, twin)
@@ -758,13 +761,16 @@
         if k:
             chip = chip.astype(BF)
             chip = exchange(chip, "dp", data, CORES * k).astype(F32)
-        total = total + chip
+        if k:
+            far.append(chip)
+        else:
+            base = mixed + chip
     reach = 1
     while reach < tensor:
         picks = jnp.concatenate([picks, exchange(picks, "tensor", tensor, reach)], axis=0)
         reach *= 2
     compacted = accepted(picks, requests, path.shape[1], n)
-    return total.astype(BF), compacted
+    return functools.reduce(jnp.add, far, base).astype(BF), compacted
 
 
 def solution(mesh):

time: 82.3 us -> 83.8 us (1.018)
  waiting for transfers between devices: 30.8 us -> 34.2 us
  starting transfers between devices: 26.5 us -> 24.7 us
    ppermute x25, waiting for transfers between devices: 30.8 us -> 34.2 us  [exchange(): return lax.ppermute(x, axis, [(i, i ^ step) for i in range(size)])]
    ppermute x25, starting transfers between devices: 26.5 us -> 24.7 us  [exchange(): return lax.ppermute(x, axis, [(i, i ^ step) for i in range(size)])]
  transfers between devices with their start and end apart: 25 -> 25, of which waited for: 12 -> 13; matrix products, arithmetic and copies ran while one was open for 0% -> 0% of each run, Pallas kernels for 20% -> 20%
where the time goes in v6:
time: 83.8 us; the launch traced here: 83.7 us
  waiting for transfers between devices  34.2 us (41%)
  starting transfers between devices  24.7 us (29%)
  Pallas kernels  22.9 us (27%)
  other arithmetic  0.96 us (1%)
  between operations  0.85 us (1%)
    ppermute x25, waiting for transfers between devices, exchange(): return lax.ppermute(x, axis, [(i, i ^ step) for i in range(size)])  34.2 us
    ppermute x25, starting transfers between devices, exchange(): return lax.ppermute(x, axis, [(i, i ^ step) for i in range(size)])  24.7 us
    pallas_call x4, Pallas kernels, experts_part(): pl.pallas_call(functools.partial(experts_kernel, step), out_shape=(jax.Sh...  7.31 us
    pallas_call x4, Pallas kernels, attend_split(): pl.pallas_call(functools.partial(attend_split_kernel, step, step == 0, co...  6.41 us
    pallas_call x1, Pallas kernels, prelude(): pl.pallas_call(prelude_kernel, out_shape=(jax.ShapeDtypeStruct((n, width)...  2.52 us
    pallas_call x1, Pallas kernels, unpack(): pl.pallas_call(unpack_kernel, out_shape=jax.ShapeDtypeStruct((requests, 2...  2.37 us
    pallas_call x1, Pallas kernels, join_split(): pl.pallas_call(functools.partial(join_split_kernel, count), out_shape=tup...  2.34 us
  transfers between devices with their start and end apart: 25, of which 13 were waited for; matrix products, arithmetic and copies ran while one was open for 0% of the time, Pallas kernels for 20%

profile of v6, /device:TPU:0, one launch (start us, length us, event | category | flops | bytes accessed | tf_op | source)
XLA Modules:
  0.0 83.7 jit_solution(16491752194098900113)
XLA Ops:
  0.6 2.5 %prelude.1 = (bf16[64,1536]{1,0:T(8,128)(2,1)S(1)}, bf16[64,512]{1,0:T(8,128)(2,1)S(1)}, bf16[64,512]{1,0:T(8,128)(2,1)S(1)}, f32[64,64]{1,0:T(8,128)S(1)}, f32[...) custom-call(s32[4]{0:T(128)} %len_hbm.1, ...), custom_call_target="tpu_custom_call" | custom-call | flops 10000000 | tf_op jit(solution)/shard_map/prelude/pallas_call | solution.py:157
  3.2 3.0 %collective-permute-start.2 = (bf16[64,1536]{1,0:T(8,128)(2,1)S(1)}, bf16[64,1536]{1,0:T(8,128)(2,1)S(1)}, u32[]{:S(2)}, u32[]{:S(2)}) collective-permute-start(bf16[64,1536]{1,0:T(8,128)(2,1)S(1)} %get-tuple-element.55.pay_ref), channel_id=1, source_target_pairs={{0,1},{1,0},{2,3},{3,2},{4,5},{5,4},{6,7},{7,6},{8,9},{9,8},{10,11... | collective-permute-start | bytes 589832 | tf_op jit(solution)/shard_map/ppermute | solution.py:56
  6.2 1.5 %collective-permute-start.1 = (bf16[64,1536]{1,0:T(8,128)(2,1)S(1)}, bf16[64,1536]{1,0:T(8,128)(2,1)S(1)}, u32[]{:S(2)}, u32[]{:S(2)}) collective-permute-start(bf16[64,1536]{1,0:T(8,128)(2,1)S(1)} %get-tuple-element.55.pay_ref), channel_id=1, source_target_pairs={{0,2},{1,3},{2,0},{3,1},{4,6},{5,7},{6,4},{7,5},{8,10},{9,11},{10,... | collective-permute-start | bytes 589832 | tf_op jit(solution)/shard_map/ppermute | solution.py:56
  7.7 0.0 collective-permute-start
  7.7 2.4 %unpack.1.kv_ref = bf16[4,8,512,128]{3,2,1,0:T(8,128)(2,1)S(1)} custom-call(bf16[4,4096,128]{2,1,0:T(8,128)(2,1)S(1)} %get-tuple-element.56.packed_ref), custom_call_target="tpu_custom_call" | custom-call | flops 100000000 | tf_op jit(solution)/shard_map/unpack/pallas_call | solution.py:197
  10.1 2.2 %attend.4 = (bf16[13,64,128]{2,1,0:T(8,128)(2,1)S(1)}, bf16[13,64,128]{2,1,0:T(8,128)(2,1)S(1)}, bf16[13,64,128]{2,1,0:T(8,128)(2,1)S(1)}, bf16[13,64,128]{2,1,0:T(8,128)(2,1)S(1)}) custom-call(bf16[64,1536]{1,0:T(8,128)(2,1)S(1)} %get-tuple-element.55.pay_ref, bf16[4,8,512,128]{3,2,1,0:T(8,128)(2,1)S(1)} %unpack.1.kv_ref, ...), custom_call_target="tpu_custom_call" | custom-call | flops 400000000 | tf_op jit(solution)/shard_map/attend/pallas_call | solution.py:434
  12.3 0.0 collective-permute-done.2.pay_ref
  12.3 1.4 %attend.5 = (bf16[13,64,128]{2,1,0:T(8,128)(2,1)S(1)}, bf16[13,64,128]{2,1,0:T(8,128)(2,1)S(1)}, bf16[13,64,128]{2,1,0:T(8,128)(2,1)S(1)}, bf16[13,64,128]{2,1,0:T(8,128)(2,1)S(1)}) custom-call(bf16[64,1536]{1,0:T(8,128)(2,1)S(1)} %collective-permute-done.2.pay_ref, ...), custom_call_target="tpu_custom_call", output_to_operand_aliasing={{0}: (7, {}), {1}: (8, {}), {2}: (9, {}), {3}: (10, {})} | custom-call | flops 400000000 | tf_op jit(solution)/shard_map/attend/pallas_call | solution.py:434
  13.7 3.0 %collective-permute-done.1.pay_ref = bf16[64,1536]{1,0:T(8,128)(2,1)S(1)} collective-permute-done((bf16[64,1536]{1,0:T(8,128)(2,1)S(1)}, bf16[64,1536]{1,0:T(8,128)(2,1)S(1)}, u32[]{:S(2)}, u32[]{:S(2)}) %collective-permute-start.1) | collective-permute-done | bytes 196640 | tf_op jit(solution)/shard_map/ppermute | solution.py:56
  16.7 1.4 %attend.6 = (bf16[13,64,128]{2,1,0:T(8,128)(2,1)S(1)}, bf16[13,64,128]{2,1,0:T(8,128)(2,1)S(1)}, bf16[13,64,128]{2,1,0:T(8,128)(2,1)S(1)}, bf16[13,64,128]{2,1,0:T(8,128)(2,1)S(1)}) custom-call(bf16[64,1536]{1,0:T(8,128)(2,1)S(1)} %collective-permute-done.1.pay_ref, ...), custom_call_target="tpu_custom_call", output_to_operand_aliasing={{0}: (7, {}), {1}: (8, {}), {2}: (9, {}), {3}: (10, {})} | custom-call | flops 400000000 | tf_op jit(solution)/shard_map/attend/pallas_call | solution.py:434
  18.1 0.0 copy-start.3
  18.2 0.0 collective-permute-done.pay_ref
  18.2 0.0 copy-start.5
  18.2 0.0 copy-start.4
  18.2 0.0 copy-start
  18.2 0.0 copy-start.1
  18.2 1.4 %attend.7 = (bf16[13,64,128]{2,1,0:T(8,128)(2,1)S(1)}, bf16[13,64,128]{2,1,0:T(8,128)(2,1)S(1)}, bf16[13,64,128]{2,1,0:T(8,128)(2,1)S(1)}, bf16[13,64,128]{2,1,0:T(8,128)(2,1)S(1)}) custom-call(bf16[64,1536]{1,0:T(8,128)(2,1)S(1)} %collective-permute-done.pay_ref, ...), custom_call_target="tpu_custom_call", output_to_operand_aliasing={{0}: (7, {}), {1}: (8, {}), {2}: (9, {}), {3}: (10, {})} | custom-call | flops 400000000 | tf_op jit(solution)/shard_map/attend/pallas_call | solution.py:434
  19.6 0.1 collective-permute-start.3
  19.7 2.0 %collective-permute-start.4 = (bf16[13,64,128]{2,1,0:T(8,128)(2,1)S(1)}, bf16[13,64,128]{2,1,0:T(8,128)(2,1)S(1)}, u32[]{:S(2)}, u32[]{:S(2)}) collective-permute-start(bf16[13,64,128]{2,1,0:T(8,128)(2,1)S(1)} %get-tuple-element.76), channel_id=1, source_target_pairs={{0,2},{1,3},{2,0},{3,1},{4,6},{5,7},{6,4},{7,5},{8,10},{9,11},{10,... | collective-permute-start | bytes 638984 | tf_op jit(solution)/shard_map/ppermute | solution.py:56
  21.7 1.4 %collective-permute-start.5 = (bf16[13,64,128]{2,1,0:T(8,128)(2,1)S(1)}, bf16[13,64,128]{2,1,0:T(8,128)(2,1)S(1)}, u32[]{:S(2)}, u32[]{:S(2)}) collective-permute-start(bf16[13,64,128]{2,1,0:T(8,128)(2,1)S(1)} %get-tuple-element.77), channel_id=1, source_target_pairs={{0,3},{1,2},{2,1},{3,0},{4,7},{5,6},{6,5},{7,4},{8,11},{9,10},{10,... | collective-permute-start | bytes 638984 | tf_op jit(solution)/shard_map/ppermute | solution.py:56
  23.2 1.1 %routing.1 = (f32[8,64,16]{2,1,0:T(8,128)S(1)}, bf16[32,1536]{1,0:T(8,128)(2,1)S(1)}) custom-call(s32[8,8,64]{2,1,0:T(8,128)} %bitcast.15, f32[16,1536]{1,0:T(8,128)} %bitcast.14), custom_call_target="tpu_custom_call" | custom-call | flops 1000000 | tf_op jit(solution)/shard_map/routing/pallas_call | solution.py:237
  24.3 2.3 %collective-permute-done.3.refs_1_ = bf16[13,64,128]{2,1,0:T(8,128)(2,1)S(1)} collective-permute-done((bf16[13,64,128]{2,1,0:T(8,128)(2,1)S(1)}, bf16[13,64,128]{2,1,0:T(8,128)(2,1)S(1)}, u32[]{:S(2)}, u32[]{:S(2)}) %collective-permute-start.3) | collective-permute-done | bytes 213024 | tf_op jit(solution)/shard_map/ppermute | solution.py:56
  26.5 3.3 %collective-permute-done.4.refs_2_ = bf16[13,64,128]{2,1,0:T(8,128)(2,1)S(1)} collective-permute-done((bf16[13,64,128]{2,1,0:T(8,128)(2,1)S(1)}, bf16[13,64,128]{2,1,0:T(8,128)(2,1)S(1)}, u32[]{:S(2)}, u32[]{:S(2)}) %collective-permute-start.4) | collective-permute-done | bytes 213024 | tf_op jit(solution)/shard_map/ppermute | solution.py:56
  29.9 2.3 %join.1 = (f32[64,1536]{1,0:T(8,128)S(1)}, bf16[64,1536]{1,0:T(8,128)(2,1)S(1)}, bf16[64,1536]{1,0:T(8,128)(2,1)S(1)}, bf16[64,1536]{1,0:T(8,128)(2,1)S(1)}) custom-call(bf16[384,1536]{1,0:T(8,128)(2,1)S(1)} %copy-done.3, bf16[13,64,128]{2,1,0:T(8,128)(2,1)S(1)} %get-tuple-element.82.refs_0_, bf16[13,64,128]{2,1,0:T(8,128)(2,1)S(1)} %collective-permute-done.3.refs_1_, ...), custom_call_target="tpu_custom_call" | custom-call | flops 400000000 | tf_op jit(solution)/shard_map/join/pallas_call | solution.py:490
  32.2 0.8 collective-permute-start.6
  33.0 2.1 %collective-permute-start.7 = (bf16[64,1536]{1,0:T(8,128)(2,1)S(1)}, bf16[64,1536]{1,0:T(8,128)(2,1)S(1)}, u32[]{:S(2)}, u32[]{:S(2)}) collective-permute-start(bf16[64,1536]{1,0:T(8,128)(2,1)S(1)} %get-tuple-element.88), channel_id=1, source_target_pairs={{0,2},{1,3},{2,0},{3,1},{4,6},{5,7},{6,4},{7,5},{8,10},{9,11},{10,... | collective-permute-start | bytes 589832 | tf_op jit(solution)/shard_map/ppermute | solution.py:56
  35.1 0.7 collective-permute-start.8
  35.8 2.2 %collective-permute-done.6.refs_0_ = bf16[64,1536]{1,0:T(8,128)(2,1)S(1)} collective-permute-done((bf16[64,1536]{1,0:T(8,128)(2,1)S(1)}, bf16[64,1536]{1,0:T(8,128)(2,1)S(1)}, u32[]{:S(2)}, u32[]{:S(2)}) %collective-permute-start.6) | collective-permute-done | bytes 196640 | tf_op jit(solution)/shard_map/ppermute | solution.py:56
  38.0 2.4 %collective-permute-done.7.refs_1_ = bf16[64,1536]{1,0:T(8,128)(2,1)S(1)} collective-permute-done((bf16[64,1536]{1,0:T(8,128)(2,1)S(1)}, bf16[64,1536]{1,0:T(8,128)(2,1)S(1)}, u32[]{:S(2)}, u32[]{:S(2)}) %collective-permute-start.7) | collective-permute-done | bytes 196640 | tf_op jit(solution)/shard_map/ppermute | solution.py:56
  40.4 1.3 %collective-permute-done.8.refs_2_ = bf16[64,1536]{1,0:T(8,128)(2,1)S(1)} collective-permute-done((bf16[64,1536]{1,0:T(8,128)(2,1)S(1)}, bf16[64,1536]{1,0:T(8,128)(2,1)S(1)}, u32[]{:S(2)}, u32[]{:S(2)}) %collective-permute-start.8) | collective-permute-done | bytes 196640 | tf_op jit(solution)/shard_map/ppermute | solution.py:56
  41.6 0.2 norm.1
  41.9 0.1 collective-permute-start.12
  41.9 1.6 %collective-permute-start.11 = (bf16[64,1536]{1,0:T(8,128)(2,1)S(1)}, bf16[64,1536]{1,0:T(8,128)(2,1)S(1)}, u32[]{:S(2)}, u32[]{:S(2)}) collective-permute-start(bf16[64,1536]{1,0:T(8,128)(2,1)S(1)} %get-tuple-element.90.a_ref), channel_id=1, source_target_pairs={{0,8},{4,12},{8,0},{12,4},{16,24},{20,28},{24,16},{28,20},{1,9},{5... | collective-permute-start | bytes 589832 | tf_op jit(solution)/shard_map/ppermute | solution.py:56
  43.6 2.6 %collective-permute-start.9 = (bf16[64,1536]{1,0:T(8,128)(2,1)S(1)}, bf16[64,1536]{1,0:T(8,128)(2,1)S(1)}, u32[]{:S(2)}, u32[]{:S(2)}) collective-permute-start(bf16[64,1536]{1,0:T(8,128)(2,1)S(1)} %get-tuple-element.90.a_ref), channel_id=1, source_target_pairs={{0,16},{4,20},{8,24},{12,28},{16,0},{20,4},{24,8},{28,12},{1,17},{... | collective-permute-start | bytes 589832 | tf_op jit(solution)/shard_map/ppermute | solution.py:56
  46.2 1.8 %experts.4 = (f32[64,1536]{1,0:T(8,128)S(1)}, bf16[64,1536]{1,0:T(8,128)(2,1)S(1)}) custom-call(f32[8,64,16]{2,1,0:T(8,128)S(1)} %get-tuple-element.91.bias_ref, bf16[32,1536]{1,0:T(8,128)(2,1)S(1)} %get-tuple-element.92.route_ref, bf16[2,1536,512]{2,1,0:T(8,128)(2,1)S(1)} %copy-done, bf16[2,1536,512]{2,1,0:T(8,128)(2,1)S(1)} %copy-done.1, ...), custom_call_target="tpu_custom_call" | custom-call | flops 1200000000 | tf_op jit(solution)/shard_map/experts/pallas_call | solution.py:645
  48.0 5.3 %collective-permute-done.11.a_ref = bf16[64,1536]{1,0:T(8,128)(2,1)S(1)} collective-permute-done((bf16[64,1536]{1,0:T(8,128)(2,1)S(1)}, bf16[64,1536]{1,0:T(8,128)(2,1)S(1)}, u32[]{:S(2)}, u32[]{:S(2)}) %collective-permute-start.11) | collective-permute-done | bytes 196640 | tf_op jit(solution)/shard_map/ppermute | solution.py:56
  53.3 2.4 %collective-permute-done.9.a_ref = bf16[64,1536]{1,0:T(8,128)(2,1)S(1)} collective-permute-done((bf16[64,1536]{1,0:T(8,128)(2,1)S(1)}, bf16[64,1536]{1,0:T(8,128)(2,1)S(1)}, u32[]{:S(2)}, u32[]{:S(2)}) %collective-permute-start.9) | collective-permute-done | bytes 196640 | tf_op jit(solution)/shard_map/ppermute | solution.py:56
  55.7 0.0 collective-permute-start.13
  55.7 0.5 collective-permute-start.15
  56.2 0.0 collective-permute-start.14
  56.2 0.4 collective-permute-start.10
  56.7 0.5 collective-permute-done.13.b_ref
  57.2 1.8 %experts.5 = (f32[64,1536]{1,0:T(8,128)S(1)}, bf16[64,1536]{1,0:T(8,128)(2,1)S(1)}) custom-call(f32[8,64,16]{2,1,0:T(8,128)S(1)} %get-tuple-element.91.bias_ref, bf16[32,1536]{1,0:T(8,128)(2,1)S(1)} %get-tuple-element.92.route_ref, bf16[2,1536,512]{2,1,0:T(8,128)(2,1)S(1)} %copy-done, bf16[2,1536,512]{2,1,0:T(8,128)(2,1)S(1)} %copy-done.1, ...), custom_call_target="tpu_custom_call" | custom-call | flops 1200000000 | tf_op jit(solution)/shard_map/experts/pallas_call | solution.py:645
  59.0 0.7 collective-permute-start.23
  59.7 1.8 %experts.6 = (f32[64,1536]{1,0:T(8,128)S(1)}, bf16[64,1536]{1,0:T(8,128)(2,1)S(1)}) custom-call(f32[8,64,16]{2,1,0:T(8,128)S(1)} %get-tuple-element.91.bias_ref, bf16[32,1536]{1,0:T(8,128)(2,1)S(1)} %get-tuple-element.92.route_ref, bf16[2,1536,512]{2,1,0:T(8,128)(2,1)S(1)} %copy-done, bf16[2,1536,512]{2,1,0:T(8,128)(2,1)S(1)} %copy-done.1, ...), custom_call_target="tpu_custom_call" | custom-call | flops 1200000000 | tf_op jit(solution)/shard_map/experts/pallas_call | solution.py:645
  61.5 0.1 collective-permute-start.16
  61.6 0.5 collective-permute-start.18
  62.1 0.1 add_add_fusion
  62.2 1.4 %collective-permute-done.10.a_ref = bf16[64,1536]{1,0:T(8,128)(2,1)S(1)} collective-permute-done((bf16[64,1536]{1,0:T(8,128)(2,1)S(1)}, bf16[64,1536]{1,0:T(8,128)(2,1)S(1)}, u32[]{:S(2)}, u32[]{:S(2)}) %collective-permute-start.10) | collective-permute-done | bytes 196640 | tf_op jit(solution)/shard_map/ppermute | solution.py:56
  63.5 0.0 collective-permute-done.16
  63.6 1.6 %collective-permute-start.17 = (bf16[64,1536]{1,0:T(8,128)(2,1)S(1)}, bf16[64,1536]{1,0:T(8,128)(2,1)S(1)}, u32[]{:S(2)}, u32[]{:S(2)}) collective-permute-start(bf16[64,1536]{1,0:T(8,128)(2,1)S(1)} %add_convert_fusion.3), channel_id=1, source_target_pairs={{0,16},{4,20},{8,24},{12,28},{16,0},{20,4},{24,8},{28,12},{1,17},{... | collective-permute-start | bytes 589832 | tf_op jit(solution)/shard_map/ppermute | solution.py:56
  65.2 1.8 %experts.7 = (f32[64,1536]{1,0:T(8,128)S(1)}, bf16[64,1536]{1,0:T(8,128)(2,1)S(1)}) custom-call(f32[8,64,16]{2,1,0:T(8,128)S(1)} %get-tuple-element.91.bias_ref, bf16[32,1536]{1,0:T(8,128)(2,1)S(1)} %get-tuple-element.92.route_ref, bf16[2,1536,512]{2,1,0:T(8,128)(2,1)S(1)} %copy-done, bf16[2,1536,512]{2,1,0:T(8,128)(2,1)S(1)} %copy-done.1, ...), custom_call_target="tpu_custom_call" | custom-call | flops 1200000000 | tf_op jit(solution)/shard_map/experts/pallas_call | solution.py:645
  67.1 0.1 collective-permute-start.21
  67.2 0.0 collective-permute-done.18
  67.2 1.7 %collective-permute-start.19 = (bf16[64,1536]{1,0:T(8,128)(2,1)S(1)}, bf16[64,1536]{1,0:T(8,128)(2,1)S(1)}, u32[]{:S(2)}, u32[]{:S(2)}) collective-permute-start(bf16[64,1536]{1,0:T(8,128)(2,1)S(1)} %add_convert_fusion.2), channel_id=1, source_target_pairs={{0,8},{4,12},{8,0},{12,4},{16,24},{20,28},{24,16},{28,20},{1,9},{5... | collective-permute-start | bytes 589832 | tf_op jit(solution)/shard_map/ppermute | solution.py:56
  68.9 0.0 collective-permute-done.21
  69.0 1.9 %collective-permute-start.22 = (bf16[64,1536]{1,0:T(8,128)(2,1)S(1)}, bf16[64,1536]{1,0:T(8,128)(2,1)S(1)}, u32[]{:S(2)}, u32[]{:S(2)}) collective-permute-start(bf16[64,1536]{1,0:T(8,128)(2,1)S(1)} %add_convert_fusion.1), channel_id=1, source_target_pairs={{0,24},{4,28},{8,16},{12,20},{16,8},{20,12},{24,0},{28,4},{1,25},{... | collective-permute-start | bytes 589832 | tf_op jit(solution)/shard_map/ppermute | solution.py:56
  70.9 0.0 collective-permute-done.23
  70.9 1.2 %collective-permute-start.24 = (bf16[16,1024]{1,0:T(8,128)(2,1)S(1)}, bf16[16,1024]{1,0:T(8,128)(2,1)S(1)}, u32[]{:S(2)}, u32[]{:S(2)}) collective-permute-start(bf16[16,1024]{1,0:T(8,128)(2,1)S(1)} %pad_maximum_fusion.1), channel_id=1, source_target_pairs={{0,2},{1,3},{2,0},{3,1},{4,6},{5,7},{6,4},{7,5},{8,10},{9,11},{10,... | collective-permute-start | bytes 98312 | tf_op jit(solution)/shard_map/ppermute | solution.py:56
  72.1 2.7 %collective-permute-done.24 = bf16[16,1024]{1,0:T(8,128)(2,1)S(1)} collective-permute-done((bf16[16,1024]{1,0:T(8,128)(2,1)S(1)}, bf16[16,1024]{1,0:T(8,128)(2,1)S(1)}, u32[]{:S(2)}, u32[]{:S(2)}) %collective-permute-start.24) | collective-permute-done | bytes 32800 | tf_op jit(solution)/shard_map/ppermute | solution.py:56
  74.8 0.7 accepted.1
  75.5 1.1 %collective-permute-done.17 = bf16[64,1536]{1,0:T(8,128)(2,1)S(1)} collective-permute-done((bf16[64,1536]{1,0:T(8,128)(2,1)S(1)}, bf16[64,1536]{1,0:T(8,128)(2,1)S(1)}, u32[]{:S(2)}, u32[]{:S(2)}) %collective-permute-start.17) | collective-permute-done | bytes 196640 | tf_op jit(solution)/shard_map/ppermute | solution.py:56
  76.6 6.3 %collective-permute-done.19 = bf16[64,1536]{1,0:T(8,128)(2,1)S(1)} collective-permute-done((bf16[64,1536]{1,0:T(8,128)(2,1)S(1)}, bf16[64,1536]{1,0:T(8,128)(2,1)S(1)}, u32[]{:S(2)}, u32[]{:S(2)}) %collective-permute-start.19) | collective-permute-done | bytes 196640 | tf_op jit(solution)/shard_map/ppermute | solution.py:56
  82.9 0.8 add_convert_fusion
  (20 shorter events, 0.2 us)
Async XLA Ops:
  3.2 9.1 %collective-permute-start.2 = (bf16[64,1536]{1,0:T(8,128)(2,1)S(1)}, bf16[64,1536]{1,0:T(8,128)(2,1)S(1)}, u32[]{:S(2)}, u32[]{:S(2)}) collective-permute-start(bf16[64,1536]{1,0:T(8,128)(2,1)S(1)} %get-tuple-element.55.pay_ref), channel_id=1, source_target_pairs={{0,1},{1,0},{2,3},{3,2},{4,5},{5,4},{6,7},{7,6},{8,9},{9,8},{10,11... | collective-permute-start | bytes 589832 | tf_op jit(solution)/shard_map/ppermute | solution.py:56
  6.2 10.6 %collective-permute-start.1 = (bf16[64,1536]{1,0:T(8,128)(2,1)S(1)}, bf16[64,1536]{1,0:T(8,128)(2,1)S(1)}, u32[]{:S(2)}, u32[]{:S(2)}) collective-permute-start(bf16[64,1536]{1,0:T(8,128)(2,1)S(1)} %get-tuple-element.55.pay_ref), channel_id=1, source_target_pairs={{0,2},{1,3},{2,0},{3,1},{4,6},{5,7},{6,4},{7,5},{8,10},{9,11},{10,... | collective-permute-start | bytes 589832 | tf_op jit(solution)/shard_map/ppermute | solution.py:56
  7.7 10.5 %collective-permute-start = (bf16[64,1536]{1,0:T(8,128)(2,1)S(1)}, bf16[64,1536]{1,0:T(8,128)(2,1)S(1)}, u32[]{:S(2)}, u32[]{:S(2)}) collective-permute-start(bf16[64,1536]{1,0:T(8,128)(2,1)S(1)} %get-tuple-element.55.pay_ref), channel_id=1, source_target_pairs={{0,3},{1,2},{2,1},{3,0},{4,7},{5,6},{6,5},{7,4},{8,11},{9,10},{10,... | collective-permute-start | bytes 589832 | tf_op jit(solution)/shard_map/ppermute | solution.py:56
  16.7 29.4 %copy-start.2 = (bf16[2,512,1536]{2,1,0:T(8,128)(2,1)S(1)}, bf16[2,512,1536]{2,1,0:T(8,128)(2,1)}, u32[]{:S(2)}) copy-start(bf16[2,512,1536]{2,1,0:T(8,128)(2,1)} %wd.7) | copy-start | bytes 9437188
  18.1 11.7 %copy-start.3 = (bf16[384,1536]{1,0:T(8,128)(2,1)S(1)}, bf16[384,1536]{1,0:T(8,128)(2,1)}, u32[]{:S(2)}) copy-start(bf16[384,1536]{1,0:T(8,128)(2,1)} %weight_ref.1) | copy-start | bytes 3538948
  18.2 17.6 %copy-start.5 = (f32[1536]{0:T(1024)S(1)}, f32[1536]{0:T(1024)}, u32[]{:S(2)}) copy-start(f32[1536]{0:T(1024)} %param.24) | copy-start | bytes 18436
  18.2 23.5 %copy-start.4 = (bf16[64,1536]{1,0:T(8,128)(2,1)S(1)}, bf16[64,1536]{1,0:T(8,128)(2,1)}, u32[]{:S(2)}) copy-start(bf16[64,1536]{1,0:T(8,128)(2,1)} %hidden_ref.1) | copy-start | bytes 589828
  18.2 28.0 %copy-start = (bf16[2,1536,512]{2,1,0:T(8,128)(2,1)S(1)}, bf16[2,1536,512]{2,1,0:T(8,128)(2,1)}, u32[]{:S(2)}) copy-start(bf16[2,1536,512]{2,1,0:T(8,128)(2,1)} %wg.7) | copy-start | bytes 9437188
  18.2 28.0 %copy-start.1 = (bf16[2,1536,512]{2,1,0:T(8,128)(2,1)S(1)}, bf16[2,1536,512]{2,1,0:T(8,128)(2,1)}, u32[]{:S(2)}) copy-start(bf16[2,1536,512]{2,1,0:T(8,128)(2,1)} %wu.7) | copy-start | bytes 9437188
  19.6 6.9 %collective-permute-start.3 = (bf16[13,64,128]{2,1,0:T(8,128)(2,1)S(1)}, bf16[13,64,128]{2,1,0:T(8,128)(2,1)S(1)}, u32[]{:S(2)}, u32[]{:S(2)}) collective-permute-start(bf16[13,64,128]{2,1,0:T(8,128)(2,1)S(1)} %get-tuple-element.75), channel_id=1, source_target_pairs={{0,1},{1,0},{2,3},{3,2},{4,5},{5,4},{6,7},{7,6},{8,9},{9,8},{10,11... | collective-permute-start | bytes 638984 | tf_op jit(solution)/shard_map/ppermute | solution.py:56
  19.7 10.2 %collective-permute-start.4 = (bf16[13,64,128]{2,1,0:T(8,128)(2,1)S(1)}, bf16[13,64,128]{2,1,0:T(8,128)(2,1)S(1)}, u32[]{:S(2)}, u32[]{:S(2)}) collective-permute-start(bf16[13,64,128]{2,1,0:T(8,128)(2,1)S(1)} %get-tuple-element.76), channel_id=1, source_target_pairs={{0,2},{1,3},{2,0},{3,1},{4,6},{5,7},{6,4},{7,5},{8,10},{9,11},{10,... | collective-permute-start | bytes 638984 | tf_op jit(solution)/shard_map/ppermute | solution.py:56
  21.7 8.1 %collective-permute-start.5 = (bf16[13,64,128]{2,1,0:T(8,128)(2,1)S(1)}, bf16[13,64,128]{2,1,0:T(8,128)(2,1)S(1)}, u32[]{:S(2)}, u32[]{:S(2)}) collective-permute-start(bf16[13,64,128]{2,1,0:T(8,128)(2,1)S(1)} %get-tuple-element.77), channel_id=1, source_target_pairs={{0,3},{1,2},{2,1},{3,0},{4,7},{5,6},{6,5},{7,4},{8,11},{9,10},{10,... | collective-permute-start | bytes 638984 | tf_op jit(solution)/shard_map/ppermute | solution.py:56
  32.2 5.7 %collective-permute-start.6 = (bf16[64,1536]{1,0:T(8,128)(2,1)S(1)}, bf16[64,1536]{1,0:T(8,128)(2,1)S(1)}, u32[]{:S(2)}, u32[]{:S(2)}) collective-permute-start(bf16[64,1536]{1,0:T(8,128)(2,1)S(1)} %get-tuple-element.87), channel_id=1, source_target_pairs={{0,1},{1,0},{2,3},{3,2},{4,5},{5,4},{6,7},{7,6},{8,9},{9,8},{10,11... | collective-permute-start | bytes 589832 | tf_op jit(solution)/shard_map/ppermute | solution.py:56
  33.0 7.4 %collective-permute-start.7 = (bf16[64,1536]{1,0:T(8,128)(2,1)S(1)}, bf16[64,1536]{1,0:T(8,128)(2,1)S(1)}, u32[]{:S(2)}, u32[]{:S(2)}) collective-permute-start(bf16[64,1536]{1,0:T(8,128)(2,1)S(1)} %get-tuple-element.88), channel_id=1, source_target_pairs={{0,2},{1,3},{2,0},{3,1},{4,6},{5,7},{6,4},{7,5},{8,10},{9,11},{10,... | collective-permute-start | bytes 589832 | tf_op jit(solution)/shard_map/ppermute | solution.py:56
  35.1 6.6 %collective-permute-start.8 = (bf16[64,1536]{1,0:T(8,128)(2,1)S(1)}, bf16[64,1536]{1,0:T(8,128)(2,1)S(1)}, u32[]{:S(2)}, u32[]{:S(2)}) collective-permute-start(bf16[64,1536]{1,0:T(8,128)(2,1)S(1)} %get-tuple-element.89), channel_id=1, source_target_pairs={{0,3},{1,2},{2,1},{3,0},{4,7},{5,6},{6,5},{7,4},{8,11},{9,10},{10,... | collective-permute-start | bytes 589832 | tf_op jit(solution)/shard_map/ppermute | solution.py:56
  41.9 4.3 %collective-permute-start.12 = (bf16[64,1536]{1,0:T(8,128)(2,1)S(1)}, bf16[64,1536]{1,0:T(8,128)(2,1)S(1)}, u32[]{:S(2)}, u32[]{:S(2)}) collective-permute-start(bf16[64,1536]{1,0:T(8,128)(2,1)S(1)} %get-tuple-element.90.a_ref), channel_id=1, source_target_pairs={{0,4},{4,0},{8,12},{12,8},{16,20},{20,16},{24,28},{28,24},{1,5},{5... | collective-permute-start | bytes 589832 | tf_op jit(solution)/shard_map/ppermute | solution.py:56
  41.9 11.4 %collective-permute-start.11 = (bf16[64,1536]{1,0:T(8,128)(2,1)S(1)}, bf16[64,1536]{1,0:T(8,128)(2,1)S(1)}, u32[]{:S(2)}, u32[]{:S(2)}) collective-permute-start(bf16[64,1536]{1,0:T(8,128)(2,1)S(1)} %get-tuple-element.90.a_ref), channel_id=1, source_target_pairs={{0,8},{4,12},{8,0},{12,4},{16,24},{20,28},{24,16},{28,20},{1,9},{5... | collective-permute-start | bytes 589832 | tf_op jit(solution)/shard_map/ppermute | solution.py:56
  43.6 12.1 %collective-permute-start.9 = (bf16[64,1536]{1,0:T(8,128)(2,1)S(1)}, bf16[64,1536]{1,0:T(8,128)(2,1)S(1)}, u32[]{:S(2)}, u32[]{:S(2)}) collective-permute-start(bf16[64,1536]{1,0:T(8,128)(2,1)S(1)} %get-tuple-element.90.a_ref), channel_id=1, source_target_pairs={{0,16},{4,20},{8,24},{12,28},{16,0},{20,4},{24,8},{28,12},{1,17},{... | collective-permute-start | bytes 589832 | tf_op jit(solution)/shard_map/ppermute | solution.py:56
  55.7 1.4 %collective-permute-start.13 = (bf16[64,1536]{1,0:T(8,128)(2,1)S(1)}, bf16[64,1536]{1,0:T(8,128)(2,1)S(1)}, u32[]{:S(2)}, u32[]{:S(2)}) collective-permute-start(bf16[64,1536]{1,0:T(8,128)(2,1)S(1)} %collective-permute-done.11.a_ref), channel_id=1, source_target_pairs={{0,4},{4,0},{8,12},{12,8},{16,20},{20,16},{24,28},{28,24},{1,5},{5... | collective-permute-start | bytes 589832 | tf_op jit(solution)/shard_map/ppermute | solution.py:56
  55.7 4.0 %collective-permute-start.15 = (bf16[64,1536]{1,0:T(8,128)(2,1)S(1)}, bf16[64,1536]{1,0:T(8,128)(2,1)S(1)}, u32[]{:S(2)}, u32[]{:S(2)}) collective-permute-start(bf16[64,1536]{1,0:T(8,128)(2,1)S(1)} %collective-permute-done.9.a_ref), channel_id=1, source_target_pairs={{0,4},{4,0},{8,12},{12,8},{16,20},{20,16},{24,28},{28,24},{1,5},{5... | collective-permute-start | bytes 589832 | tf_op jit(solution)/shard_map/ppermute | solution.py:56
  56.2 5.9 %collective-permute-start.14 = (bf16[64,1536]{1,0:T(8,128)(2,1)S(1)}, bf16[64,1536]{1,0:T(8,128)(2,1)S(1)}, u32[]{:S(2)}, u32[]{:S(2)}) collective-permute-start(bf16[64,1536]{1,0:T(8,128)(2,1)S(1)} %get-tuple-element.97), channel_id=1, source_target_pairs={{0,4},{4,0},{8,12},{12,8},{16,20},{20,16},{24,28},{28,24},{1,5},{5... | collective-permute-start | bytes 589832 | tf_op jit(solution)/shard_map/ppermute | solution.py:56
  56.2 7.3 %collective-permute-start.10 = (bf16[64,1536]{1,0:T(8,128)(2,1)S(1)}, bf16[64,1536]{1,0:T(8,128)(2,1)S(1)}, u32[]{:S(2)}, u32[]{:S(2)}) collective-permute-start(bf16[64,1536]{1,0:T(8,128)(2,1)S(1)} %collective-permute-done.9.a_ref), channel_id=1, source_target_pairs={{0,8},{4,12},{8,0},{12,4},{16,24},{20,28},{24,16},{28,20},{1,9},{5... | collective-permute-start | bytes 589832 | tf_op jit(solution)/shard_map/ppermute | solution.py:56
  59.0 11.9 %collective-permute-start.23 = (bf16[8,1024]{1,0:T(8,128)(2,1)S(1)}, bf16[8,1024]{1,0:T(8,128)(2,1)S(1)}, u32[]{:S(2)}, u32[]{:S(2)}) collective-permute-start(bf16[8,1024]{1,0:T(8,128)(2,1)S(1)} %get-tuple-element.107), channel_id=1, source_target_pairs={{0,1},{1,0},{2,3},{3,2},{4,5},{5,4},{6,7},{7,6},{8,9},{9,8},{10,11... | collective-permute-start | bytes 49160 | tf_op jit(solution)/shard_map/ppermute | solution.py:56
  61.5 2.0 %collective-permute-start.16 = (bf16[64,1536]{1,0:T(8,128)(2,1)S(1)}, bf16[64,1536]{1,0:T(8,128)(2,1)S(1)}, u32[]{:S(2)}, u32[]{:S(2)}) collective-permute-start(bf16[64,1536]{1,0:T(8,128)(2,1)S(1)} %get-tuple-element.101), channel_id=1, source_target_pairs={{0,4},{4,0},{8,12},{12,8},{16,20},{20,16},{24,28},{28,24},{1,5},{5... | collective-permute-start | bytes 589832 | tf_op jit(solution)/shard_map/ppermute | solution.py:56
  61.6 5.6 %collective-permute-start.18 = (bf16[64,1536]{1,0:T(8,128)(2,1)S(1)}, bf16[64,1536]{1,0:T(8,128)(2,1)S(1)}, u32[]{:S(2)}, u32[]{:S(2)}) collective-permute-start(bf16[64,1536]{1,0:T(8,128)(2,1)S(1)} %get-tuple-element.102), channel_id=1, source_target_pairs={{0,4},{4,0},{8,12},{12,8},{16,20},{20,16},{24,28},{28,24},{1,5},{5... | collective-permute-start | bytes 589832 | tf_op jit(solution)/shard_map/ppermute | solution.py:56
  63.5 1.7 %collective-permute-start.20 = (bf16[64,1536]{1,0:T(8,128)(2,1)S(1)}, bf16[64,1536]{1,0:T(8,128)(2,1)S(1)}, u32[]{:S(2)}, u32[]{:S(2)}) collective-permute-start(bf16[64,1536]{1,0:T(8,128)(2,1)S(1)} %collective-permute-done.10.a_ref), channel_id=1, source_target_pairs={{0,4},{4,0},{8,12},{12,8},{16,20},{20,16},{24,28},{28,24},{1,5},{5... | collective-permute-start | bytes 589832 | tf_op jit(solution)/shard_map/ppermute | solution.py:56
  63.6 13.0 %collective-permute-start.17 = (bf16[64,1536]{1,0:T(8,128)(2,1)S(1)}, bf16[64,1536]{1,0:T(8,128)(2,1)S(1)}, u32[]{:S(2)}, u32[]{:S(2)}) collective-permute-start(bf16[64,1536]{1,0:T(8,128)(2,1)S(1)} %add_convert_fusion.3), channel_id=1, source_target_pairs={{0,16},{4,20},{8,24},{12,28},{16,0},{20,4},{24,8},{28,12},{1,17},{... | collective-permute-start | bytes 589832 | tf_op jit(solution)/shard_map/ppermute | solution.py:56
  67.1 1.9 %collective-permute-start.21 = (bf16[64,1536]{1,0:T(8,128)(2,1)S(1)}, bf16[64,1536]{1,0:T(8,128)(2,1)S(1)}, u32[]{:S(2)}, u32[]{:S(2)}) collective-permute-start(bf16[64,1536]{1,0:T(8,128)(2,1)S(1)} %get-tuple-element.105), channel_id=1, source_target_pairs={{0,4},{4,0},{8,12},{12,8},{16,20},{20,16},{24,28},{28,24},{1,5},{5... | collective-permute-start | bytes 589832 | tf_op jit(solution)/shard_map/ppermute | solution.py:56
  67.2 15.7 %collective-permute-start.19 = (bf16[64,1536]{1,0:T(8,128)(2,1)S(1)}, bf16[64,1536]{1,0:T(8,128)(2,1)S(1)}, u32[]{:S(2)}, u32[]{:S(2)}) collective-permute-start(bf16[64,1536]{1,0:T(8,128)(2,1)S(1)} %add_convert_fusion.2), channel_id=1, source_target_pairs={{0,8},{4,12},{8,0},{12,4},{16,24},{20,28},{24,16},{28,20},{1,9},{5... | collective-permute-start | bytes 589832 | tf_op jit(solution)/shard_map/ppermute | solution.py:56
  69.0 13.9 %collective-permute-start.22 = (bf16[64,1536]{1,0:T(8,128)(2,1)S(1)}, bf16[64,1536]{1,0:T(8,128)(2,1)S(1)}, u32[]{:S(2)}, u32[]{:S(2)}) collective-permute-start(bf16[64,1536]{1,0:T(8,128)(2,1)S(1)} %add_convert_fusion.1), channel_id=1, source_target_pairs={{0,24},{4,28},{8,16},{12,20},{16,8},{20,12},{24,0},{28,4},{1,25},{... | collective-permute-start | bytes 589832 | tf_op jit(solution)/shard_map/ppermute | solution.py:56
  70.9 3.9 %collective-permute-start.24 = (bf16[16,1024]{1,0:T(8,128)(2,1)S(1)}, bf16[16,1024]{1,0:T(8,128)(2,1)S(1)}, u32[]{:S(2)}, u32[]{:S(2)}) collective-permute-start(bf16[16,1024]{1,0:T(8,128)(2,1)S(1)} %pad_maximum_fusion.1), channel_id=1, source_target_pairs={{0,2},{1,3},{2,0},{3,1},{4,6},{5,7},{6,4},{7,5},{8,10},{9,11},{10,... | collective-permute-start | bytes 98312 | tf_op jit(solution)/shard_map/ppermute | solution.py:56
